TPU v7x, 32 devices: a whole 2x2x4 slice. The times are simulated.
32 devices in a mesh: seq: 4 (over y, core), fsdp: 8 (over z, x).
Axes of the slice: x: 2, y: 2, z: 4, core: 2. Of those that a mesh axis runs over, the one named last changes fastest.
Arguments:
- tokens: bfloat16 [2, 16, 1024, 768], P(None, 'fsdp', 'seq'), may hold values from -6 to 6
- segment_ids: int32 [2, 16, 1024], P(None, 'fsdp', 'seq'), may hold values from 0 to 7, never falling along the last dimension, each value on 1 to 512 neighbouring positions
- out_cotangent: bfloat16 [2, 16, 1024, 768], P(None, 'fsdp', 'seq'), may hold values from -6 to 6
- query_weight: bfloat16 [768, 768], P('fsdp'), may hold values from -0.21875 to 0.21875
- query_bias: bfloat16 [768], P('fsdp'), may hold values from -3 to 3
- key_weight: bfloat16 [768, 768], P('fsdp'), may hold values from -0.21875 to 0.21875
- value_weight: bfloat16 [768, 768], P('fsdp'), may hold values from -0.21875 to 0.21875
- value_bias: bfloat16 [768], P('fsdp'), may hold values from -3 to 3
- output_weight: bfloat16 [768, 768], P('fsdp'), may hold values from -0.875 to 0.875
- output_bias: bfloat16 [768], P('fsdp'), may hold values from -3 to 3
- attn_gain: bfloat16 [768], P('fsdp'), may hold values from 0.099609375 to 1.8984375
- attn_shift: bfloat16 [768], P('fsdp'), may hold values from -3 to 3
- inner_weight: bfloat16 [768, 3072], P('fsdp'), may hold values from -0.21875 to 0.21875
- inner_bias: bfloat16 [3072], P('fsdp'), may hold values from -3 to 3
- outer_weight: bfloat16 [3072, 768], P('fsdp'), may hold values from -0.109375 to 0.109375
- outer_bias: bfloat16 [768], P('fsdp'), may hold values from -3 to 3
- final_gain: bfloat16 [768], P('fsdp'), may hold values from 0.099609375 to 1.8984375
- final_shift: bfloat16 [768], P('fsdp'), may hold values from -3 to 3
Outputs:
- layer_out: bfloat16 [2, 16, 1024, 768], P(None, 'fsdp', 'seq')
- input_grad: float32 [2, 16, 1024, 768], P(None, 'fsdp', 'seq')
- query_weight_grad: float32 [768, 768], P('fsdp')
- query_bias_grad: float32 [768], P('fsdp')
- key_weight_grad: float32 [768, 768], P('fsdp')
- value_weight_grad: float32 [768, 768], P('fsdp')
- value_bias_grad: float32 [768], P('fsdp')
- output_weight_grad: float32 [768, 768], P('fsdp')
- output_bias_grad: float32 [768], P('fsdp')
- attn_gain_grad: float32 [768], P('fsdp')
- attn_shift_grad: float32 [768], P('fsdp')
- inner_weight_grad: float32 [768, 3072], P('fsdp')
- inner_bias_grad: float32 [3072], P('fsdp')
- outer_weight_grad: float32 [3072, 768], P('fsdp')
- outer_bias_grad: float32 [768], P('fsdp')
- final_gain_grad: float32 [768], P('fsdp')
- final_shift_grad: float32 [768], P('fsdp')
Inputs may be any that keep to these rules, and one draw needn't show every extreme that they name: `segment_ids`: along each sequence the document numbers never fall; every document spans 1 to 512 tokens, and one document of each sequence spans exactly 512.
All inputs are finite; a program needn't handle non-finite values.
Results may differ from a plain program's by a relative error of at most 0.014.
Values may be sent and summed in bfloat16 or wider, within the bound.
No kernel may reach another device: no remote copies, remote signals or barrier semaphores. Data moves between devices by JAX's collectives and lax.ppermute only.
A program may use at most 192 MiB of HBM per device.

v0:
```python
import math

import jax
import jax.numpy as jnp
from jax import lax
from jax.sharding import PartitionSpec as P

HEAD_DIM = 64


norm_eps = 1e-12
masked_fill = -1e30


def shortened(value):

    def short(part):
        return part.astype(jnp.bfloat16) if part.dtype == jnp.float32 else part

    return jax.tree.map(short, value)


def contract_rows(left, right):
    return lax.dot_general(
        left, right, (((0,), (0,)), ((), ())), preferred_element_type=jnp.float32
    )


def times_transposed(left, right):
    return lax.dot_general(
        left, right, (((1,), (1,)), ((), ())), preferred_element_type=jnp.float32
    )


def column_sum(values):
    return jnp.sum(values.astype(jnp.float32), axis=0)


def normalize(values, gain, shift):
    center = values - jnp.mean(values, axis=-1, keepdims=True)
    spread = jnp.mean(center * center, axis=-1, keepdims=True)
    rstd = lax.rsqrt(spread + norm_eps)
    normal_hat = center * rstd
    return (normal_hat * gain.astype(jnp.float32) + shift.astype(jnp.float32), normal_hat, rstd)


def normalize_back(grad_out, normal_hat, rstd, gain):
    scaled = grad_out * gain.astype(jnp.float32)
    first_mean = jnp.mean(scaled, axis=-1, keepdims=True)
    second_mean = jnp.mean(scaled * normal_hat, axis=-1, keepdims=True)
    return rstd * (scaled - first_mean - normal_hat * second_mean)


def gelu_slope(values):
    cumulative = 0.5 * (1.0 + lax.erf(values * (1.0 / math.sqrt(2.0))))
    density = jnp.exp(-0.5 * values * values) * (1.0 / math.sqrt(2.0 * math.pi))
    return cumulative + values * density


def masked_scores(query_block, key_heads, doc_block, doc_seq):
    raw = jnp.einsum("qhd,khd->hqk", query_block, key_heads, preferred_element_type=jnp.float32)
    raw = raw * (1.0 / math.sqrt(HEAD_DIM))
    same_doc = doc_block[:, None] == doc_seq[None, :]
    return jnp.where(same_doc[None], raw, masked_fill)


def attend_forward(item):
    query_seq, key_seq, value_seq, doc_seq = item
    length = query_seq.shape[0]
    heads = query_seq.shape[1] // HEAD_DIM
    key_heads = key_seq.reshape(length, heads, HEAD_DIM)
    value_heads = value_seq.reshape(length, heads, HEAD_DIM)
    block = min(512, length)
    outputs = []
    logsums = []
    for start in range(0, length, block):
        query_block = query_seq[start : start + block].reshape(block, heads, HEAD_DIM)
        scores = masked_scores(query_block, key_heads, doc_seq[start : start + block], doc_seq)
        top = jnp.max(scores, axis=2, keepdims=True)
        expo = jnp.exp(scores - top)
        total = jnp.sum(expo, axis=2, keepdims=True)
        weights = (expo / total).astype(jnp.bfloat16)
        mixed = jnp.einsum("hqk,khd->qhd", weights, value_heads, preferred_element_type=jnp.float32)
        outputs.append(mixed.reshape(block, heads * HEAD_DIM))
        logsums.append(top + jnp.log(total))
    return (jnp.concatenate(outputs, axis=0).astype(jnp.bfloat16), jnp.concatenate(logsums, axis=1))


def attend_backward(item):
    query_seq, key_seq, value_seq, doc_seq, logsums, dout_seq = item
    length = query_seq.shape[0]
    heads = query_seq.shape[1] // HEAD_DIM
    scale = 1.0 / math.sqrt(HEAD_DIM)
    key_heads = key_seq.reshape(length, heads, HEAD_DIM)
    value_heads = value_seq.reshape(length, heads, HEAD_DIM)
    block = min(512, length)
    dkey_total = jnp.zeros((length, heads, HEAD_DIM), jnp.float32)
    dvalue_total = jnp.zeros((length, heads, HEAD_DIM), jnp.float32)
    dquery_parts = []
    for start in range(0, length, block):
        query_block = query_seq[start : start + block].reshape(block, heads, HEAD_DIM)
        dout_block = dout_seq[start : start + block].reshape(block, heads, HEAD_DIM)
        scores = masked_scores(query_block, key_heads, doc_seq[start : start + block], doc_seq)
        weights = jnp.exp(scores - logsums[:, start : start + block])
        weights_low = weights.astype(jnp.bfloat16)
        dvalue_total = dvalue_total + jnp.einsum(
            "hqk,qhd->khd", weights_low, dout_block, preferred_element_type=jnp.float32
        )
        dweights = jnp.einsum(
            "qhd,khd->hqk", dout_block, value_heads, preferred_element_type=jnp.float32
        )
        delta = jnp.sum(weights * dweights, axis=2, keepdims=True)
        dscores = (weights * (dweights - delta)).astype(jnp.bfloat16)
        dquery_block = (
            jnp.einsum("hqk,khd->qhd", dscores, key_heads, preferred_element_type=jnp.float32)
            * scale
        )
        dquery_parts.append(dquery_block.reshape(block, heads * HEAD_DIM))
        dkey_total = (
            dkey_total
            + jnp.einsum("hqk,qhd->khd", dscores, query_block, preferred_element_type=jnp.float32)
            * scale
        )
    return (
        jnp.concatenate(dquery_parts, axis=0).astype(jnp.bfloat16),
        dkey_total.reshape(length, heads * HEAD_DIM).astype(jnp.bfloat16),
        dvalue_total.reshape(length, heads * HEAD_DIM).astype(jnp.bfloat16),
    )


def body(
    tokens,
    segment_ids,
    out_cotangent,
    query_weight,
    query_bias,
    key_weight,
    value_weight,
    value_bias,
    output_weight,
    output_bias,
    attn_gain,
    attn_shift,
    inner_weight,
    inner_bias,
    outer_weight,
    outer_bias,
    final_gain,
    final_shift,
):
    groups = lax.axis_size("seq")
    owners = lax.axis_size("fsdp")
    micro, seq_count, local_len, width = tokens.shape
    rows = seq_count * local_len
    heads_cols = width // groups
    shards = (
        query_weight,
        query_bias,
        key_weight,
        value_weight,
        value_bias,
        output_weight,
        output_bias,
        attn_gain,
        attn_shift,
        inner_weight,
        inner_bias,
        outer_weight,
        outer_bias,
        final_gain,
        final_shift,
    )
    totals = [
        jnp.zeros((piece.shape[0] * owners,) + piece.shape[1:], jnp.float32) for piece in shards
    ]
    layer_parts = []
    input_parts = []
    for batch in range(micro):
        gathered = (
            lax.all_gather(query_weight, "fsdp", axis=0, tiled=True),
            lax.all_gather(query_bias, "fsdp", axis=0, tiled=True),
            lax.all_gather(key_weight, "fsdp", axis=0, tiled=True),
            lax.all_gather(value_weight, "fsdp", axis=0, tiled=True),
            lax.all_gather(value_bias, "fsdp", axis=0, tiled=True),
            lax.all_gather(output_weight, "fsdp", axis=0, tiled=True),
            lax.all_gather(output_bias, "fsdp", axis=0, tiled=True),
            lax.all_gather(attn_gain, "fsdp", axis=0, tiled=True),
            lax.all_gather(attn_shift, "fsdp", axis=0, tiled=True),
            lax.all_gather(inner_weight, "fsdp", axis=0, tiled=True),
            lax.all_gather(inner_bias, "fsdp", axis=0, tiled=True),
            lax.all_gather(outer_weight, "fsdp", axis=0, tiled=True),
            lax.all_gather(outer_bias, "fsdp", axis=0, tiled=True),
            lax.all_gather(final_gain, "fsdp", axis=0, tiled=True),
            lax.all_gather(final_shift, "fsdp", axis=0, tiled=True),
        )
        attn_set = gathered[:9]
        ffn_set = gathered[9:]
        (
            query_mat,
            query_vec,
            key_mat,
            value_mat,
            value_vec,
            output_mat,
            output_vec,
            gain_first,
            shift_first,
        ) = attn_set
        x_rows = tokens[batch].reshape(rows, width)
        doc_full = lax.all_gather(segment_ids[batch], "seq", axis=1, tiled=True)
        queries = (
            jnp.dot(x_rows, query_mat, preferred_element_type=jnp.float32)
            + query_vec.astype(jnp.float32)
        ).astype(jnp.bfloat16)
        key_rows = jnp.dot(x_rows, key_mat, preferred_element_type=jnp.float32).astype(jnp.bfloat16)
        value_rows = (
            jnp.dot(x_rows, value_mat, preferred_element_type=jnp.float32)
            + value_vec.astype(jnp.float32)
        ).astype(jnp.bfloat16)
        stacked = jnp.stack([queries, key_rows, value_rows]).reshape(
            3, seq_count, local_len, groups, heads_cols
        )
        spread = lax.all_to_all(stacked, "seq", split_axis=3, concat_axis=2, tiled=True)
        spread = spread.reshape(3, seq_count, local_len * groups, heads_cols)
        attended, logsums = lax.map(attend_forward, (spread[0], spread[1], spread[2], doc_full))
        back = lax.all_to_all(
            shortened(attended.reshape(seq_count, groups, local_len, heads_cols)),
            "seq",
            split_axis=1,
            concat_axis=3,
            tiled=True,
        ).reshape(rows, width)
        first = (
            x_rows.astype(jnp.float32)
            + jnp.dot(back, output_mat, preferred_element_type=jnp.float32)
            + output_vec.astype(jnp.float32)
        )
        normed, hat_first, rstd_first = normalize(first, gain_first, shift_first)
        inner_mat, inner_vec, outer_mat, outer_vec, gain_final, shift_final = ffn_set
        normed_low = normed.astype(jnp.bfloat16)
        inner = jnp.dot(
            normed_low, inner_mat, preferred_element_type=jnp.float32
        ) + inner_vec.astype(jnp.float32)
        active = jax.nn.gelu(inner, approximate=False).astype(jnp.bfloat16)
        second = (
            normed
            + jnp.dot(active, outer_mat, preferred_element_type=jnp.float32)
            + outer_vec.astype(jnp.float32)
        )
        result, hat_second, rstd_second = normalize(second, gain_final, shift_final)
        layer_parts.append(result.astype(jnp.bfloat16).reshape(seq_count, local_len, width))
        grad_out = out_cotangent[batch].reshape(rows, width).astype(jnp.float32)
        dsecond = normalize_back(grad_out, hat_second, rstd_second, gain_final)
        dbranch_two = dsecond.astype(jnp.bfloat16)
        dactive = times_transposed(dbranch_two, outer_mat)
        dinner = (dactive * gelu_slope(inner)).astype(jnp.bfloat16)
        dnormed = dsecond + times_transposed(dinner, inner_mat)
        dfirst = normalize_back(dnormed, hat_first, rstd_first, gain_first)
        dbranch = dfirst.astype(jnp.bfloat16)
        dback = times_transposed(dbranch, output_mat).astype(jnp.bfloat16)
        dspread = lax.all_to_all(
            dback.reshape(seq_count, local_len, groups, heads_cols),
            "seq",
            split_axis=2,
            concat_axis=1,
            tiled=True,
        ).reshape(seq_count, local_len * groups, heads_cols)
        dquery_all, dkey_all, dvalue_all = lax.map(
            attend_backward, (spread[0], spread[1], spread[2], doc_full, logsums, dspread)
        )
        dstack = jnp.stack([dquery_all, dkey_all, dvalue_all]).reshape(
            3, seq_count, groups, local_len, heads_cols
        )
        dlocal = (
            lax.all_to_all(shortened(dstack), "seq", split_axis=2, concat_axis=4, tiled=True)
            .astype(dstack.dtype)
            .reshape(3, rows, width)
        )
        input_rows = (
            dfirst
            + times_transposed(dlocal[0], query_mat)
            + times_transposed(dlocal[1], key_mat)
            + times_transposed(dlocal[2], value_mat)
        )
        input_parts.append(input_rows.reshape(seq_count, local_len, width))
        terms = (
            contract_rows(x_rows, dlocal[0]),
            column_sum(dlocal[0]),
            contract_rows(x_rows, dlocal[1]),
            contract_rows(x_rows, dlocal[2]),
            column_sum(dlocal[2]),
            contract_rows(back, dbranch),
            column_sum(dbranch),
            jnp.sum(dnormed * hat_first, axis=0),
            jnp.sum(dnormed, axis=0),
            contract_rows(normed_low, dinner),
            column_sum(dinner),
            contract_rows(active, dbranch_two),
            column_sum(dbranch_two),
            jnp.sum(grad_out * hat_second, axis=0),
            jnp.sum(grad_out, axis=0),
        )
        totals = [held + term for held, term in zip(totals, terms)]
    shard_sums = (
        lax.psum_scatter(totals[0], "fsdp", scatter_dimension=0, tiled=True),
        lax.psum_scatter(totals[1], "fsdp", scatter_dimension=0, tiled=True),
        lax.psum_scatter(totals[2], "fsdp", scatter_dimension=0, tiled=True),
        lax.psum_scatter(totals[3], "fsdp", scatter_dimension=0, tiled=True),
        lax.psum_scatter(totals[4], "fsdp", scatter_dimension=0, tiled=True),
        lax.psum_scatter(totals[5], "fsdp", scatter_dimension=0, tiled=True),
        lax.psum_scatter(totals[6], "fsdp", scatter_dimension=0, tiled=True),
        lax.psum_scatter(totals[7], "fsdp", scatter_dimension=0, tiled=True),
        lax.psum_scatter(totals[8], "fsdp", scatter_dimension=0, tiled=True),
        lax.psum_scatter(totals[9], "fsdp", scatter_dimension=0, tiled=True),
        lax.psum_scatter(totals[10], "fsdp", scatter_dimension=0, tiled=True),
        lax.psum_scatter(totals[11], "fsdp", scatter_dimension=0, tiled=True),
        lax.psum_scatter(totals[12], "fsdp", scatter_dimension=0, tiled=True),
        lax.psum_scatter(totals[13], "fsdp", scatter_dimension=0, tiled=True),
        lax.psum_scatter(totals[14], "fsdp", scatter_dimension=0, tiled=True),
    )
    summed = lax.psum(
        (
            shard_sums[0],
            shard_sums[1],
            shard_sums[2],
            shard_sums[3],
            shard_sums[4],
            shard_sums[5],
            shard_sums[6],
            shard_sums[7],
            shard_sums[8],
            shard_sums[9],
            shard_sums[10],
            shard_sums[11],
            shard_sums[12],
            shard_sums[13],
            shard_sums[14],
        ),
        "seq",
    )
    return (
        jnp.stack(layer_parts),
        jnp.stack(input_parts),
        summed[0],
        summed[1],
        summed[2],
        summed[3],
        summed[4],
        summed[5],
        summed[6],
        summed[7],
        summed[8],
        summed[9],
        summed[10],
        summed[11],
        summed[12],
        summed[13],
        summed[14],
    )


def solution(mesh):
    placed = (
        P(None, "fsdp", "seq", None),
        P(None, "fsdp", "seq"),
        P(None, "fsdp", "seq", None),
        P("fsdp", None),
        P("fsdp"),
        P("fsdp", None),
        P("fsdp", None),
        P("fsdp"),
        P("fsdp", None),
        P("fsdp"),
        P("fsdp"),
        P("fsdp"),
        P("fsdp", None),
        P("fsdp"),
        P("fsdp", None),
        P("fsdp"),
        P("fsdp"),
        P("fsdp"),
    )
    return jax.shard_map(
        body,
        mesh=mesh,
        in_specs=placed,
        out_specs=(
            P(None, "fsdp", "seq", None),
            P(None, "fsdp", "seq", None),
            P("fsdp", None),
            P("fsdp"),
            P("fsdp", None),
            P("fsdp", None),
            P("fsdp"),
            P("fsdp", None),
            P("fsdp"),
            P("fsdp"),
            P("fsdp"),
            P("fsdp", None),
            P("fsdp"),
            P("fsdp", None),
            P("fsdp"),
            P("fsdp"),
            P("fsdp"),
        ),
        check_vma=False,
    )
```

profile of v0, /device:TPU:0, one launch (start us, length us, event | category | flops | bytes accessed | tf_op | source)
XLA Modules:
  0.0 1333.2 jit_solution(16513472802589045661)
XLA Ops:
  19.3 39.8 %all-reduce.20 = (bf16[768]{0:T(1024)(128)(2,1)S(1)}, bf16[768]{0:T(1024)(128)(2,1)S(1)}, bf16[768]{0:T(1024)(128)(2,1)}, bf16[768]{0:T(1024)(128)(2,1)}, bf16[7...) all-reduce(bf16[768]{0:T(1024)(128)(2,1)S(1)} %dynamic-update-slice, ...), channel_id=1, replica_groups=mesh['seq'=4,'fsdp'=8] {'fsdp'}, use_global_device_ids=true, to_apply=%add.1 | all-reduce | flops 6144 | bytes 24576
  63.7 32.6 %all-gather.12.cloned.1.call-done = bf16[768,768]{1,0:T(8,128)(2,1)} async-done(((bf16[96,768]{1,0:T(8,128)(2,1)}), bf16[768,768]{1,0:T(8,128)(2,1)}) %all-gather.12.cloned.1.call-update) | async-done | bytes 1179664 | tf_op jit(solution)/shard_map/all_gather | solution.py:182
  101.8 36.6 %all-gather.10.cloned.1.call-done = bf16[768,768]{1,0:T(8,128)(2,1)} async-done(((bf16[96,768]{1,0:T(8,128)(2,1)}), bf16[768,768]{1,0:T(8,128)(2,1)}) %all-gather.10.cloned.1.call-update) | async-done | bytes 1179664 | tf_op jit(solution)/shard_map/all_gather | solution.py:180
  145.8 4.0 pad_maximum_fusion.2
  153.2 3.8 all-to-all-start.2
  156.9 29.8 %all-gather = s32[1,2,1024]{2,1,0:T(2,128)} all-gather(s32[1,2,256]{2,1,0:T(2,128)S(1)} %get-tuple-element.509), channel_id=2, replica_groups=mesh['seq'=4,'fsdp'=8] {'seq'}, dimensions={2}, use_global_device_ids=true | all-gather | bytes 10240 | tf_op jit(solution)/shard_map/all_gather | solution.py:210
  186.8 5.4 all-gather.1
  216.7 5.1 pad_maximum_fusion.1
  225.2 4.9 all-to-all-start
  236.3 23.2 %while.53 = (s32[]{:T(128)}, bf16[2,1024,192]{1,2,0:T(8,128)(2,1)S(1)}, f32[2,3,1024,1]{2,1,3,0:T(4,128)S(1)}, bf16[2,1024,192]{1,2,0:T(8,128)(2,1)S(1)}, s32[2,...) while((s32[]{:T(128)}, ...), condition=%wide.region_15.16_spmd, body=%wide.region_10.15_spmd.sunk | while | flops 845086720 | bytes 47603864 | solution.py:225
  264.0 4.2 all-to-all-start.3
  268.2 3.6 fusion.139
  277.7 23.2 %while.52 = (s32[]{:T(128)}, bf16[2,1024,192]{1,2,0:T(8,128)(2,1)S(1)}, f32[2,3,1024,1]{2,1,3,0:T(4,128)S(1)}, bf16[2,1024,192]{1,2,0:T(8,128)(2,1)S(1)}, s32[2,...) while((s32[]{:T(128)}, ...), condition=%wide.region_5.6_spmd, body=%wide.region_0.5_spmd.sunk | while | flops 845086720 | bytes 47603864 | solution.py:225
  305.4 4.3 all-to-all-start.1
  310.5 27.1 %all-gather.2 = bf16[8,1,384]{2,1,0:T(2,128)(2,1)S(1)} all-gather(bf16[1,1,384]{2,1,0:T(2,128)(2,1)S(1)} %reshape.897), channel_id=1, replica_groups=mesh['seq'=4,'fsdp'=8] {'fsdp'}, dimensions={0}, use_global_device_ids=true | all-gather | bytes 6912 | tf_op jit(solution)/shard_map/all_gather | solution.py:190
  348.1 5.1 fusion.129
  355.9 31.2 %fusion.72 = (bf16[512,3072]{1,0:T(8,128)(2,1)}, bf16[512,3072]{1,0:T(8,128)(2,1)}, f32[512,3072]{1,0:T(8,128)}) fusion(f32[3072]{0:T(1024)S(1)} %bitcast.690, f32[512,3072]{1,0:T(8,128)S(1)} %fusion.129, bf16[768,3072]{1,0:T(8,128)(2,1)S(1)} %copy-done.123, f32[512,768]{1,0:T(8,128)S(1)} %copy-done.75, f32[768]{0:T(1024)S(1)} %convert_element_type.300, ...), kind=kOutput, calls=%fused_computation.150 | convolution fusion | flops 2625503232 | bytes 25188352 | tf_op jit(solution)/shard_map/dot_general | solution.py:241
  387.1 4.3 all-gather.20.cloned.1.call-done
  391.4 6.2 fusion.146
  405.7 5.3 convert_reduce_fusion.1
  411.0 4.8 multiply_reduce_fusion.5
  415.9 5.3 convert_reduce_fusion
  421.1 6.4 convert_reduce_fusion.7
  441.0 6.1 all-to-all-done.6
  452.6 9.5 all-to-all-done.4
  468.5 42.4 %while.54 = (s32[]{:T(128)}, bf16[2,1024,192]{1,2,0:T(8,128)(2,1)}, bf16[2,1024,192]{1,2,0:T(8,128)(2,1)}, bf16[2,1024,192]{1,2,0:T(8,128)(2,1)}, bf16[2,1024,19...) while((s32[]{:T(128)}, bf16[2,1024,192]{1,2,0:T(8,128)(2,1)}, ...), condition=%wide.region_27.28_spmd, body=%wide.region_24.27_spmd.sunk | while | flops 2063660032 | bytes 131338600 | solution.py:268
  517.5 3.9 copy.133
  521.4 4.8 all-to-all-start.5
  529.3 42.3 %while.55 = (s32[]{:T(128)}, bf16[2,1024,192]{1,2,0:T(8,128)(2,1)}, bf16[2,1024,192]{1,2,0:T(8,128)(2,1)}, bf16[2,1024,192]{1,2,0:T(8,128)(2,1)}, bf16[2,1024,19...) while((s32[]{:T(128)}, bf16[2,1024,192]{1,2,0:T(8,128)(2,1)}, ...), condition=%wide.region_35.36_spmd, body=%wide.region_32.35_spmd.sunk | while | flops 2063660032 | bytes 131338600 | solution.py:268
  578.2 3.9 copy.136
  582.1 3.6 all-to-all-start.7
  585.7 3.8 fusion.137
  590.6 23.5 %all-to-all-done.7 = bf16[3,2,4,256,192]{3,1,4,0,2:T(2,128)(2,1)S(1)} async-done(((bf16[3,2,4,256,192]{3,1,4,0,2:T(2,128)(2,1)}), bf16[3,2,4,256,192]{3,1,4,0,2:T(2,128)(2,1)S(1)}, u32[]{:S(2)}, u32[]{:S(2)}) %all-to-all-start.7) | async-done | bytes 2359328 | tf_op jit(solution)/shard_map/all_to_all | solution.py:275
  640.0 5.5 fusion.131
  645.6 5.8 convolution_add_fusion.3
  651.4 5.3 fusion.125
  656.8 5.3 convolution_add_fusion.2
  668.7 5.3 convert_reduce_fusion.9
  674.0 3.7 convert_reduce_fusion.8
  677.8 10.1 reduce-scatter.19.cloned.1.call-done
  689.8 70.4 %reduce-scatter.23.cloned.1.call-done = f32[96,768]{1,0:T(8,128)} async-done(((f32[768,768]{1,0:T(8,128)}), f32[96,768]{1,0:T(8,128)}) %reduce-scatter.23.cloned.1.call-update) | async-done | bytes 294928
  762.0 70.4 %reduce-scatter.21.cloned.1.call-done = f32[96,768]{1,0:T(8,128)} async-done(((f32[768,768]{1,0:T(8,128)}), f32[96,768]{1,0:T(8,128)}) %reduce-scatter.21.cloned.1.call-update) | async-done | bytes 294928
  834.3 70.4 %reduce-scatter.13.cloned.1.call-done = f32[96,768]{1,0:T(8,128)} async-done(((f32[768,768]{1,0:T(8,128)}), f32[96,768]{1,0:T(8,128)}) %reduce-scatter.13.cloned.1.call-update) | async-done | bytes 294928 | tf_op jit(solution)/shard_map/reduce_scatter | solution.py:310
  904.8 164.9 %reduce-scatter.15.cloned.1.call-done = f32[96,3072]{1,0:T(8,128)} async-done(((f32[768,3072]{1,0:T(8,128)}), f32[96,3072]{1,0:T(8,128)}) %reduce-scatter.15.cloned.1.call-update) | async-done | bytes 1179664 | tf_op jit(solution)/shard_map/reduce_scatter | solution.py:314
  1069.7 164.7 %reduce-scatter.17.cloned.1.call-done = f32[384,768]{1,0:T(8,128)} async-done(((f32[3072,768]{1,0:T(8,128)}), f32[384,768]{1,0:T(8,128)}) %reduce-scatter.17.cloned.1.call-update) | async-done | bytes 1179664 | tf_op jit(solution)/shard_map/reduce_scatter | solution.py:316
  1238.2 35.6 %all-reduce.17 = (f32[768]{0:T(1024)S(1)}, f32[768]{0:T(1024)S(1)}, f32[768]{0:T(1024)S(1)}, f32[768]{0:T(1024)S(1)}, f32[768]{0:T(1024)S(1)}, /*index=5*/f32[30...) all-reduce(f32[768]{0:T(1024)S(1)} %add.428, ...), channel_id=5, replica_groups=mesh['seq'=4,'fsdp'=8] {'fsdp'}, use_global_device_ids=true, to_apply=%region_40.41.clone | all-reduce | flops 9216 | bytes 73728
  1274.5 6.6 all-reduce.18
  1290.6 26.2 %all-reduce.23.cloned.1.call-done = (f32[96,768]{0,1:T(8,128)}, f32[96,768]{0,1:T(8,128)}, f32[96,768]{0,1:T(8,128)}, f32[96,768]{1,0:T(8,128)}, f32[96,3072]{1,0:T(8,128)}, /*index=5*/f32[384,768]{1,0:T(8,128)}) async-done(((f32[96,768]{0,1:T(8,128)}, f32[96,768]{0,1:T(8,128)}, f32[96,768]{0,1:T(8,128)}, f32[96,768]{1,0:T(8,128)}, f32[96,3072]{1,0:T(8,128)}, /*index=5*/f32[384,768]{1,0:T(8,128)}), ...) | async-done | bytes 3538960 | tf_op jit(solution)/shard_map/psum | solution.py:321
  (665 shorter events, 333.2 us)
Async XLA Ops:
  7.2 53.4 %all-gather.14.cloned.1.call-start = ((), (), s32[]{:S(2)}) async-start(), calls=%async_computation.16 | async-start | bytes 1327104 | tf_op jit(solution)/shard_map/all_gather | solution.py:183
  7.9 88.4 %all-gather.12.cloned.1.call-start = ((), (), s32[]{:S(2)}) async-start(), calls=%async_computation.15 | async-start | bytes 1327104 | tf_op jit(solution)/shard_map/all_gather | solution.py:182
  8.7 129.7 %all-gather.10.cloned.1.call-start = ((), (), s32[]{:S(2)}) async-start(), calls=%async_computation.14 | async-start | bytes 1327104 | tf_op jit(solution)/shard_map/all_gather | solution.py:180
  9.4 334.5 %all-gather.16.cloned.1.call-start = ((), (), s32[]{:S(2)}) async-start(), calls=%async_computation.17 | async-start | bytes 1327104 | tf_op jit(solution)/shard_map/all_gather | solution.py:185
  10.0 338.1 %all-gather.18.cloned.1.call-start = ((), (), s32[]{:S(2)}) async-start(), calls=%async_computation.18 | async-start | bytes 5308416 | tf_op jit(solution)/shard_map/all_gather | solution.py:189
  60.6 77.8 %copy-start.19 = (bf16[1,2,256,768]{3,2,1,0:T(8,128)(2,1)}, bf16[1,2,256,768]{3,2,1,0:T(8,128)(2,1)S(1)}, u32[]{:S(2)}) copy-start(bf16[1,2,256,768]{3,2,1,0:T(8,128)(2,1)S(1)} %get-tuple-element.502) | copy-start | bytes 2359300
  60.6 147.9 %copy-start.22 = (bf16[1,2,256,768]{3,2,1,0:T(8,128)(2,1)}, bf16[1,2,256,768]{3,2,1,0:T(8,128)(2,1)S(1)}, u32[]{:S(2)}) copy-start(bf16[1,2,256,768]{3,2,1,0:T(8,128)(2,1)S(1)} %get-tuple-element.501) | copy-start | bytes 2359300
  153.2 72.0 %all-to-all-start.2 = ((bf16[3,2,256,4,192]{2,1,4,0,3:T(2,128)(2,1)}), bf16[3,2,256,4,192]{2,1,4,0,3:T(2,128)(2,1)S(1)}, u32[]{:S(2)}, u32[]{:S(2)}) async-start(bf16[3,2,256,4,192]{2,1,4,0,3:T(2,128)(2,1)} %copy.126), calls=%async_computation.2 | async-start | bytes 4718592 | tf_op jit(solution)/shard_map/all_to_all | solution.py:223
  225.2 38.8 %all-to-all-start = ((bf16[3,2,256,4,192]{2,1,4,0,3:T(2,128)(2,1)}), bf16[3,2,256,4,192]{2,1,4,0,3:T(2,128)(2,1)}, u32[]{:S(2)}, u32[]{:S(2)}) async-start(bf16[3,2,256,4,192]{2,1,4,0,3:T(2,128)(2,1)} %copy.118), calls=%async_computation | async-start | bytes 4718592 | tf_op jit(solution)/shard_map/all_to_all | solution.py:223
  259.5 12.4 copy-start
  259.5 12.3 copy-start.4
  259.5 12.3 copy-start.6
  259.5 12.3 copy-start.81
  264.0 41.4 %all-to-all-start.3 = ((bf16[2,4,256,192]{2,0,3,1:T(2,128)(2,1)}), bf16[2,4,256,192]{2,0,3,1:T(2,128)(2,1)}, u32[]{:S(2)}, u32[]{:S(2)}) async-start(bf16[2,4,256,192]{2,0,3,1:T(2,128)(2,1)} %copy.130), calls=%async_computation.3 | async-start | bytes 1572864 | tf_op jit(solution)/shard_map/all_to_all | solution.py:226
  300.9 39.4 %copy-start.2 = (bf16[2,1024,192]{1,2,0:T(8,128)(2,1)}, bf16[2,1024,192]{1,2,0:T(8,128)(2,1)S(1)}, u32[]{:S(2)}) copy-start(bf16[2,1024,192]{1,2,0:T(8,128)(2,1)S(1)} %get-tuple-element.1036) | copy-start | bytes 2359300
  300.9 39.4 %copy-start.8 = (bf16[2,1024,192]{1,2,0:T(8,128)(2,1)}, bf16[2,1024,192]{1,2,0:T(8,128)(2,1)S(1)}, u32[]{:S(2)}) copy-start(bf16[2,1024,192]{1,2,0:T(8,128)(2,1)S(1)} %get-tuple-element.1039) | copy-start | bytes 2359300
  301.0 39.4 %copy-start.10 = (bf16[2,1024,192]{1,2,0:T(8,128)(2,1)}, bf16[2,1024,192]{1,2,0:T(8,128)(2,1)S(1)}, u32[]{:S(2)}) copy-start(bf16[2,1024,192]{1,2,0:T(8,128)(2,1)S(1)} %get-tuple-element.1040) | copy-start | bytes 2359300
  301.0 39.4 %copy-start.85 = (f32[2,3,1024,1]{2,1,3,0:T(4,128)}, f32[2,3,1024,1]{2,1,3,0:T(4,128)S(1)}, u32[]{:S(2)}) copy-start(f32[2,3,1024,1]{2,1,3,0:T(4,128)S(1)} %get-tuple-element.958) | copy-start | bytes 73732
  305.4 38.5 %copy-start.23 = (bf16[1,2,256,768]{3,2,1,0:T(8,128)(2,1)S(1)}, bf16[1,2,256,768]{3,2,1,0:T(8,128)(2,1)}, u32[]{:S(2)}) copy-start(bf16[1,2,256,768]{3,2,1,0:T(8,128)(2,1)} %copy-done.22) | copy-start | bytes 2359300
  305.4 37.1 %all-to-all-start.1 = ((bf16[2,4,256,192]{2,0,3,1:T(2,128)(2,1)}), bf16[2,4,256,192]{2,0,3,1:T(2,128)(2,1)}, u32[]{:S(2)}, u32[]{:S(2)}) async-start(bf16[2,4,256,192]{2,0,3,1:T(2,128)(2,1)} %copy.122), calls=%async_computation.1 | async-start | bytes 1572864 | tf_op jit(solution)/shard_map/all_to_all | solution.py:226
  309.8 81.6 %all-gather.20.cloned.1.call-start = ((), (), s32[]{:S(2)}) async-start(), calls=%async_computation.19 | async-start | bytes 5308416 | tf_op jit(solution)/shard_map/all_gather | solution.py:191
  310.4 117.1 %copy-start.89 = (f32[768]{0:T(1024)}, f32[768]{0:T(1024)S(1)}, u32[]{:S(2)}) copy-start(f32[768]{0:T(1024)S(1)} %convert_element_type.299) | copy-start | bytes 9220
  310.4 87.5 %copy-start.91 = (f32[768]{0:T(1024)}, f32[768]{0:T(1024)S(1)}, u32[]{:S(2)}) copy-start(f32[768]{0:T(1024)S(1)} %convert_element_type.300) | copy-start | bytes 9220
  346.4 74.7 %copy-start.106 = (f32[512]{0:T(512)}, f32[512]{0:T(512)S(1)}, u32[]{:S(2)}) copy-start(f32[512]{0:T(512)S(1)} %broadcast_multiply_fusion.9) | copy-start | bytes 6148
  346.8 74.4 %copy-start.120 = (f32[512]{0:T(512)}, f32[512]{0:T(512)S(1)}, u32[]{:S(2)}) copy-start(f32[512]{0:T(512)S(1)} %add_rsqrt_fusion.3) | copy-start | bytes 6148
  347.7 79.8 %copy-start.12 = (f32[512,768]{1,0:T(8,128)}, f32[512,768]{1,0:T(8,128)S(1)}, u32[]{:S(2)}) copy-start(f32[512,768]{1,0:T(8,128)S(1)} %get-tuple-element.516) | copy-start | bytes 4718596
  347.8 79.8 %copy-start.93 = (f32[512]{0:T(512)}, f32[512]{0:T(512)S(1)}, u32[]{:S(2)}) copy-start(f32[512]{0:T(512)S(1)} %broadcast_multiply_fusion.7) | copy-start | bytes 6148
  348.1 79.5 %copy-start.95 = (f32[512]{0:T(512)}, f32[512]{0:T(512)S(1)}, u32[]{:S(2)}) copy-start(f32[512]{0:T(512)S(1)} %add_rsqrt_fusion.1) | copy-start | bytes 6148
  402.8 13.0 slice-start.2
  405.7 15.4 %copy-start.33 = (f32[512,768]{1,0:T(8,128)}, f32[512,768]{1,0:T(8,128)S(1)}, u32[]{:S(2)}) copy-start(f32[512,768]{1,0:T(8,128)S(1)} %get-tuple-element.421) | copy-start | bytes 4718596
  432.0 15.1 %all-to-all-start.6 = ((bf16[2,256,4,192]{1,0,3,2:T(2,128)(2,1)}), bf16[2,256,4,192]{1,0,3,2:T(2,128)(2,1)S(1)}, u32[]{:S(2)}, u32[]{:S(2)}) async-start(bf16[2,256,4,192]{1,0,3,2:T(2,128)(2,1)} %reshape.867), calls=%async_computation.6 | async-start | bytes 1572864 | tf_op jit(solution)/shard_map/all_to_all | solution.py:261
  447.1 15.1 %all-to-all-start.4 = ((bf16[2,256,4,192]{1,0,3,2:T(2,128)(2,1)}), bf16[2,256,4,192]{1,0,3,2:T(2,128)(2,1)S(1)}, u32[]{:S(2)}, u32[]{:S(2)}) async-start(bf16[2,256,4,192]{1,0,3,2:T(2,128)(2,1)} %reshape.865), calls=%async_computation.4 | async-start | bytes 1572864 | tf_op jit(solution)/shard_map/all_to_all | solution.py:261
  452.6 15.8 %copy-start.3 = (bf16[2,1024,192]{1,2,0:T(8,128)(2,1)S(1)}, bf16[2,1024,192]{1,2,0:T(8,128)(2,1)}, u32[]{:S(2)}) copy-start(bf16[2,1024,192]{1,2,0:T(8,128)(2,1)} %copy-done.2) | copy-start | bytes 2359300
  452.6 15.8 %copy-start.9 = (bf16[2,1024,192]{1,2,0:T(8,128)(2,1)S(1)}, bf16[2,1024,192]{1,2,0:T(8,128)(2,1)}, u32[]{:S(2)}) copy-start(bf16[2,1024,192]{1,2,0:T(8,128)(2,1)} %copy-done.8) | copy-start | bytes 2359300
  452.6 15.8 %copy-start.11 = (bf16[2,1024,192]{1,2,0:T(8,128)(2,1)S(1)}, bf16[2,1024,192]{1,2,0:T(8,128)(2,1)}, u32[]{:S(2)}) copy-start(bf16[2,1024,192]{1,2,0:T(8,128)(2,1)} %copy-done.10) | copy-start | bytes 2359300
  452.6 15.8 %copy-start.84 = (s32[1,2,1024]{2,1,0:T(2,128)S(1)}, s32[1,2,1024]{2,1,0:T(2,128)}, u32[]{:S(2)}) copy-start(s32[1,2,1024]{2,1,0:T(2,128)} %all-gather) | copy-start | bytes 24580
  452.6 15.8 %copy-start.86 = (f32[2,3,1024,1]{2,1,3,0:T(4,128)S(1)}, f32[2,3,1024,1]{2,1,3,0:T(4,128)}, u32[]{:S(2)}) copy-start(f32[2,3,1024,1]{2,1,3,0:T(4,128)} %copy-done.85) | copy-start | bytes 73732
  521.4 60.6 %all-to-all-start.5 = ((bf16[3,2,4,256,192]{3,1,4,0,2:T(2,128)(2,1)}), bf16[3,2,4,256,192]{3,1,4,0,2:T(2,128)(2,1)}, u32[]{:S(2)}, u32[]{:S(2)}) async-start(bf16[3,2,4,256,192]{3,1,4,0,2:T(2,128)(2,1)} %copy.133), calls=%async_computation.5 | async-start | bytes 4718592 | tf_op jit(solution)/shard_map/all_to_all | solution.py:275
  582.1 32.1 %all-to-all-start.7 = ((bf16[3,2,4,256,192]{3,1,4,0,2:T(2,128)(2,1)}), bf16[3,2,4,256,192]{3,1,4,0,2:T(2,128)(2,1)S(1)}, u32[]{:S(2)}, u32[]{:S(2)}) async-start(bf16[3,2,4,256,192]{3,1,4,0,2:T(2,128)(2,1)} %copy.136), calls=%async_computation.7 | async-start | bytes 4718592 | tf_op jit(solution)/shard_map/all_to_all | solution.py:275
  585.7 102.2 %reduce-scatter.19.cloned.1.call-start = ((), (), s32[]{:S(2)}) async-start(), calls=%async_computation.23 | async-start | bytes 2654208
  620.7 139.5 %reduce-scatter.23.cloned.1.call-start = ((), (), s32[]{:S(2)}) async-start(), calls=%async_computation.25 | async-start | bytes 2654208
  629.2 203.3 %reduce-scatter.21.cloned.1.call-start = ((), (), s32[]{:S(2)}) async-start(), calls=%async_computation.24 | async-start | bytes 2654208
  634.2 270.6 %reduce-scatter.13.cloned.1.call-start = ((), (), s32[]{:S(2)}) async-start(), calls=%async_computation.20 | async-start | bytes 2654208 | tf_op jit(solution)/shard_map/reduce_scatter | solution.py:310
  639.9 429.8 %reduce-scatter.15.cloned.1.call-start = ((), (), s32[]{:S(2)}) async-start(), calls=%async_computation.21 | async-start | bytes 10616832 | tf_op jit(solution)/shard_map/reduce_scatter | solution.py:314
  651.4 583.0 %reduce-scatter.17.cloned.1.call-start = ((), (), s32[]{:S(2)}) async-start(), calls=%async_computation.22 | async-start | bytes 10616832 | tf_op jit(solution)/shard_map/reduce_scatter | solution.py:316
  662.2 654.6 %all-reduce.23.cloned.1.call-start = ((), (), s32[]{:S(2)}) async-start(), calls=%async_computation.26 | async-start | bytes 7667712 | tf_op jit(solution)/shard_map/psum | solution.py:321
  1234.4 46.6 %copy-start.46 = (bf16[96,8,2,256]{3,1,2,0:T(8,128)(2,1)S(1)}, bf16[96,8,2,256]{3,1,2,0:T(8,128)(2,1)}, u32[]{:S(2)}) copy-start(bf16[96,8,2,256]{3,1,2,0:T(8,128)(2,1)} %copy-done.45) | copy-start | bytes 2359300
  1234.4 48.9 %copy-start.72 = (bf16[96,8,2,256]{3,1,2,0:T(8,128)(2,1)S(1)}, bf16[96,8,2,256]{3,1,2,0:T(8,128)(2,1)}, u32[]{:S(2)}) copy-start(bf16[96,8,2,256]{3,1,2,0:T(8,128)(2,1)} %copy-done.71) | copy-start | bytes 2359300
  (121 other events, 452.1 us)
Sparse Core Ops, SparseCore 0:
  10.2 44.0 all-gather.13
  56.5 39.8 all-gather.11
  98.5 39.8 all-gather.9
  140.4 39.8 all-gather.15
  182.3 77.9 all-gather.17
  312.4 78.8 all-gather.19
  620.8 67.0 reduce-scatter.18
  691.4 68.6 reduce-scatter.22
  763.6 68.7 reduce-scatter.20
  835.8 68.9 reduce-scatter.12
  908.3 161.2 reduce-scatter.14
  1073.1 161.2 reduce-scatter.16
  1237.8 78.9 all-reduce.22
where the time goes:
time: 1340 us; the launch traced here: 1330 us
  waiting for transfers between devices  694 us (52%)
  matrix products  220 us (16%)
  local copies, waits for them, and re-layouts  150 us (11%)
  blocking collectives  144 us (11%)
  other arithmetic  70.9 us (5%)
  starting transfers between devices  33.5 us (2%)
  between operations  18.5 us (1%)
    reduce_scatter x1, waiting for transfers between devices, body(): lax.psum_scatter(totals[9], 'fsdp', scatter_dimension=0, tiled=True)  165 us
    reduce_scatter x1, waiting for transfers between devices, body(): lax.psum_scatter(totals[11], 'fsdp', scatter_dimension=0, tiled=True)  165 us
    unnamed x16, waiting for transfers between devices  155 us
    unnamed x2, blocking collectives  75.4 us
    reduce_scatter x1, waiting for transfers between devices, body(): lax.psum_scatter(totals[5], 'fsdp', scatter_dimension=0, tiled=True)  70.4 us
    unnamed x297, local copies, waits for them, and re-layouts  46.2 us
    dot_general x12, matrix products, times_transposed(): lax.dot_general(left, right, (((1,), (1,)), ((), ())), preferred_element_...  37.2 us
    all_gather x1, waiting for transfers between devices, body(): lax.all_gather(query_weight, 'fsdp', axis=0, tiled=True)  36.6 us
  transfers between devices with their start and end apart: 21, of which 13 were waited for; matrix products, arithmetic and copies ran while one was open for 24% of the time, Pallas kernels for 0%

commit v1 on v0

v1 whole, which is shorter than its diff:
```python
import math

import jax
import jax.numpy as jnp
from jax import lax
from jax.experimental import pallas as pl
from jax.experimental.pallas import tpu as pltpu
from jax.sharding import PartitionSpec as P

F32=jnp.float32; BF=jnp.bfloat16
PAIR=128; HD=64; BIG=1e30

def dot_nn(a,b): return lax.dot_general(a,b,(((1,),(0,)),((),())),preferred_element_type=F32)
def dot_nt(a,b): return lax.dot_general(a,b,(((1,),(1,)),((),())),preferred_element_type=F32)
def dot_tn(a,b): return lax.dot_general(a,b,(((0,),(0,)),((),())),preferred_element_type=F32)

def split3(v):
    hi=v.astype(BF); r=v-hi.astype(F32); mid=r.astype(BF); lo=(r-mid.astype(F32)).astype(BF)
    return hi,mid,lo

def fwd_kernel(doc_ref,q_ref,k_ref,v_ref,o_ref,lse_ref,qa,ka,va):
    rows=q_ref.shape[0]
    lane=lax.broadcasted_iota(jnp.int32,(rows,PAIR),1)
    doc=doc_ref[...]
    for h in range(2):
        base=(1-h)*HD
        mine=(lane>=h*HD)&(lane<(h+1)*HD)
        same=(lane-base)==doc
        qa[...]=jnp.where(mine,q_ref[...]*jnp.asarray(0.125,BF),jnp.where(same,1.0,0.0).astype(BF))
        ka[...]=jnp.where(mine,k_ref[...],jnp.where(same|(lane<base)|(lane>=base+8),0.0,-BIG).astype(BF))
        va[...]=jnp.where(mine,v_ref[...],jnp.ones((),BF))
        bq=256
        for i in range(rows//bq):
            sl=slice(i*bq,(i+1)*bq)
            sc=dot_nt(qa[sl,:],ka[...])
            m=jnp.max(sc,axis=1,keepdims=True)
            p=jnp.exp(sc-m).astype(BF)
            o=dot_nn(p,va[...])
            l=o[:,base:base+1]
            lse_ref[sl,h:h+1]=m+jnp.log(l)
            out=(o/l).astype(BF)
            if h==0: o_ref[sl,:]=out
            else: o_ref[sl,:]=jnp.where(lane[sl,:]>=HD,out,o_ref[sl,:])

def attend(doc,qkv,interpret=False):
    rows=qkv.shape[0]; pairs=qkv.shape[1]//3//PAIR
    return pl.pallas_call(fwd_kernel,grid=(pairs,),
        in_specs=[pl.BlockSpec((rows,1),lambda h:(0,0))]+[pl.BlockSpec((rows,PAIR),lambda h,j=j:(0,h+j*pairs)) for j in range(3)],
        out_specs=[pl.BlockSpec((rows,PAIR),lambda h:(0,h)),pl.BlockSpec((None,rows,2),lambda h:(h,0,0))],
        out_shape=[jax.ShapeDtypeStruct((rows,pairs*PAIR),BF),jax.ShapeDtypeStruct((pairs,rows,2),F32)],
        scratch_shapes=[pltpu.VMEM((rows,PAIR),BF)]*3,
        compiler_params=pltpu.CompilerParams(vmem_limit_bytes=60<<20),
        cost_estimate=pl.CostEstimate(flops=4*rows*rows*PAIR*pairs*2,bytes_accessed=rows*PAIR*pairs*8,transcendentals=rows*rows*pairs*2),
        name="attend")(doc,qkv,qkv,qkv)

def bwd_kernel(doc_ref,q_ref,k_ref,v_ref,o_ref,do_ref,lse_ref,dq_ref,dk_ref,dv_ref,qa,ka,va,da,dqs):
    rows=q_ref.shape[0]
    lane=lax.broadcasted_iota(jnp.int32,(rows,PAIR),1)
    doc=doc_ref[...]
    dof=do_ref[...].astype(F32)*o_ref[...].astype(F32)
    for h in range(2):
        base=(1-h)*HD
        mine=(lane>=h*HD)&(lane<(h+1)*HD)
        rel=lane-base
        same=rel==doc
        delta=jnp.sum(jnp.where(mine,dof,0.0),axis=1,keepdims=True)
        lh,lm,ll=split3(-lse_ref[:,h:h+1]); dh,dm,dl=split3(-delta)
        one=jnp.ones((),BF); zero=jnp.zeros((),BF)
        aug_q=jnp.where(same,one,zero)
        aug_q=jnp.where(rel==8,lh,jnp.where(rel==9,lm,jnp.where(rel==10,ll,aug_q)))
        aug_k=jnp.where((rel>=0)&(rel<8)&(~same),jnp.asarray(-BIG,BF),zero)
        aug_k=jnp.where((rel>=8)&(rel<11),one,aug_k)
        aug_d=jnp.where(rel==8,dh,jnp.where(rel==9,dm,jnp.where(rel==10,dl,zero)))
        aug_v=jnp.where((rel>=8)&(rel<11),one,zero)
        qa[...]=jnp.where(mine,q_ref[...]*jnp.asarray(0.125,BF),aug_q)
        ka[...]=jnp.where(mine,k_ref[...],aug_k)
        va[...]=jnp.where(mine,v_ref[...],aug_v)
        da[...]=jnp.where(mine,do_ref[...],aug_d)
        bk=256
        for i in range(rows//bk):
            sl=slice(i*bk,(i+1)*bk)
            st=dot_nt(ka[sl,:],qa[...])
            pt=jnp.exp(st)
            dpt=dot_nt(va[sl,:],da[...])
            dst=(pt*dpt).astype(BF)
            dv=dot_nn(pt.astype(BF),da[...])
            dk=dot_nn(dst,qa[...])
            dq=dot_tn(dst,ka[sl,:])
            if i==0: dqs[...]=dq
            else: dqs[...]+=dq
            msl=mine[sl,:]
            if h==0:
                dv_ref[sl,:]=dv.astype(BF); dk_ref[sl,:]=dk.astype(BF)
            else:
                dv_ref[sl,:]=jnp.where(msl,dv.astype(BF),dv_ref[sl,:]); dk_ref[sl,:]=jnp.where(msl,dk.astype(BF),dk_ref[sl,:])
        dqv=(dqs[...]*0.125).astype(BF)
        if h==0: dq_ref[...]=dqv
        else: dq_ref[...]=jnp.where(mine,dqv,dq_ref[...])

def attend_back(doc,qkv,att,datt,lse,first=0,count=None):
    rows=qkv.shape[0]; pairs=qkv.shape[1]//3//PAIR
    n=count or pairs
    col=lambda h:(0,h+first)
    return pl.pallas_call(bwd_kernel,grid=(n,),
        in_specs=[pl.BlockSpec((rows,1),lambda h:(0,0))]+[pl.BlockSpec((rows,PAIR),lambda h,j=j:(0,h+first+j*pairs)) for j in range(3)]
          +[pl.BlockSpec((rows,PAIR),col),pl.BlockSpec((rows,PAIR),col),pl.BlockSpec((None,rows,2),lambda h:(h+first,0,0))],
        out_specs=[pl.BlockSpec((rows,PAIR),lambda h:(0,h))]*3,
        out_shape=[jax.ShapeDtypeStruct((rows,n*PAIR),BF)]*3,
        scratch_shapes=[pltpu.VMEM((rows,PAIR),BF)]*4+[pltpu.VMEM((rows,PAIR),F32)],
        compiler_params=pltpu.CompilerParams(vmem_limit_bytes=60<<20),
        cost_estimate=pl.CostEstimate(flops=10*rows*rows*PAIR*n*2,bytes_accessed=rows*PAIR*n*16,transcendentals=rows*rows*n*2),
        name="attend_back")(doc,qkv,qkv,qkv,att,datt,lse)

norm_eps = 1e-12


def normalize(values, gain, shift):
    center = values - jnp.mean(values, axis=-1, keepdims=True)
    spread = jnp.mean(center * center, axis=-1, keepdims=True)
    rstd = lax.rsqrt(spread + norm_eps)
    hat = center * rstd
    return hat * gain.astype(F32) + shift.astype(F32), hat, rstd


def normalize_back(grad_out, hat, rstd, gain):
    scaled = grad_out * gain.astype(F32)
    first_mean = jnp.mean(scaled, axis=-1, keepdims=True)
    second_mean = jnp.mean(scaled * hat, axis=-1, keepdims=True)
    return rstd * (scaled - first_mean - hat * second_mean)


def gelu_slope(values):
    cumulative = 0.5 * (1.0 + lax.erf(values * (1.0 / math.sqrt(2.0))))
    density = jnp.exp(-0.5 * values * values) * (1.0 / math.sqrt(2.0 * math.pi))
    return cumulative + values * density


def swap(value, axis, mask):
    size = lax.axis_size(axis)
    return lax.ppermute(value, axis, [(i, i ^ mask) for i in range(size)])


def bits_of(count):
    return [1 << i for i in reversed(range(count.bit_length() - 1))]


def pick(flag, low, high):
    return jnp.where(flag == 0, low, high)


def gather_full(shard, owners):
    core = lax.axis_index("seq") & 1
    index = lax.axis_index("fsdp")
    half = shard.shape[1] // 2
    held = pick(core, shard[:, :half], shard[:, half:])[None]
    for bit in bits_of(owners):
        other = swap(held, "fsdp", bit)
        flag = (index // bit) & 1
        held = pick(flag, jnp.stack([held, other], axis=1), jnp.stack([other, held], axis=1))
        held = held.reshape((-1,) + held.shape[2:])
    other = swap(held, "seq", 1)
    return pick(core, jnp.concatenate([held, other], axis=2), jnp.concatenate([other, held], axis=2))


def reduce_to_owner(lower, upper, owners):
    core = lax.axis_index("seq") & 1
    index = lax.axis_index("fsdp")
    parts = [pick(core, lower, upper), swap(pick(core, upper, lower), "seq", 1)]
    for bit in reversed(bits_of(owners)):
        flag = (index // bit) & 1
        pairs = [part.reshape((-1, 2) + part.shape[1:]) for part in parts]
        sent = sum(pick(flag, pair[:, 1], pair[:, 0]).astype(F32) for pair in pairs).astype(BF)
        parts = [pick(flag, pair[:, 0], pair[:, 1]) for pair in pairs]
        parts.append(swap(sent, "fsdp", bit))
    own = sum(part[0].astype(F32) for part in parts).astype(BF)
    total = own.astype(F32) + swap(own, "seq", 2).astype(F32)
    other = swap(total, "seq", 1)
    return pick(core, total, other), pick(core, other, total)


def body(
    tokens, segment_ids, out_cotangent, query_weight, query_bias, key_weight, value_weight, value_bias,
    output_weight, output_bias, attn_gain, attn_shift, inner_weight, inner_bias, outer_weight, outer_bias,
    final_gain, final_shift,
):
    groups = lax.axis_size("seq")
    owners = lax.axis_size("fsdp")
    micro, seq_count, local_len, width = tokens.shape
    assert micro * seq_count == groups
    rows = groups * local_len
    shard = query_weight.shape[0]
    hidden = inner_weight.shape[1]
    wide = hidden // owners

    def to_sequences(value):
        return lax.all_to_all(value.reshape((groups, local_len) + value.shape[3:]), "seq", 0, 0, tiled=True)

    x_rows = to_sequences(tokens).reshape(rows, width)
    doc = to_sequences(segment_ids).reshape(rows, 1)
    small = jnp.concatenate(
        [query_bias, value_bias, output_bias, attn_gain, attn_shift, outer_bias, final_gain, final_shift, inner_bias]
    )
    small = jnp.pad(small, (0, 3 * width - small.shape[0]))[None]
    small = jnp.concatenate([small, jnp.zeros((15, 3 * width), BF)], axis=0)
    shard_a = jnp.concatenate(
        [jnp.concatenate([query_weight, key_weight, value_weight], axis=1), small], axis=0
    )
    full_a = gather_full(shard_a, owners)
    qkv_mat = full_a[:, :shard].reshape(width, 3 * width)
    vectors = full_a[:, shard, :]
    query_vec, value_vec, output_vec, gain_first, shift_first, outer_vec, gain_final, shift_final = (
        vectors[:, i * shard : (i + 1) * shard].reshape(width) for i in range(8)
    )
    inner_vec = vectors[:, 8 * shard : 8 * shard + wide].reshape(hidden)
    full_b = gather_full(jnp.concatenate([inner_weight, output_weight], axis=1), owners)
    inner_mat = full_b[:, :, :hidden].reshape(width, hidden)
    output_mat = full_b[:, :, hidden:].reshape(width, width)
    outer_mat = gather_full(outer_weight, owners).reshape(hidden, width)

    qkv_vec = jnp.concatenate([query_vec, jnp.zeros_like(query_vec), value_vec]).astype(F32)
    qkv = (jnp.dot(x_rows, qkv_mat, preferred_element_type=F32) + qkv_vec).astype(BF)
    attended, logsums = attend(doc, qkv)
    first = x_rows.astype(F32) + dot_nn(attended, output_mat) + output_vec.astype(F32)
    normed, hat_first, rstd_first = normalize(first, gain_first, shift_first)
    normed_low = normed.astype(BF)
    inner = dot_nn(normed_low, inner_mat) + inner_vec.astype(F32)
    active = jax.nn.gelu(inner, approximate=False).astype(BF)
    second = normed + dot_nn(active, outer_mat) + outer_vec.astype(F32)
    result, hat_second, rstd_second = normalize(second, gain_final, shift_final)

    def to_tokens(value):
        moved = lax.all_to_all(value.reshape(groups, local_len, width), "seq", 0, 0, tiled=True)
        return moved.reshape(micro, seq_count, local_len, width)

    layer_out = to_tokens(result.astype(BF))
    grad_out = to_sequences(out_cotangent).reshape(rows, width).astype(F32)
    dsecond = normalize_back(grad_out, hat_second, rstd_second, gain_final)
    dbranch_two = dsecond.astype(BF)
    douter = dot_tn(active, dbranch_two).astype(BF).reshape(owners, 2, wide // 2, width)
    douter_sum = jnp.concatenate(reduce_to_owner(douter[:, 0], douter[:, 1], owners), axis=0)
    dactive = dot_nt(dbranch_two, outer_mat)
    dinner = (dactive * gelu_slope(inner)).astype(BF)
    dinner_mat = dot_tn(normed_low, dinner).astype(BF).reshape(owners, shard, hidden)
    dinner_sum = jnp.concatenate(
        reduce_to_owner(dinner_mat[:, :, : hidden // 2], dinner_mat[:, :, hidden // 2 :], owners), axis=1
    )
    dnormed = dsecond + dot_nt(dinner, inner_mat)
    dfirst = normalize_back(dnormed, hat_first, rstd_first, gain_first)
    dbranch = dfirst.astype(BF)
    dattended = dot_nt(dbranch, output_mat).astype(BF)
    dquery, dkey, dvalue = attend_back(doc, qkv, attended, dattended, logsums)
    dqkv = jnp.concatenate([dquery, dkey, dvalue], axis=1)
    input_grad = to_tokens((dfirst + dot_nt(dqkv, qkv_mat)).astype(BF)).astype(F32)
    dqkv_mat = dot_tn(x_rows, dqkv).astype(BF).reshape(owners, shard, 3 * width)
    doutput = dot_tn(attended, dbranch).astype(BF).reshape(owners, shard, width)

    def column_sum(value):
        return jnp.sum(value.astype(F32), axis=0)

    smalls = (
        column_sum(dquery), column_sum(dvalue), column_sum(dbranch), jnp.sum(dnormed * hat_first, axis=0),
        jnp.sum(dnormed, axis=0), column_sum(dbranch_two), jnp.sum(grad_out * hat_second, axis=0),
        jnp.sum(grad_out, axis=0),
    )
    packed = jnp.concatenate(
        [value.reshape(owners, shard) for value in smalls] + [column_sum(dinner).reshape(owners, wide)], axis=1
    )
    packed = jnp.pad(packed, ((0, 0), (0, 2 * width - packed.shape[1]))).astype(BF).reshape(owners, 2, 1, width)
    packed = jnp.pad(packed, ((0, 0), (0, 0), (0, 15), (0, 0)))
    lower = jnp.concatenate([dqkv_mat[:, :, :width], dqkv_mat[:, :, width : 2 * width], packed[:, 0]], axis=1)
    upper = jnp.concatenate([dqkv_mat[:, :, 2 * width :], doutput, packed[:, 1]], axis=1)
    lower, upper = reduce_to_owner(lower, upper, owners)
    flat = jnp.concatenate([lower[2 * shard], upper[2 * shard]])
    vecs = [flat[i * shard : (i + 1) * shard] for i in range(8)]
    dinner_vec = flat[8 * shard : 8 * shard + wide]
    return (
        layer_out, input_grad, lower[:shard], vecs[0], lower[shard : 2 * shard], upper[:shard], vecs[1],
        upper[shard : 2 * shard], vecs[2], vecs[3], vecs[4], dinner_sum, dinner_vec, douter_sum, vecs[5], vecs[6],
        vecs[7],
    )


def solution(mesh):
    rows = P(None, "fsdp", "seq", None)
    mat = P("fsdp", None)
    vec = P("fsdp")
    return jax.shard_map(
        body,
        mesh=mesh,
        in_specs=(
            rows, P(None, "fsdp", "seq"), rows, mat, vec, mat, mat, vec, mat, vec, vec, vec, mat, vec, mat, vec, vec, vec,
        ),
        out_specs=(rows, rows, mat, vec, mat, mat, vec, mat, vec, vec, vec, mat, vec, mat, vec, vec, vec),
        check_vma=False,
    )
```

time: 1340 us -> 557 us (0.42)
  waiting for transfers between devices: 694 us -> 196 us
  blocking collectives: 144 us -> 0 us
  local copies, waits for them, and re-layouts: 150 us -> 33.8 us
  matrix products: 220 us -> 113 us
  Pallas kernels: 0 us -> 72.7 us
  starting transfers between devices: 33.5 us -> 50.9 us
  between operations: 18.5 us -> 2.04 us
    reduce_scatter x3 -> x0, waiting for transfers between devices: 400 us -> none  [the longest x1 165 us: body(): lax.psum_scatter(totals[9], 'fsdp', scatter_dimension=0, tiled=True)]
    ppermute x0 -> x30, waiting for transfers between devices: none -> 180 us  [swap(): return lax.ppermute(value, axis, [(i, i ^ mask) for i in range(size)])]
    unnamed x16 -> x0, waiting for transfers between devices: 155 us -> none
    dot_general x92 -> x12, matrix products: 220 us -> 113 us  [the longest x3 49.3 us: dot_nn(): lax.dot_general(a, b, (((1,), (0,)), ((), ())), preferred_element_type=F32)]
    unnamed x2 -> x0, blocking collectives: 75.4 us -> none
    all_gather x6 -> x0, waiting for transfers between devices: 73.5 us -> none  [the longest x1 36.6 us: body(): lax.all_gather(query_weight, 'fsdp', axis=0, tiled=True)]
    pallas_call x0 -> x2, Pallas kernels: none -> 72.7 us  [the longest x1 43.5 us: attend_back(): pl.pallas_call(bwd_kernel, grid=(n,), in_specs=[pl.BlockSpec((rows, 1), l...]
    all_gather x3 -> x0, blocking collectives: 62.3 us -> none  [the longest x2 35.2 us: body(): doc_full = lax.all_gather(segment_ids[batch], 'seq', axis=1, tiled=True)]
  transfers between devices with their start and end apart: 21 -> 35, of which waited for: 13 -> 13; matrix products, arithmetic and copies ran while one was open for 24% -> 25% of each run, Pallas kernels for 0% -> 5%
where the time goes in v1:
time: 557 us; the launch traced here: 552 us
  waiting for transfers between devices  196 us (35%)
  matrix products  113 us (20%)
  other arithmetic  83.8 us (15%)
  Pallas kernels  72.7 us (13%)
  starting transfers between devices  50.9 us (9%)
  local copies, waits for them, and re-layouts  33.8 us (6%)
    ppermute x30, waiting for transfers between devices, swap(): return lax.ppermute(value, axis, [(i, i ^ mask) for i in range(size)])  180 us
    dot_general x3, matrix products, dot_nn(): lax.dot_general(a, b, (((1,), (0,)), ((), ())), preferred_element_type=F32)  49.3 us
    select_n x36, other arithmetic, pick(): return jnp.where(flag == 0, low, high)  44.7 us
    pallas_call x1, Pallas kernels, attend_back(): pl.pallas_call(bwd_kernel, grid=(n,), in_specs=[pl.BlockSpec((rows, 1), l...  43.5 us
    ppermute x30, starting transfers between devices, swap(): return lax.ppermute(value, axis, [(i, i ^ mask) for i in range(size)])  31.6 us
    dot_general x4, matrix products, dot_nt(): lax.dot_general(a, b, (((1,), (1,)), ((), ())), preferred_element_type=F32)  30.9 us
    pallas_call x1, Pallas kernels, attend(): pl.pallas_call(fwd_kernel, grid=(pairs,), in_specs=[pl.BlockSpec((rows, 1...  29.2 us
    dot_general x4, matrix products, dot_tn(): lax.dot_general(a, b, (((0,), (0,)), ((), ())), preferred_element_type=F32)  24.2 us
  transfers between devices with their start and end apart: 35, of which 13 were waited for; matrix products, arithmetic and copies ran while one was open for 25% of the time, Pallas kernels for 5%

profile of v1, /device:TPU:0, one launch (start us, length us, event | category | flops | bytes accessed | tf_op | source)
XLA Modules:
  0.0 551.9 jit_solution(4523061453077071874)
XLA Ops:
  0.7 6.2 %concatenate.143 = bf16[1152]{0:T(1024)(128)(2,1)S(1)} concatenate(bf16[96]{0:T(256)(128)(2,1)} %param.22, bf16[96]{0:T(256)(128)(2,1)} %param.25, bf16[96]{0:T(256)(128)(2,1)} %param.27, bf16[96]{0:T(256)(128)(2,1)} %param.28, bf16[96]{0:T(256)(128)(2,1)} %param.29, bf16[96]{0:T(256)(128)(2,1)} %param.33, bf16[96]{0:T(256)(128)(2,1)} %param.34, bf16[96]{0:T(256)(128)(2,1)} %param.35, ...), dimensions={0} | concatenate | bytes 4608 | tf_op jit(solution)/shard_map/concatenate | solution.py:200
  8.3 4.1 collective-permute-start
  13.7 3.2 all-to-all-start.1
  17.0 7.2 %collective-permute-done = bf16[1,112,1152]{2,1,0:T(8,128)(2,1)S(1)} collective-permute-done((bf16[1,112,1152]{2,1,0:T(8,128)(2,1)S(1)}, bf16[1,112,1152]{2,1,0:T(8,128)(2,1)S(1)}, u32[]{:S(2)}, u32[]{:S(2)}) %collective-permute-start) | collective-permute-done | bytes 258080 | tf_op jit(solution)/shard_map/ppermute | solution.py:140
  25.9 3.4 collective-permute-start.4
  29.6 19.6 %collective-permute-done.1 = bf16[2,112,1152]{2,1,0:T(8,128)(2,1)} collective-permute-done((bf16[2,112,1152]{2,1,0:T(8,128)(2,1)}, bf16[2,112,1152]{2,1,0:T(8,128)(2,1)}, u32[]{:S(2)}, u32[]{:S(2)}) %collective-permute-start.1) | collective-permute-done | bytes 516128 | tf_op jit(solution)/shard_map/ppermute | solution.py:140
  52.0 6.4 %collective-permute-done.8 = bf16[1,384,384]{2,1,0:T(8,128)(2,1)S(1)} collective-permute-done((bf16[1,384,384]{2,1,0:T(8,128)(2,1)S(1)}, bf16[1,384,384]{2,1,0:T(8,128)(2,1)S(1)}, u32[]{:S(2)}, u32[]{:S(2)}) %collective-permute-start.8) | collective-permute-done | bytes 294944 | tf_op jit(solution)/shard_map/ppermute | solution.py:140
  62.6 11.1 %collective-permute-done.2 = bf16[4,112,1152]{2,1,0:T(8,128)(2,1)S(1)} collective-permute-done((bf16[4,112,1152]{2,1,0:T(8,128)(2,1)S(1)}, bf16[4,112,1152]{2,1,0:T(8,128)(2,1)S(1)}, u32[]{:S(2)}, u32[]{:S(2)}) %collective-permute-start.2) | collective-permute-done | bytes 1032224 | tf_op jit(solution)/shard_map/ppermute | solution.py:140
  75.5 14.2 %collective-permute-done.5 = bf16[2,96,1920]{2,1,0:T(8,128)(2,1)S(1)} collective-permute-done((bf16[2,96,1920]{2,1,0:T(8,128)(2,1)S(1)}, bf16[2,96,1920]{2,1,0:T(8,128)(2,1)S(1)}, u32[]{:S(2)}, u32[]{:S(2)}) %collective-permute-start.5) | collective-permute-done | bytes 737312 | tf_op jit(solution)/shard_map/ppermute | solution.py:140
  91.5 3.6 all-to-all-start.3
  95.1 2.9 maximum_select_fusion.9
  99.6 15.5 %all-to-all-done.3 = bf16[4,256,768]{2,1,0:T(8,128)(2,1)S(1)} async-done(((bf16[4,256,768]{2,1,0:T(8,128)(2,1)}), bf16[4,256,768]{2,1,0:T(8,128)(2,1)S(1)}, u32[]{:S(2)}, u32[]{:S(2)}) %all-to-all-start.3) | async-done | bytes 1572896 | tf_op jit(solution)/shard_map/all_to_all | solution.py:196
  115.1 4.5 all-to-all-start
  120.6 27.3 %collective-permute-done.10 = bf16[4,384,384]{2,1,0:T(8,128)(2,1)} collective-permute-done((bf16[4,384,384]{2,1,0:T(8,128)(2,1)}, bf16[4,384,384]{2,1,0:T(8,128)(2,1)}, u32[]{:S(2)}, u32[]{:S(2)}) %collective-permute-start.10) | collective-permute-done | bytes 1179680 | tf_op jit(solution)/shard_map/ppermute | solution.py:140
  147.9 3.0 maximum_select_fusion.6
  152.5 2.4 maximum_select_fusion.3
  157.2 4.3 maximum_select_fusion.2
  164.8 8.5 %fusion.16.q_ref.k_ref.v_ref = bf16[1024,2304]{1,0:T(8,128)(2,1)} fusion(bf16[1024,768]{1,0:T(8,128)(2,1)} %bitcast.1, bf16[768,2304]{1,0:T(8,128)(2,1)} %bitcast.370, f32[2304]{0:T(1024)S(1)} %maximum_convert_fusion), kind=kOutput, calls=%fused_computation.31 | convolution fusion | flops 3628597248 | bytes 9839616 | tf_op jit(solution)/shard_map/dot_general | solution.py:221
  173.3 29.2 %attend.1 = (bf16[1024,768]{1,0:T(8,128)(2,1)}, f32[6,1024,2]{2,1,0:T(8,128)}) custom-call(s32[1024,1]{1,0:T(8,128)} %copy.119.doc_ref, bf16[1024,2304]{1,0:T(8,128)(2,1)} %fusion.16.q_ref.k_ref.v_ref, bf16[1024,2304]{1,0:T(8,128)(2,1)} %fusion.16.q_ref.k_ref.v_ref, bf16[1024,2304]{1,0:T(8,128)(2,1)} %fusion.16.q_ref.k_ref.v_ref), custom_call_target="tpu_custom_call" | custom-call | flops 6442450944 | bytes 6291456 | tf_op jit(solution)/shard_map/attend/pallas_call | solution.py:47
  202.5 5.7 %maximum_select_fusion = bf16[8,96,3840]{2,1,0:T(8,128)(2,1)S(1)} fusion(bf16[8,96,1920]{2,1,0:T(8,128)(2,1)} %collective-permute-done.7, bf16[8,96,1920]{2,1,0:T(8,128)(2,1)} %bitcast.20, pred[]{:T(512)S(6)} %eq.8), kind=kLoop, calls=%fused_computation.27 | loop fusion | flops 26542080 | bytes 11796481 | tf_op jit(solution)/shard_map/jit(_where)/select_n | solution.py:148
  210.2 2.9 fusion.63
  213.6 34.8 %fusion.2 = (bf16[1024,3072]{1,0:T(8,128)(2,1)S(1)}, f32[1024,3072]{1,0:T(8,128)}) fusion(f32[3072]{0:T(1024)S(1)} %reshape.1474, bf16[768,3072]{1,0:T(8,128)(2,1)S(1)} %bitcast.360, f32[1024,768]{1,0:T(8,128)S(1)} %get-tuple-element.82, f32[768]{0:T(1024)S(1)} %reshape.1473, f32[768]{0:T(1024)S(1)} %reshape.1472, f32[1024]{0:T(1024)S(1)} %add_rsqrt_fusion.1, ...), kind=kOutput, calls=%fused_computation.4 | convolution fusion | flops 5043388416 | bytes 26765312 | tf_op jit(solution)/shard_map/dot_general | solution.py:13
  248.5 11.6 %fusion.64 = (f32[1024]{0:T(1024)S(1)}, f32[1024,768]{1,0:T(8,128)S(1)}) fusion(f32[768]{0:T(1024)S(1)} %reshape.1475, bf16[1024,3072]{1,0:T(8,128)(2,1)S(1)} %get-tuple-element.83, bf16[3072,384]{1,0:T(8,128)(2,1)} %bitcast.32, bf16[3072,384]{1,0:T(8,128)(2,1)} %bitcast.30, pred[]{:T(512)S(6)} %eq.8, f32[768]{0:T(1024)S(1)} %reshape.1473, ...), kind=kOutput, calls=%fused_computation.210 | convolution fusion | flops 4858575872 | bytes 17323008 | tf_op jit(solution)/shard_map/dot_general | solution.py:13
  260.6 2.8 fusion.23
  265.0 7.0 %convolution_convert_fusion = bf16[3072,768]{1,0:T(8,128)(2,1)} fusion(bf16[1024,3072]{1,0:T(8,128)(2,1)S(1)} %bitcast.398, f32[1024,768]{1,0:T(8,128)S(1)} %get-tuple-element.34), kind=kOutput, calls=%fused_computation.28 | convolution fusion | flops 4834983936 | bytes 14155776 | tf_op jit(solution)/shard_map/dot_general | solution.py:15
  272.0 15.1 %fusion.65 = (bf16[3072]{0:T(1024)(128)(2,1)S(1)}, bf16[1024,3072]{1,0:T(8,128)(2,1)}) fusion(f32[1024,3072]{1,0:T(8,128)} %get-tuple-element.84, f32[3072]{0:T(1024)S(1)} %reshape.1474, bf16[3072,384]{1,0:T(8,128)(2,1)} %bitcast.32, bf16[3072,384]{1,0:T(8,128)(2,1)} %bitcast.30, pred[]{:T(512)S(6)} %eq.8, f32[1024,768]{1,0:T(8,128)S(1)} %get-tuple-element.34), kind=kOutput, calls=%fused_computation.211 | convolution fusion | flops 4891603968 | bytes 26757120 | tf_op jit(solution)/shard_map/dot_general | solution.py:14
  287.0 9.9 %convolution_convert_fusion.1 = bf16[768,3072]{1,0:T(8,128)(2,1)} fusion(bf16[1024,3072]{1,0:T(8,128)(2,1)} %get-tuple-element.89, f32[1024,768]{1,0:T(8,128)S(1)} %get-tuple-element.82, f32[768]{0:T(1024)S(1)} %reshape.1473, f32[768]{0:T(1024)S(1)} %reshape.1472, f32[1024]{0:T(1024)S(1)} %add_rsqrt_fusion.1, f32[1024]{0:T(1024)S(1)} %broadcast_multiply_fusion.4), kind=kOutput, calls=%fused_computation.29 | convolution fusion | flops 4838129664 | bytes 14170112 | tf_op jit(solution)/shard_map/dot_general | solution.py:15
  297.0 8.3 %multiply_reduce_fusion = (bf16[768]{0:T(1024)(128)(2,1)S(1)}, f32[1024]{0:T(1024)S(1)}, f32[1024]{0:T(1024)S(1)}, bf16[768]{0:T(1024)(128)(2,1)S(1)}, f32[1024,768]{1,0:T(8,128)S(1)}) fusion(f32[1024,768]{1,0:T(8,128)S(1)} %get-tuple-element.82, f32[1024]{0:T(1024)S(1)} %add_rsqrt_fusion.1, f32[1024]{0:T(1024)S(1)} %broadcast_multiply_fusion.4, ...), kind=kOutput, calls=%fused_computation.44 | convolution fusion | flops 4839698432 | bytes 20469760 | tf_op jit(solution)/shard_map/dot_general | solution.py:14
  306.6 2.6 convolution_convert_fusion.3.do_ref
  310.7 43.5 %attend_back.1 = (bf16[1024,768]{1,0:T(8,128)(2,1)}, bf16[1024,768]{1,0:T(8,128)(2,1)}, bf16[1024,768]{1,0:T(8,128)(2,1)}) custom-call(s32[1024,1]{1,0:T(8,128)} %copy.119.doc_ref, bf16[1024,2304]{1,0:T(8,128)(2,1)} %fusion.16.q_ref.k_ref.v_ref, bf16[1024,2304]{1,0:T(8,128)(2,1)} %fusion.16.q_ref.k_ref.v_ref, bf16[1024,2304]{1,0:T(8,128)(2,1)} %fusion.16.q_ref.k_ref.v_ref, ...), custom_call_target="tpu_custom_call" | custom-call | flops 16106127360 | bytes 12582912 | tf_op jit(solution)/shard_map/attend_back/pallas_call | solution.py:104
  360.9 4.2 broadcast_select_fusion
  367.5 2.8 slice-done.2
  370.4 5.8 %convolution_convert_fusion.2 = bf16[2304,768]{0,1:T(8,128)(2,1)S(1)} fusion(bf16[1024,2304]{1,0:T(8,128)(2,1)S(1)} %bitcast.392, bf16[1024,768]{1,0:T(8,128)(2,1)} %bitcast.1), kind=kOutput, calls=%fused_computation.30 | convolution fusion | flops 3625648128 | bytes 9830400 | tf_op jit(solution)/shard_map/dot_general | solution.py:15
  384.6 4.9 add_convert_fusion.1
  390.5 4.4 all-to-all-start.4
  394.8 3.1 fusion.28
  399.5 2.2 fusion.27
  406.0 2.5 fusion.25
  412.0 40.1 %collective-permute-done.19 = bf16[4,96,1536]{2,1,0:T(8,128)(2,1)S(1)} collective-permute-done((bf16[4,96,1536]{2,1,0:T(8,128)(2,1)S(1)}, bf16[4,96,1536]{2,1,0:T(8,128)(2,1)S(1)}, u32[]{:S(2)}, u32[]{:S(2)}) %collective-permute-start.19) | collective-permute-done | bytes 1179680 | tf_op jit(solution)/shard_map/ppermute | solution.py:140
  455.4 23.6 %collective-permute-done.13 = bf16[4,208,768]{2,1,0:T(8,128)(2,1)S(1)} collective-permute-done((bf16[4,208,768]{2,1,0:T(8,128)(2,1)S(1)}, bf16[4,208,768]{2,1,0:T(8,128)(2,1)S(1)}, u32[]{:S(2)}, u32[]{:S(2)}) %collective-permute-start.13) | collective-permute-done | bytes 1277984 | tf_op jit(solution)/shard_map/ppermute | solution.py:140
  485.4 11.3 %collective-permute-done.21 = bf16[1,96,1536]{2,1,0:T(8,128)(2,1)S(1)} collective-permute-done((bf16[1,96,1536]{2,1,0:T(8,128)(2,1)S(1)}, bf16[1,96,1536]{2,1,0:T(8,128)(2,1)S(1)}, u32[]{:S(2)}, u32[]{:S(2)}) %collective-permute-start.21) | collective-permute-done | bytes 294944 | tf_op jit(solution)/shard_map/ppermute | solution.py:140
  499.0 3.6 all-to-all-start.2
  502.5 5.9 %collective-permute-done.27 = bf16[1,192,768]{2,1,0:T(8,128)(2,1)} collective-permute-done((bf16[1,192,768]{2,1,0:T(8,128)(2,1)}, bf16[1,192,768]{2,1,0:T(8,128)(2,1)}, u32[]{:S(2)}, u32[]{:S(2)}) %collective-permute-start.27) | collective-permute-done | bytes 294944 | tf_op jit(solution)/shard_map/ppermute | solution.py:140
  508.4 2.7 fusion.38
  513.7 3.4 collective-permute-start.15
  519.1 10.7 %collective-permute-done.15 = bf16[1,208,768]{2,1,0:T(8,128)(2,1)S(1)} collective-permute-done((bf16[1,208,768]{2,1,0:T(8,128)(2,1)S(1)}, bf16[1,208,768]{2,1,0:T(8,128)(2,1)S(1)}, u32[]{:S(2)}, u32[]{:S(2)}) %collective-permute-start.15) | collective-permute-done | bytes 319520 | tf_op jit(solution)/shard_map/ppermute | solution.py:140
  533.2 3.3 convert.83
  537.7 2.8 collective-permute-done.16
  (239 shorter events, 91.5 us)
Async XLA Ops:
  0.7 25.1 %copy-start.24 = (bf16[96,768]{1,0:T(8,128)(2,1)S(1)}, bf16[96,768]{1,0:T(8,128)(2,1)}, u32[]{:S(2)}) copy-start(bf16[96,768]{1,0:T(8,128)(2,1)} %param.26) | copy-start | bytes 442372
  0.7 25.1 %copy-start.9 = (bf16[96,3072]{1,0:T(8,128)(2,1)S(1)}, bf16[96,3072]{1,0:T(8,128)(2,1)}, u32[]{:S(2)}) copy-start(bf16[96,3072]{1,0:T(8,128)(2,1)} %param.30) | copy-start | bytes 1769476
  0.7 28.6 %copy-start.23 = (bf16[384,768]{1,0:T(8,128)(2,1)S(1)}, bf16[384,768]{1,0:T(8,128)(2,1)}, u32[]{:S(2)}) copy-start(bf16[384,768]{1,0:T(8,128)(2,1)} %param.32) | copy-start | bytes 1769476
  8.3 15.9 %collective-permute-start = (bf16[1,112,1152]{2,1,0:T(8,128)(2,1)S(1)}, bf16[1,112,1152]{2,1,0:T(8,128)(2,1)S(1)}, u32[]{:S(2)}, u32[]{:S(2)}) collective-permute-start(bf16[1,112,1152]{2,1,0:T(8,128)(2,1)S(1)} %get-tuple-element.70), channel_id=1, source_target_pairs={{0,4},{1,5},{2,6},{3,7},{4,0},{5,1},{6,2},{7,3},{8,12},{9,13},{10,... | collective-permute-start | bytes 774152 | tf_op jit(solution)/shard_map/ppermute | solution.py:140
  13.7 77.8 %all-to-all-start.1 = ((s32[4,1,256]{2,1,0:T(1,128)}), s32[4,1,256]{2,1,0:T(1,128)S(1)}, u32[]{:S(2)}, u32[]{:S(2)}) async-start(s32[4,1,256]{2,1,0:T(1,128)} %all_to_all.19), calls=%async_computation.1 | async-start | bytes 8192 | tf_op jit(solution)/shard_map/all_to_all | solution.py:196
  25.0 24.1 %collective-permute-start.1 = (bf16[2,112,1152]{2,1,0:T(8,128)(2,1)}, bf16[2,112,1152]{2,1,0:T(8,128)(2,1)}, u32[]{:S(2)}, u32[]{:S(2)}) collective-permute-start(bf16[2,112,1152]{2,1,0:T(8,128)(2,1)} %maximum_select_fusion.18), channel_id=1, source_target_pairs={{0,2},{1,3},{2,0},{3,1},{4,6},{5,7},{6,4},{7,5},{8,10},{9,11},{10,... | collective-permute-start | bytes 1548296 | tf_op jit(solution)/shard_map/ppermute | solution.py:140
  25.9 33.4 %collective-permute-start.4 = (bf16[1,96,1920]{2,1,0:T(8,128)(2,1)S(1)}, bf16[1,96,1920]{2,1,0:T(8,128)(2,1)S(1)}, u32[]{:S(2)}, u32[]{:S(2)}) collective-permute-start(bf16[1,96,1920]{2,1,0:T(8,128)(2,1)S(1)} %fusion.83), channel_id=1, source_target_pairs={{0,4},{1,5},{2,6},{3,7},{4,0},{5,1},{6,2},{7,3},{8,12},{9,13},{10,... | collective-permute-start | bytes 1105928 | tf_op jit(solution)/shard_map/ppermute | solution.py:140
  29.4 29.0 %collective-permute-start.8 = (bf16[1,384,384]{2,1,0:T(8,128)(2,1)S(1)}, bf16[1,384,384]{2,1,0:T(8,128)(2,1)S(1)}, u32[]{:S(2)}, u32[]{:S(2)}) collective-permute-start(bf16[1,384,384]{2,1,0:T(8,128)(2,1)S(1)} %get-tuple-element.68), channel_id=1, source_target_pairs={{0,4},{1,5},{2,6},{3,7},{4,0},{5,1},{6,2},{7,3},{8,12},{9,13},{10,... | collective-permute-start | bytes 884744 | tf_op jit(solution)/shard_map/ppermute | solution.py:140
  50.5 23.2 %collective-permute-start.2 = (bf16[4,112,1152]{2,1,0:T(8,128)(2,1)S(1)}, bf16[4,112,1152]{2,1,0:T(8,128)(2,1)S(1)}, u32[]{:S(2)}, u32[]{:S(2)}) collective-permute-start(bf16[4,112,1152]{2,1,0:T(8,128)(2,1)S(1)} %bitcast.368), channel_id=1, source_target_pairs={{0,1},{1,0},{2,3},{3,2},{4,5},{5,4},{6,7},{7,6},{8,9},{9,8},{10,11... | collective-permute-start | bytes 3096584 | tf_op jit(solution)/shard_map/ppermute | solution.py:140
  59.3 35.8 %collective-permute-start.9 = (bf16[2,384,384]{2,1,0:T(8,128)(2,1)}, bf16[2,384,384]{2,1,0:T(8,128)(2,1)}, u32[]{:S(2)}, u32[]{:S(2)}) collective-permute-start(bf16[2,384,384]{2,1,0:T(8,128)(2,1)} %maximum_select_fusion.16), channel_id=1, source_target_pairs={{0,2},{1,3},{2,0},{3,1},{4,6},{5,7},{6,4},{7,5},{8,10},{9,11},{10,... | collective-permute-start | bytes 1769480 | tf_op jit(solution)/shard_map/ppermute | solution.py:140
  59.5 30.2 %collective-permute-start.5 = (bf16[2,96,1920]{2,1,0:T(8,128)(2,1)S(1)}, bf16[2,96,1920]{2,1,0:T(8,128)(2,1)S(1)}, u32[]{:S(2)}, u32[]{:S(2)}) collective-permute-start(bf16[2,96,1920]{2,1,0:T(8,128)(2,1)S(1)} %maximum_select_fusion.14), channel_id=1, source_target_pairs={{0,2},{1,3},{2,0},{3,1},{4,6},{5,7},{6,4},{7,5},{8,10},{9,11},{10,... | collective-permute-start | bytes 2211848 | tf_op jit(solution)/shard_map/ppermute | solution.py:140
  75.5 81.7 %collective-permute-start.3 = (bf16[8,112,1152]{2,1,0:T(8,128)(2,1)}, bf16[8,112,1152]{2,1,0:T(8,128)(2,1)}, u32[]{:S(2)}, u32[]{:S(2)}) collective-permute-start(bf16[8,112,1152]{2,1,0:T(8,128)(2,1)} %bitcast.10), channel_id=1, source_target_pairs={{0,8},{8,0},{16,24},{24,16},{1,9},{9,1},{17,25},{25,17},{2,10},{10... | collective-permute-start | bytes 6193160 | tf_op jit(solution)/shard_map/ppermute | solution.py:140
  90.0 62.5 %collective-permute-start.6 = (bf16[4,96,1920]{2,1,0:T(8,128)(2,1)S(1)}, bf16[4,96,1920]{2,1,0:T(8,128)(2,1)}, u32[]{:S(2)}, u32[]{:S(2)}) collective-permute-start(bf16[4,96,1920]{2,1,0:T(8,128)(2,1)S(1)} %bitcast.352), channel_id=1, source_target_pairs={{0,1},{1,0},{2,3},{3,2},{4,5},{5,4},{6,7},{7,6},{8,9},{9,8},{10,11... | collective-permute-start | bytes 4423688 | tf_op jit(solution)/shard_map/ppermute | solution.py:140
  91.5 23.6 %all-to-all-start.3 = ((bf16[4,256,768]{2,1,0:T(8,128)(2,1)}), bf16[4,256,768]{2,1,0:T(8,128)(2,1)S(1)}, u32[]{:S(2)}, u32[]{:S(2)}) async-start(bf16[4,256,768]{2,1,0:T(8,128)(2,1)} %bitcast.377), calls=%async_computation.3 | async-start | bytes 3145728 | tf_op jit(solution)/shard_map/all_to_all | solution.py:196
  98.0 49.9 %collective-permute-start.10 = (bf16[4,384,384]{2,1,0:T(8,128)(2,1)}, bf16[4,384,384]{2,1,0:T(8,128)(2,1)}, u32[]{:S(2)}, u32[]{:S(2)}) collective-permute-start(bf16[4,384,384]{2,1,0:T(8,128)(2,1)} %bitcast.28), channel_id=1, source_target_pairs={{0,1},{1,0},{2,3},{3,2},{4,5},{5,4},{6,7},{7,6},{8,9},{9,8},{10,11... | collective-permute-start | bytes 3538952 | tf_op jit(solution)/shard_map/ppermute | solution.py:140
  115.1 49.7 %all-to-all-start = ((bf16[4,256,768]{2,1,0:T(8,128)(2,1)}), bf16[4,256,768]{2,1,0:T(8,128)(2,1)}, u32[]{:S(2)}, u32[]{:S(2)}) async-start(bf16[4,256,768]{2,1,0:T(8,128)(2,1)} %bitcast.378), calls=%async_computation | async-start | bytes 3145728 | tf_op jit(solution)/shard_map/all_to_all | solution.py:196
  152.5 96.0 %collective-permute-start.11 = (bf16[8,384,384]{2,1,0:T(8,128)(2,1)}, bf16[8,384,384]{2,1,0:T(8,128)(2,1)}, u32[]{:S(2)}, u32[]{:S(2)}) collective-permute-start(bf16[8,384,384]{2,1,0:T(8,128)(2,1)} %bitcast.31), channel_id=1, source_target_pairs={{0,8},{8,0},{16,24},{24,16},{1,9},{9,1},{17,25},{25,17},{2,10},{10... | collective-permute-start | bytes 7077896 | tf_op jit(solution)/shard_map/ppermute | solution.py:140
  156.7 45.8 %collective-permute-start.7 = (bf16[8,96,1920]{2,1,0:T(8,128)(2,1)}, bf16[8,96,1920]{2,1,0:T(8,128)(2,1)}, u32[]{:S(2)}, u32[]{:S(2)}) collective-permute-start(bf16[8,96,1920]{2,1,0:T(8,128)(2,1)} %bitcast.20), channel_id=1, source_target_pairs={{0,8},{8,0},{16,24},{24,16},{1,9},{9,1},{17,25},{25,17},{2,10},{10... | collective-permute-start | bytes 8847368 | tf_op jit(solution)/shard_map/ppermute | solution.py:140
  310.7 66.0 %copy-start.14 = (bf16[768,768]{1,0:T(8,128)(2,1)}, bf16[768,768]{1,0:T(8,128)(2,1)S(1)}, u32[]{:S(2)}) copy-start(bf16[768,768]{1,0:T(8,128)(2,1)S(1)} %convolution_convert_fusion.4) | copy-start | bytes 3538948
  365.1 15.4 %copy-start.2 = (bf16[8,1,192,768]{3,2,0,1:T(8,128)(2,1)}, bf16[8,1,192,768]{3,2,0,1:T(8,128)(2,1)S(1)}, u32[]{:S(2)}) copy-start(bf16[8,1,192,768]{3,2,0,1:T(8,128)(2,1)S(1)} %get-tuple-element.37) | copy-start | bytes 7077892
  365.1 29.7 %collective-permute-start.24 = (bf16[8,192,768]{2,1,0:T(8,128)(2,1)}, bf16[8,192,768]{2,1,0:T(8,128)(2,1)}, u32[]{:S(2)}, u32[]{:S(2)}) collective-permute-start(bf16[8,192,768]{2,1,0:T(8,128)(2,1)} %get-tuple-element.38), channel_id=1, source_target_pairs={{0,8},{8,0},{16,24},{24,16},{1,9},{9,1},{17,25},{25,17},{2,10},{10... | collective-permute-start | bytes 7077896 | tf_op jit(solution)/shard_map/ppermute | solution.py:140
  366.9 32.6 %collective-permute-start.18 = (bf16[8,96,1536]{2,1,0:T(8,128)(2,1)}, bf16[8,96,1536]{2,1,0:T(8,128)(2,1)}, u32[]{:S(2)}, u32[]{:S(2)}) collective-permute-start(bf16[8,96,1536]{2,1,0:T(8,128)(2,1)} %get-tuple-element.40), channel_id=1, source_target_pairs={{0,8},{8,0},{16,24},{24,16},{1,9},{9,1},{17,25},{25,17},{2,10},{10... | collective-permute-start | bytes 7077896 | tf_op jit(solution)/shard_map/ppermute | solution.py:140
  367.5 14.2 %copy-start.5 = (bf16[4,1,96,1536]{3,2,1,0:T(8,128)(2,1)}, bf16[4,1,96,1536]{3,2,1,0:T(8,128)(2,1)S(1)}, u32[]{:S(2)}) copy-start(bf16[4,1,96,1536]{3,2,1,0:T(8,128)(2,1)S(1)} %broadcast_select_fusion.8) | copy-start | bytes 3538948
  378.4 27.6 %collective-permute-start.12 = (bf16[8,208,768]{2,1,0:T(8,128)(2,1)}, bf16[8,208,768]{2,1,0:T(8,128)(2,1)}, u32[]{:S(2)}, u32[]{:S(2)}) collective-permute-start(bf16[8,208,768]{2,1,0:T(8,128)(2,1)} %maximum_select_fusion.5), channel_id=1, source_target_pairs={{0,8},{8,0},{16,24},{24,16},{1,9},{9,1},{17,25},{25,17},{2,10},{10... | collective-permute-start | bytes 7667720 | tf_op jit(solution)/shard_map/ppermute | solution.py:140
  390.5 108.5 %all-to-all-start.4 = ((bf16[4,256,768]{2,1,0:T(8,128)(2,1)}), bf16[4,256,768]{2,1,0:T(8,128)(2,1)}, u32[]{:S(2)}, u32[]{:S(2)}) async-start(bf16[4,256,768]{2,1,0:T(8,128)(2,1)} %bitcast.379), calls=%async_computation.4 | async-start | bytes 3145728 | tf_op jit(solution)/shard_map/all_to_all | solution.py:232
  397.9 55.3 %collective-permute-start.25 = (bf16[4,192,768]{2,1,0:T(8,128)(2,1)S(1)}, bf16[4,192,768]{2,1,0:T(8,128)(2,1)S(1)}, u32[]{:S(2)}, u32[]{:S(2)}) collective-permute-start(bf16[4,192,768]{2,1,0:T(8,128)(2,1)S(1)} %fusion.28), channel_id=1, source_target_pairs={{0,1},{1,0},{2,3},{3,2},{4,5},{5,4},{6,7},{7,6},{8,9},{9,8},{10,11... | collective-permute-start | bytes 3538952 | tf_op jit(solution)/shard_map/ppermute | solution.py:140
  401.7 50.4 %collective-permute-start.19 = (bf16[4,96,1536]{2,1,0:T(8,128)(2,1)S(1)}, bf16[4,96,1536]{2,1,0:T(8,128)(2,1)S(1)}, u32[]{:S(2)}, u32[]{:S(2)}) collective-permute-start(bf16[4,96,1536]{2,1,0:T(8,128)(2,1)S(1)} %fusion.27), channel_id=1, source_target_pairs={{0,1},{1,0},{2,3},{3,2},{4,5},{5,4},{6,7},{7,6},{8,9},{9,8},{10,11... | collective-permute-start | bytes 3538952 | tf_op jit(solution)/shard_map/ppermute | solution.py:140
  406.0 77.8 %copy-start.12 = (bf16[1,2,192,768]{3,2,1,0:T(8,128)(2,1)}, bf16[1,2,192,768]{3,2,1,0:T(8,128)(2,1)S(1)}, u32[]{:S(2)}) copy-start(bf16[1,2,192,768]{3,2,1,0:T(8,128)(2,1)S(1)} %select_bitcast_fusion.4) | copy-start | bytes 1769476
  408.5 43.6 %copy-start.6 = (bf16[4,1,96,1536]{3,2,1,0:T(8,128)(2,1)S(1)}, bf16[4,1,96,1536]{3,2,1,0:T(8,128)(2,1)}, u32[]{:S(2)}) copy-start(bf16[4,1,96,1536]{3,2,1,0:T(8,128)(2,1)} %copy-done.5) | copy-start | bytes 3538948
  408.6 70.5 %collective-permute-start.13 = (bf16[4,208,768]{2,1,0:T(8,128)(2,1)S(1)}, bf16[4,208,768]{2,1,0:T(8,128)(2,1)S(1)}, u32[]{:S(2)}, u32[]{:S(2)}) collective-permute-start(bf16[4,208,768]{2,1,0:T(8,128)(2,1)S(1)} %fusion.25), channel_id=1, source_target_pairs={{0,1},{1,0},{2,3},{3,2},{4,5},{5,4},{6,7},{7,6},{8,9},{9,8},{10,11... | collective-permute-start | bytes 3833864 | tf_op jit(solution)/shard_map/ppermute | solution.py:140
  412.0 41.3 %copy-start.8 = (bf16[4,1,192,768]{3,2,1,0:T(8,128)(2,1)S(1)}, bf16[4,1,192,768]{3,2,1,0:T(8,128)(2,1)}, u32[]{:S(2)}) copy-start(bf16[4,1,192,768]{3,2,1,0:T(8,128)(2,1)} %copy-done.7) | copy-start | bytes 3538948
  452.6 27.8 %collective-permute-start.20 = (bf16[2,96,1536]{2,1,0:T(8,128)(2,1)S(1)}, bf16[2,96,1536]{2,1,0:T(8,128)(2,1)S(1)}, u32[]{:S(2)}, u32[]{:S(2)}) collective-permute-start(bf16[2,96,1536]{2,1,0:T(8,128)(2,1)S(1)} %fusion.34), channel_id=1, source_target_pairs={{0,2},{1,3},{2,0},{3,1},{4,6},{5,7},{6,4},{7,5},{8,10},{9,11},{10,... | collective-permute-start | bytes 1769480 | tf_op jit(solution)/shard_map/ppermute | solution.py:140
  453.3 25.8 %copy-start.4 = (bf16[4,1,208,768]{3,2,1,0:T(8,128)(2,1)S(1)}, bf16[4,1,208,768]{3,2,1,0:T(8,128)(2,1)}, u32[]{:S(2)}) copy-start(bf16[4,1,208,768]{3,2,1,0:T(8,128)(2,1)} %copy-done.3) | copy-start | bytes 3833860
  453.8 26.6 %copy-start.11 = (bf16[1,2,96,1536]{3,2,1,0:T(8,128)(2,1)S(1)}, bf16[1,2,96,1536]{3,2,1,0:T(8,128)(2,1)}, u32[]{:S(2)}) copy-start(bf16[1,2,96,1536]{3,2,1,0:T(8,128)(2,1)} %fusion.37) | copy-start | bytes 1769476
  453.8 30.0 %collective-permute-start.26 = (bf16[2,192,768]{2,1,0:T(8,128)(2,1)S(1)}, bf16[2,192,768]{2,1,0:T(8,128)(2,1)S(1)}, u32[]{:S(2)}, u32[]{:S(2)}) collective-permute-start(bf16[2,192,768]{2,1,0:T(8,128)(2,1)S(1)} %fusion.35), channel_id=1, source_target_pairs={{0,2},{1,3},{2,0},{3,1},{4,6},{5,7},{6,4},{7,5},{8,10},{9,11},{10,... | collective-permute-start | bytes 1769480 | tf_op jit(solution)/shard_map/ppermute | solution.py:140
  455.4 28.4 %copy-start.13 = (bf16[1,2,192,768]{3,2,1,0:T(8,128)(2,1)}, bf16[1,2,192,768]{3,2,1,0:T(8,128)(2,1)S(1)}, u32[]{:S(2)}) copy-start(bf16[1,2,192,768]{3,2,1,0:T(8,128)(2,1)S(1)} %select_bitcast_fusion.3) | copy-start | bytes 1769476
  480.6 16.0 %collective-permute-start.21 = (bf16[1,96,1536]{2,1,0:T(8,128)(2,1)S(1)}, bf16[1,96,1536]{2,1,0:T(8,128)(2,1)S(1)}, u32[]{:S(2)}, u32[]{:S(2)}) collective-permute-start(bf16[1,96,1536]{2,1,0:T(8,128)(2,1)S(1)} %fusion.42), channel_id=1, source_target_pairs={{0,4},{1,5},{2,6},{3,7},{4,0},{5,1},{6,2},{7,3},{8,12},{9,13},{10,... | collective-permute-start | bytes 884744 | tf_op jit(solution)/shard_map/ppermute | solution.py:140
  482.2 30.1 %collective-permute-start.14 = (bf16[2,208,768]{2,1,0:T(8,128)(2,1)}, bf16[2,208,768]{2,1,0:T(8,128)(2,1)}, u32[]{:S(2)}, u32[]{:S(2)}) collective-permute-start(bf16[2,208,768]{2,1,0:T(8,128)(2,1)} %fusion.31), channel_id=1, source_target_pairs={{0,2},{1,3},{2,0},{3,1},{4,6},{5,7},{6,4},{7,5},{8,10},{9,11},{10,... | collective-permute-start | bytes 1916936 | tf_op jit(solution)/shard_map/ppermute | solution.py:140
  483.8 13.9 %copy-start.18 = (bf16[2,192,768]{2,1,0:T(8,128)(2,1)}, bf16[2,192,768]{2,1,0:T(8,128)(2,1)S(1)}, u32[]{:S(2)}) copy-start(bf16[2,192,768]{2,1,0:T(8,128)(2,1)S(1)} %collective-permute-done.26) | copy-start | bytes 1769476
  484.8 23.5 %collective-permute-start.27 = (bf16[1,192,768]{2,1,0:T(8,128)(2,1)}, bf16[1,192,768]{2,1,0:T(8,128)(2,1)}, u32[]{:S(2)}, u32[]{:S(2)}) collective-permute-start(bf16[1,192,768]{2,1,0:T(8,128)(2,1)} %fusion.43), channel_id=1, source_target_pairs={{0,4},{1,5},{2,6},{3,7},{4,0},{5,1},{6,2},{7,3},{8,12},{9,13},{10,... | collective-permute-start | bytes 884744 | tf_op jit(solution)/shard_map/ppermute | solution.py:140
  497.7 19.5 %collective-permute-start.22 = (bf16[96,1536]{1,0:T(8,128)(2,1)}, bf16[96,1536]{1,0:T(8,128)(2,1)}, u32[]{:S(2)}, u32[]{:S(2)}) collective-permute-start(bf16[96,1536]{1,0:T(8,128)(2,1)} %fusion.39), channel_id=1, source_target_pairs={{0,16},{8,24},{16,0},{24,8},{1,17},{9,25},{17,1},{25,9},{2,18},{10... | collective-permute-start | bytes 884744 | tf_op jit(solution)/shard_map/ppermute | solution.py:140
  499.0 37.6 %all-to-all-start.2 = ((bf16[4,256,768]{2,1,0:T(8,128)(2,1)}), bf16[4,256,768]{2,1,0:T(8,128)(2,1)S(1)}, u32[]{:S(2)}, u32[]{:S(2)}) async-start(bf16[4,256,768]{2,1,0:T(8,128)(2,1)} %bitcast.33), calls=%async_computation.2 | async-start | bytes 3145728 | tf_op jit(solution)/shard_map/all_to_all | solution.py:232
  511.1 25.4 %collective-permute-start.28 = (bf16[192,768]{1,0:T(8,128)(2,1)}, bf16[192,768]{1,0:T(8,128)(2,1)}, u32[]{:S(2)}, u32[]{:S(2)}) collective-permute-start(bf16[192,768]{1,0:T(8,128)(2,1)} %fusion.38), channel_id=1, source_target_pairs={{0,16},{8,24},{16,0},{24,8},{1,17},{9,25},{17,1},{25,9},{2,18},{10... | collective-permute-start | bytes 884744 | tf_op jit(solution)/shard_map/ppermute | solution.py:140
  513.7 16.1 %collective-permute-start.15 = (bf16[1,208,768]{2,1,0:T(8,128)(2,1)S(1)}, bf16[1,208,768]{2,1,0:T(8,128)(2,1)S(1)}, u32[]{:S(2)}, u32[]{:S(2)}) collective-permute-start(bf16[1,208,768]{2,1,0:T(8,128)(2,1)S(1)} %fusion.41), channel_id=1, source_target_pairs={{0,4},{1,5},{2,6},{3,7},{4,0},{5,1},{6,2},{7,3},{8,12},{9,13},{10,... | collective-permute-start | bytes 958472 | tf_op jit(solution)/shard_map/ppermute | solution.py:140
  519.1 22.5 %collective-permute-start.23 = (f32[96,1536]{1,0:T(8,128)}, f32[96,1536]{1,0:T(8,128)}, u32[]{:S(2)}, u32[]{:S(2)}) collective-permute-start(f32[96,1536]{1,0:T(8,128)} %convert_add_fusion.11), channel_id=1, source_target_pairs={{0,8},{8,0},{16,24},{24,16},{1,9},{9,1},{17,25},{25,17},{2,10},{10... | collective-permute-start | bytes 1769480 | tf_op jit(solution)/shard_map/ppermute | solution.py:140
  532.0 8.5 %collective-permute-start.16 = (bf16[208,768]{1,0:T(8,128)(2,1)}, bf16[208,768]{1,0:T(8,128)(2,1)S(1)}, u32[]{:S(2)}, u32[]{:S(2)}) collective-permute-start(bf16[208,768]{1,0:T(8,128)(2,1)} %fusion.33), channel_id=1, source_target_pairs={{0,16},{8,24},{16,0},{24,8},{1,17},{9,25},{17,1},{25,9},{2,18},{10... | collective-permute-start | bytes 958472 | tf_op jit(solution)/shard_map/ppermute | solution.py:140
  537.6 5.4 collective-permute-start.29
  541.5 4.8 collective-permute-start.17
  (23 other events, 90.4 us)

commit v2 on v1

v2 whole, which is shorter than its diff:
```python
import math

import jax
import jax.numpy as jnp
from jax import lax
from jax.experimental import pallas as pl
from jax.experimental.pallas import tpu as pltpu
from jax.sharding import PartitionSpec as P

F32=jnp.float32; BF=jnp.bfloat16
PAIR=128; HD=64; BIG=1e30

def dot_nn(a,b): return lax.dot_general(a,b,(((1,),(0,)),((),())),preferred_element_type=F32)
def dot_nt(a,b): return lax.dot_general(a,b,(((1,),(1,)),((),())),preferred_element_type=F32)
def dot_tn(a,b): return lax.dot_general(a,b,(((0,),(0,)),((),())),preferred_element_type=F32)

def split3(v):
    hi=v.astype(BF); r=v-hi.astype(F32); mid=r.astype(BF); lo=(r-mid.astype(F32)).astype(BF)
    return hi,mid,lo

def fwd_kernel(doc_ref,q_ref,k_ref,v_ref,o_ref,lse_ref,qa,ka,va):
    rows=q_ref.shape[0]
    lane=lax.broadcasted_iota(jnp.int32,(rows,PAIR),1)
    doc=doc_ref[...]
    for h in range(2):
        base=(1-h)*HD
        mine=(lane>=h*HD)&(lane<(h+1)*HD)
        same=(lane-base)==doc
        qa[...]=jnp.where(mine,q_ref[...]*jnp.asarray(0.125,BF),jnp.where(same,1.0,0.0).astype(BF))
        ka[...]=jnp.where(mine,k_ref[...],jnp.where(same|(lane<base)|(lane>=base+8),0.0,-BIG).astype(BF))
        va[...]=jnp.where(mine,v_ref[...],jnp.ones((),BF))
        bq=256
        for i in range(rows//bq):
            sl=slice(i*bq,(i+1)*bq)
            sc=dot_nt(qa[sl,:],ka[...])
            m=jnp.max(sc,axis=1,keepdims=True)
            p=jnp.exp(sc-m).astype(BF)
            o=dot_nn(p,va[...])
            l=o[:,base:base+1]
            lse_ref[sl,h:h+1]=m+jnp.log(l)
            out=(o/l).astype(BF)
            if h==0: o_ref[sl,:]=out
            else: o_ref[sl,:]=jnp.where(lane[sl,:]>=HD,out,o_ref[sl,:])

def attend(doc,qkv,first,n):
    rows=qkv.shape[0]; pairs=qkv.shape[1]//3//PAIR
    return pl.pallas_call(fwd_kernel,grid=(n,),
        in_specs=[pl.BlockSpec((rows,1),lambda h:(0,0))]+[pl.BlockSpec((rows,PAIR),lambda h,j=j:(0,h+first+j*pairs)) for j in range(3)],
        out_specs=[pl.BlockSpec((rows,PAIR),lambda h:(0,h)),pl.BlockSpec((None,rows,2),lambda h:(h,0,0))],
        out_shape=[jax.ShapeDtypeStruct((rows,n*PAIR),BF),jax.ShapeDtypeStruct((n,rows,2),F32)],
        scratch_shapes=[pltpu.VMEM((rows,PAIR),BF)]*3,
        compiler_params=pltpu.CompilerParams(vmem_limit_bytes=60<<20),
        cost_estimate=pl.CostEstimate(flops=16*rows*rows*PAIR*n,bytes_accessed=rows*PAIR*n*8,transcendentals=rows*rows*n*2),
        name="attend")(doc,qkv,qkv,qkv)

def bwd_kernel(doc_ref,q_ref,k_ref,v_ref,o_ref,do_ref,lse_ref,dq_ref,dk_ref,dv_ref,dqsum_ref,dvsum_ref,qa,ka,va,da,dqs):
    rows=q_ref.shape[0]
    lane=lax.broadcasted_iota(jnp.int32,(rows,PAIR),1)
    doc=doc_ref[...]
    dof=do_ref[...].astype(F32)*o_ref[...].astype(F32)
    for h in range(2):
        base=(1-h)*HD
        mine=(lane>=h*HD)&(lane<(h+1)*HD)
        rel=lane-base
        same=rel==doc
        delta=jnp.sum(jnp.where(mine,dof,0.0),axis=1,keepdims=True)
        lh,lm,ll=split3(-lse_ref[:,h:h+1]); dh,dm,dl=split3(-delta)
        one=jnp.ones((),BF); zero=jnp.zeros((),BF)
        aug_q=jnp.where(same,one,zero)
        aug_q=jnp.where(rel==8,lh,jnp.where(rel==9,lm,jnp.where(rel==10,ll,aug_q)))
        aug_k=jnp.where((rel>=0)&(rel<8)&(~same),jnp.asarray(-BIG,BF),zero)
        aug_k=jnp.where((rel>=8)&(rel<11),one,aug_k)
        aug_d=jnp.where(rel==8,dh,jnp.where(rel==9,dm,jnp.where(rel==10,dl,zero)))
        aug_v=jnp.where((rel>=8)&(rel<11),one,zero)
        qa[...]=jnp.where(mine,q_ref[...]*jnp.asarray(0.125,BF),aug_q)
        ka[...]=jnp.where(mine,k_ref[...],aug_k)
        va[...]=jnp.where(mine,v_ref[...],aug_v)
        da[...]=jnp.where(mine,do_ref[...],aug_d)
        bk=256
        for i in range(rows//bk):
            sl=slice(i*bk,(i+1)*bk)
            st=dot_nt(ka[sl,:],qa[...])
            pt=jnp.exp(st)
            dpt=dot_nt(va[sl,:],da[...])
            dst=(pt*dpt).astype(BF)
            dv=dot_nn(pt.astype(BF),da[...])
            dk=dot_nn(dst,qa[...])
            dq=dot_tn(dst,ka[sl,:])
            if i==0: dqs[...]=dq
            else: dqs[...]+=dq
            msl=mine[sl,:]
            if h==0:
                dv_ref[sl,:]=dv.astype(BF); dk_ref[sl,:]=dk.astype(BF)
            else:
                dv_ref[sl,:]=jnp.where(msl,dv.astype(BF),dv_ref[sl,:]); dk_ref[sl,:]=jnp.where(msl,dk.astype(BF),dk_ref[sl,:])
        dqv=(dqs[...]*0.125).astype(BF)
        if h==0: dq_ref[...]=dqv
        else: dq_ref[...]=jnp.where(mine,dqv,dq_ref[...])
    dqsum_ref[...]=jnp.sum(dq_ref[...].astype(F32),axis=0,keepdims=True)
    dvsum_ref[...]=jnp.sum(dv_ref[...].astype(F32),axis=0,keepdims=True)

def attend_back(doc,qkv,att,datt,lse,first,n):
    rows=qkv.shape[0]; pairs=qkv.shape[1]//3//PAIR
    col=lambda h:(0,h+first)
    return pl.pallas_call(bwd_kernel,grid=(n,),
        in_specs=[pl.BlockSpec((rows,1),lambda h:(0,0))]+[pl.BlockSpec((rows,PAIR),lambda h,j=j:(0,h+first+j*pairs)) for j in range(3)]
          +[pl.BlockSpec((rows,PAIR),lambda h:(0,h)),pl.BlockSpec((rows,PAIR),col),pl.BlockSpec((None,rows,2),lambda h:(h,0,0))],
        out_specs=[pl.BlockSpec((rows,PAIR),lambda h:(0,h))]*3+[pl.BlockSpec((1,PAIR),lambda h:(0,h))]*2,
        out_shape=[jax.ShapeDtypeStruct((rows,n*PAIR),BF)]*3+[jax.ShapeDtypeStruct((1,n*PAIR),F32)]*2,
        scratch_shapes=[pltpu.VMEM((rows,PAIR),BF)]*4+[pltpu.VMEM((rows,PAIR),F32)],
        compiler_params=pltpu.CompilerParams(vmem_limit_bytes=60<<20),
        cost_estimate=pl.CostEstimate(flops=24*rows*rows*PAIR*n,bytes_accessed=rows*PAIR*n*16,transcendentals=rows*rows*n*2),
        name="attend_back")(doc,qkv,qkv,qkv,att,datt,lse)

norm_eps = 1e-12
MAT = pl.BlockSpec(memory_space=pl.ANY)
SCALAR = pl.BlockSpec(memory_space=pltpu.SMEM)
LIMIT = 60 << 20


def swap(value, axis, mask):
    size = lax.axis_size(axis)
    return lax.ppermute(value, axis, [(i, i ^ mask) for i in range(size)])


def after(value, *deps):
    return lax.optimization_barrier((value,) + deps)[0]


def pick(flag, low, high):
    return jnp.where(flag == 0, low, high)


def bits_of(count):
    return [1 << i for i in reversed(range(count.bit_length() - 1))]


def order_of(owners):
    masks = [0]
    for bit in bits_of(owners):
        masks = masks + [m ^ bit for m in masks]
    return masks


def absolute(held, owners):
    index = lax.axis_index("fsdp")
    for bit in bits_of(owners):
        other = swap(held, "fsdp", bit)
        flag = (index // bit) & 1
        held = pick(flag, jnp.stack([held, other], axis=1), jnp.stack([other, held], axis=1))
        held = held.reshape((-1,) + held.shape[2:])
    return held


def load(copies, sems):
    started = [pltpu.make_async_copy(src, dst, sems.at[i]) for i, (src, dst) in enumerate(copies)]
    for copy in started:
        copy.start()
    return started


def piece_copies(plan, refs, at_ref, place):
    owner, part = at_ref[0], at_ref[1]
    copies = []
    for (masks, seq_mask), ref in zip(plan, refs):
        if masks is None:
            copies += place(ref, None, part ^ seq_mask)
        else:
            for i, mask in enumerate(masks):
                copies += place(ref.at[i], owner ^ mask, part ^ seq_mask)
    return copies


def project_kernel(plan, shard, at_ref, x_ref, bias_ref, *rest):
    pieces, (out_ref, mat, sems) = rest[:-3], rest[-3:]
    half = mat.shape[1] // 2

    @pl.when(pl.program_id(0) == 0)
    def _():
        for copy in load(qkv_copies(plan, pieces, at_ref, mat, shard), sems):
            copy.wait()

    out_ref[...] = (dot_nn(x_ref[...], mat[...]) + bias_ref[...]).astype(BF)


def columns(part, size):
    return pl.ds(pl.multiple_of(part * size, 128), size)


def lines(owner, size):
    return pl.ds(pl.multiple_of(owner * size, 16), size)


def qkv_copies(plan, refs, at_ref, mat, shard):
    half = mat.shape[1] // 2

    def place(src, owner, part):
        if owner is None:
            return [(src, mat.at[:, columns(part & 1, half)])]
        return [(src, mat.at[lines(owner, shard), columns(part & 1, half)])]

    return piece_copies(plan, refs, at_ref, place)


def project(at, x_rows, bias, plan, pieces, shard):
    rows, width = x_rows.shape
    blocks = 4
    count = sum(1 if masks is None else len(masks) for masks, _ in plan)
    return pl.pallas_call(
        lambda *refs: project_kernel(plan, shard, *refs),
        grid=(blocks,),
        in_specs=[SCALAR, pl.BlockSpec((rows // blocks, width), lambda i: (i, 0)), pl.BlockSpec((1, 3 * width), lambda i: (0, 0))]
        + [MAT] * len(pieces),
        out_specs=pl.BlockSpec((rows // blocks, 3 * width), lambda i: (i, 0)),
        out_shape=jax.ShapeDtypeStruct((rows, 3 * width), BF),
        scratch_shapes=[pltpu.VMEM((width, 3 * width), BF), pltpu.SemaphoreType.DMA((count,))],
        compiler_params=pltpu.CompilerParams(vmem_limit_bytes=LIMIT),
        cost_estimate=pl.CostEstimate(flops=6 * rows * width * width, bytes_accessed=14 * rows * width, transcendentals=0),
        name="project",
    )(at, x_rows, bias, *pieces)


def mean_of(value):
    return jnp.mean(value, axis=-1, keepdims=True)


def ffn_kernel(plans, shard, at_ref, x_ref, gout_ref, vec_ref, bias_ref, *rest):
    count_att = plans[2]
    atts, rest = rest[:count_att], rest[count_att:]
    inner_pieces, rest = rest[: len(plans[0])], rest[len(plans[0]) :]
    outer_pieces, rest = rest[: len(plans[1])], rest[len(plans[1]) :]
    (
        res_ref, act_ref, din_ref, low_ref, db2_ref, db_ref, dfirst_ref, datt_ref, sums_ref, dsum_ref,
        w1, wo, w2, slope, sem_a, sem_b,
    ) = rest
    width, hidden = w1.shape
    step = pl.program_id(0)

    @pl.when(step == 0)
    def _():
        def place(src, owner, part):
            if owner is None:
                rows = slice(None)
            else:
                rows = lines(owner, shard)
            part = part & 1
            return [
                (src.at[:, : hidden // 2], w1.at[rows, columns(part, hidden // 2)]),
                (src.at[:, hidden // 2 :], wo.at[rows, columns(part, width // 2)]),
            ]

        def place_outer(src, owner, part):
            if owner is None:
                return [(src, w2)]
            size = src.shape[0]
            return [(src, w2.at[lines(owner * 4 + part, size)])]

        first = load(piece_copies(plans[0], inner_pieces, at_ref, place), sem_a)
        later = load(piece_copies(plans[1], outer_pieces, at_ref, place_outer), sem_b)
        for copy in first + later:
            copy.wait()
        sums_ref[...] = jnp.zeros_like(sums_ref)
        dsum_ref[...] = jnp.zeros_like(dsum_ref)

    output_vec, gain_first, shift_first, outer_vec, gain_final, shift_final = (
        vec_ref[i : i + 1, :] for i in range(6)
    )
    wide = atts[0].shape[1]
    first = x_ref[...].astype(F32) + output_vec
    for i, att in enumerate(atts):
        first = first + dot_nn(att[...], wo[i * wide : (i + 1) * wide, :])
    center = first - mean_of(first)
    rstd1 = lax.rsqrt(mean_of(center * center) + norm_eps)
    hat1 = center * rstd1
    normed = hat1 * gain_first + shift_first
    low = normed.astype(BF)
    low_ref[...] = low
    chunk = 768
    second = normed + outer_vec
    for start in range(0, hidden, chunk):
        sl = slice(start, start + chunk)
        inner = dot_nn(low, w1[:, sl]) + bias_ref[:, sl]
        cdf = 0.5 * (1.0 + lax.erf(inner * (1.0 / math.sqrt(2.0))))
        act = (inner * cdf).astype(BF)
        slope[:, sl] = cdf + inner * (jnp.exp(-0.5 * inner * inner) * (1.0 / math.sqrt(2.0 * math.pi)))
        act_ref[:, sl] = act
        second = second + dot_nn(act, w2[sl, :])
    center = second - mean_of(second)
    rstd2 = lax.rsqrt(mean_of(center * center) + norm_eps)
    hat2 = center * rstd2
    res_ref[...] = (hat2 * gain_final + shift_final).astype(BF)
    gout = gout_ref[...].astype(F32)
    scaled = gout * gain_final
    dsecond = rstd2 * (scaled - mean_of(scaled) - hat2 * mean_of(scaled * hat2))
    db2 = dsecond.astype(BF)
    db2_ref[...] = db2
    dnormed = dsecond
    for start in range(0, hidden, chunk):
        sl = slice(start, start + chunk)
        dinner = (dot_nt(db2, w2[sl, :]) * slope[:, sl]).astype(BF)
        din_ref[:, sl] = dinner
        dsum_ref[:, sl] += jnp.sum(dinner.astype(F32), axis=0, keepdims=True)
        dnormed = dnormed + dot_nt(dinner, w1[:, sl])
    scaled = dnormed * gain_first
    dfirst = rstd1 * (scaled - mean_of(scaled) - hat1 * mean_of(scaled * hat1))
    dfirst_ref[...] = dfirst
    db = dfirst.astype(BF)
    db_ref[...] = db
    datt_ref[...] = dot_nt(db, wo[...]).astype(BF)

    def total(value):
        return jnp.sum(value, axis=0, keepdims=True)

    parts = (db.astype(F32), dnormed * hat1, dnormed, db2.astype(F32), gout * hat2, gout)
    for i, value in enumerate(parts):
        sums_ref[i : i + 1, :] += total(value)


def ffn(at, x_rows, gout, vecs, bias, atts, inner_plan, inner_pieces, outer_plan, outer_pieces, shard):
    rows, width = x_rows.shape
    hidden = bias.shape[1]
    blocks = 4
    tall = rows // blocks

    def row(cols):
        return pl.BlockSpec((tall, cols), lambda i: (i, 0))

    def whole(shape):
        return pl.BlockSpec(shape, lambda i: (0, 0))

    def count(plan, times):
        return times * sum(1 if masks is None else len(masks) for masks, _ in plan)

    shape = jax.ShapeDtypeStruct
    return pl.pallas_call(
        lambda *refs: ffn_kernel((inner_plan, outer_plan, len(atts)), shard, *refs),
        grid=(blocks,),
        in_specs=[SCALAR, row(width), row(width), whole(vecs.shape), whole(bias.shape)]
        + [row(att.shape[1]) for att in atts]
        + [MAT] * (len(inner_pieces) + len(outer_pieces)),
        out_specs=[
            row(width), row(hidden), row(hidden), row(width), row(width), row(width), row(width), row(width),
            whole((8, width)), whole((1, hidden)),
        ],
        out_shape=[
            shape((rows, width), BF), shape((rows, hidden), BF), shape((rows, hidden), BF), shape((rows, width), BF),
            shape((rows, width), BF), shape((rows, width), BF), shape((rows, width), F32), shape((rows, width), BF),
            shape((8, width), F32), shape((1, hidden), F32),
        ],
        scratch_shapes=[
            pltpu.VMEM((width, hidden), BF), pltpu.VMEM((width, width), BF), pltpu.VMEM((hidden, width), BF),
            pltpu.VMEM((tall, hidden), F32), pltpu.SemaphoreType.DMA((count(inner_plan, 2),)),
            pltpu.SemaphoreType.DMA((count(outer_plan, 1),)),
        ],
        compiler_params=pltpu.CompilerParams(vmem_limit_bytes=LIMIT),
        cost_estimate=pl.CostEstimate(
            flops=4 * rows * width * (2 * hidden + width), bytes_accessed=rows * (4 * hidden + 20 * width), transcendentals=2 * rows * hidden
        ),
        name="ffn",
    )(at, x_rows, gout, vecs, bias, *atts, *inner_pieces, *outer_pieces)


def grad_kernel(masks, extra_ref, at_ref, *refs):
    left_ref, rights, (keep_ref, send_ref, done) = refs[0], refs[1:-3], refs[-3:]
    step = pl.program_id(0)
    for number, right in enumerate(rights):
        @pl.when(step == number)
        def _(right=right):
            done[...] = dot_tn(left_ref[...], right[...]).astype(BF)

    size = done.shape[0] // len(masks)
    half = size // 2
    owner, core = at_ref[0], at_ref[1] & 1
    for i, mask in enumerate(masks):
        base = (owner ^ mask) * size
        keep_ref[i, :half] = done[pl.ds(pl.multiple_of(base + core * half, 16), half), :]
        send_ref[i, :half] = done[pl.ds(pl.multiple_of(base + (1 - core) * half, 16), half), :]
        if extra_ref is not None:
            more = jnp.where(step == 0, extra_ref[owner ^ mask], jnp.zeros((), BF))
            keep_ref[i, half:] = more
            send_ref[i, half:] = more


def grad_wide(at, masks, left, rights, extra=None):
    rows, width = left.shape
    steps = len(rights)
    chunk = rights[0].shape[1]
    lines_out = width // len(masks) // 2 + (0 if extra is None else extra.shape[1])
    whole = [pl.BlockSpec((rows, width), lambda i: (0, 0))] + [pl.BlockSpec((rows, chunk), lambda i: (0, 0))] * steps
    extras = [] if extra is None else [extra]
    extra_specs = [pl.BlockSpec(value.shape, lambda i: (0, 0, 0)) for value in extras]
    out = jax.ShapeDtypeStruct((len(masks), lines_out, steps * chunk), BF)
    spec = pl.BlockSpec((len(masks), lines_out, chunk), lambda i: (0, 0, i))

    def kernel(at_ref, *refs):
        if extra is None:
            grad_kernel(masks, None, at_ref, *refs)
        else:
            grad_kernel(masks, refs[0], at_ref, *refs[1:])

    return pl.pallas_call(
        kernel,
        grid=(steps,),
        in_specs=[SCALAR] + extra_specs + whole,
        out_specs=[spec, spec],
        out_shape=[out, out],
        scratch_shapes=[pltpu.VMEM((width, chunk), BF)],
        compiler_params=pltpu.CompilerParams(vmem_limit_bytes=LIMIT),
        cost_estimate=pl.CostEstimate(flops=2 * rows * width * steps * chunk, bytes_accessed=2 * steps * chunk * (rows + width), transcendentals=0),
        name="grad_wide",
    )(at, *extras, left, *rights)


def grad_inner_kernel(masks, at_ref, low_ref, din_ref, att_refs, db_ref, outs, done):
    step = pl.program_id(0)
    last = pl.num_programs(0) - 1
    size = done.shape[0] // len(masks)
    half = size // 2
    wide = done.shape[1] // 2

    @pl.when(step < last)
    def _():
        done[...] = dot_tn(low_ref[...], din_ref[...]).astype(BF)

    @pl.when(step == last)
    def _():
        cols = att_refs[0].shape[1]
        for i, att in enumerate(att_refs):
            done[i * cols : (i + 1) * cols, :] = dot_tn(att[...], db_ref[...]).astype(BF)

    owner, core, side = at_ref[0], at_ref[1] & 1, at_ref[1] >> 1
    for i, mask in enumerate(masks):
        base = (owner ^ mask) * size
        for j, (other_core, other_side) in enumerate(((0, 0), (0, 1), (1, 0), (1, 1))):
            line = pl.multiple_of(base + (core ^ other_core) * half, 16)
            column = pl.multiple_of((side ^ other_side) * wide, 128)
            outs[j][i] = done[pl.ds(line, half), pl.ds(column, wide)]


def grad_inner(at, masks, low, dinner, atts, db):
    rows, width = low.shape
    hidden = dinner.shape[1]
    chunk = width
    steps = hidden // chunk + 1
    size = width // len(masks)
    whole = pl.BlockSpec((rows, width), lambda i: (0, 0))
    out = jax.ShapeDtypeStruct((len(masks), size // 2, steps * chunk // 2), BF)
    spec = pl.BlockSpec((len(masks), size // 2, chunk // 2), lambda i: (0, 0, i))
    n = len(atts)
    return pl.pallas_call(
        lambda at_ref, low_ref, din_ref, *refs: grad_inner_kernel(
            masks, at_ref, low_ref, din_ref, refs[:n], refs[n], refs[n + 1 : n + 5], refs[n + 5]
        ),
        grid=(steps,),
        in_specs=[SCALAR, whole, pl.BlockSpec((rows, chunk), lambda i: (0, jnp.minimum(i, steps - 2)))]
        + [pl.BlockSpec((rows, att.shape[1]), lambda i: (0, 0)) for att in atts]
        + [whole],
        out_specs=[spec] * 4,
        out_shape=[out] * 4,
        scratch_shapes=[pltpu.VMEM((width, chunk), BF)],
        compiler_params=pltpu.CompilerParams(vmem_limit_bytes=LIMIT),
        cost_estimate=pl.CostEstimate(flops=2 * rows * width * (hidden + width), bytes_accessed=4 * rows * hidden, transcendentals=0),
        name="grad_inner",
    )(at, low, dinner, *atts, db)


def grad_outer_kernel(half, at_ref, act_ref, db2_ref, keep_ref, send_ref, done):
    core = at_ref[1] & 1
    done[...] = dot_tn(act_ref[...], db2_ref[...]).astype(BF)
    keep_ref[0] = done[pl.ds(pl.multiple_of(core * half, 16), half), :]
    send_ref[0] = done[pl.ds(pl.multiple_of((1 - core) * half, 16), half), :]


def grad_outer(at, owners, act, db2):
    rows, hidden = act.shape
    width = db2.shape[1]
    size = hidden // owners
    levels = owners.bit_length() - 1

    def column(i, at_ref):
        mask = 0
        for level in range(levels):
            mask = mask | (((i >> level) & 1) << (levels - 1 - level))
        return (0, at_ref[0] ^ mask)

    out = jax.ShapeDtypeStruct((owners, size // 2, width), BF)
    spec = pl.BlockSpec((1, size // 2, width), lambda i, at_ref: (i, 0, 0))
    return pl.pallas_call(
        lambda *refs: grad_outer_kernel(size // 2, *refs),
        grid_spec=pltpu.PrefetchScalarGridSpec(
            num_scalar_prefetch=1,
            grid=(owners,),
            in_specs=[pl.BlockSpec((rows, size), column), pl.BlockSpec((rows, width), lambda i, at_ref: (0, 0))],
            out_specs=[spec, spec],
            scratch_shapes=[pltpu.VMEM((size, width), BF)],
        ),
        out_shape=[out, out],
        compiler_params=pltpu.CompilerParams(vmem_limit_bytes=LIMIT),
        cost_estimate=pl.CostEstimate(flops=2 * rows * width * hidden, bytes_accessed=4 * rows * hidden, transcendentals=0),
        name="grad_outer",
    )(at, act, db2)


def input_kernel(plan, shard, count, at_ref, dfirst_ref, *rest):
    parts, rest = rest[:count], rest[count:]
    pieces, (out_ref, mat, sems) = rest[:-3], rest[-3:]

    @pl.when(pl.program_id(0) == 0)
    def _():
        for copy in load(qkv_copies(plan, pieces, at_ref, mat, shard), sems):
            copy.wait()

    width = mat.shape[0]
    wide = parts[0].shape[1]
    total = dfirst_ref[...]
    for i, part in enumerate(parts):
        start = (i % 3) * width + (i // 3) * wide
        total = total + dot_nt(part[...], mat[:, start : start + wide])
    out_ref[...] = total.astype(BF)


def input_gradient(at, dfirst, parts, plan, pieces, shard):
    rows, width = dfirst.shape
    blocks = 4
    count = sum(1 if masks is None else len(masks) for masks, _ in plan)

    def row(cols):
        return pl.BlockSpec((rows // blocks, cols), lambda i: (i, 0))

    return pl.pallas_call(
        lambda *refs: input_kernel(plan, shard, len(parts), *refs),
        grid=(blocks,),
        in_specs=[SCALAR, row(width)] + [row(part.shape[1]) for part in parts] + [MAT] * len(pieces),
        out_specs=row(width),
        out_shape=jax.ShapeDtypeStruct((rows, width), BF),
        scratch_shapes=[pltpu.VMEM((width, 3 * width), BF), pltpu.SemaphoreType.DMA((count,))],
        compiler_params=pltpu.CompilerParams(vmem_limit_bytes=LIMIT),
        cost_estimate=pl.CostEstimate(flops=6 * rows * width * width, bytes_accessed=14 * rows * width, transcendentals=0),
        name="input_gradient",
    )(at, dfirst, *parts, *pieces)


def column_sum(value):
    return jnp.sum(value.astype(F32), axis=0)


def fold(parts):
    return sum(part.astype(F32) for part in parts)


def halve(parts):
    half = parts[0].shape[0] // 2
    return fold([part[half:] for part in parts]).astype(BF), [part[:half] for part in parts]


def reduce_to_owner(value, owners):
    index = lax.axis_index("fsdp")
    parts = [value]
    for bit in reversed(bits_of(owners)):
        flag = (index // bit) & 1
        pairs = [part.reshape((-1, 2) + part.shape[1:]) for part in parts]
        sent = fold([pick(flag, pair[:, 1], pair[:, 0]) for pair in pairs]).astype(BF)
        parts = [pick(flag, pair[:, 0], pair[:, 1]) for pair in pairs] + [swap(sent, "fsdp", bit)]
    total = fold([part[0] for part in parts])
    for bit in (1, 2):
        own = total.astype(BF)
        total = own.astype(F32) + swap(own, "seq", bit).astype(F32)
    return total


def body(
    tokens, segment_ids, out_cotangent, query_weight, query_bias, key_weight, value_weight, value_bias,
    output_weight, output_bias, attn_gain, attn_shift, inner_weight, inner_bias, outer_weight, outer_bias,
    final_gain, final_shift,
):
    groups = lax.axis_size("seq")
    owners = lax.axis_size("fsdp")
    micro, seq_count, local_len, width = tokens.shape
    assert micro * seq_count == groups == 4
    rows = groups * local_len
    shard = query_weight.shape[0]
    hidden = inner_weight.shape[1]
    wide = hidden // owners
    lots = wide // shard
    aligned = shard % 32 == 0 and owners == 8
    place = lax.axis_index("seq")
    core = place & 1
    at = jnp.stack([lax.axis_index("fsdp"), place]).astype(jnp.int32)
    masks = order_of(owners)

    def to_sequences(value):
        return lax.all_to_all(value.reshape((groups, local_len) + value.shape[3:]), "seq", 0, 0, tiled=True)

    def to_tokens(value):
        moved = lax.all_to_all(value.reshape(groups, local_len, width), "seq", 0, 0, tiled=True)
        return moved.reshape(micro, seq_count, local_len, width)

    small = jnp.stack(
        [query_bias, value_bias, output_bias, attn_gain, attn_shift, outer_bias, final_gain, final_shift]
        + [inner_bias[i * shard : (i + 1) * shard] for i in range(lots)]
    )
    piece_a = pick(
        core,
        jnp.concatenate([query_weight, key_weight[:, : width // 2]], axis=1),
        jnp.concatenate([key_weight[:, width // 2 :], value_weight], axis=1),
    )
    piece_b = pick(
        core,
        jnp.concatenate([inner_weight[:, : hidden // 2], output_weight[:, : width // 2]], axis=1),
        jnp.concatenate([inner_weight[:, hidden // 2 :], output_weight[:, width // 2 :]], axis=1),
    )
    if aligned:
        a_far = swap(piece_a[None], "fsdp", 4)
        small_full = absolute(small[None], owners)
        x_rows = to_sequences(tokens).reshape(rows, width)
        doc = to_sequences(segment_ids).reshape(rows, 1)
        a_low = jnp.concatenate([piece_a[None], a_far])
        a_two = swap(a_low, "fsdp", 2)
        a_one = swap(a_low, "fsdp", 1)
        quarter = wide // 4
        piece_c = lax.dynamic_slice(outer_weight, (place * quarter, 0), (quarter, width))[None]
        c_far = swap(after(piece_c, a_two), "fsdp", 4)
        a_three = swap(a_two, "fsdp", 1)
        a_mine = [a_low, a_two, a_one, a_three]
        a_other = [swap(value, "seq", 1) for value in a_mine]
        quads = [(0, 4), (2, 6), (1, 5), (3, 7)]
        plan_a = [(quad, 0) for quad in quads] + [(quad, 1) for quad in quads]
        pieces_a = a_mine + a_other
    else:
        small_full = absolute(small[None], owners)
        x_rows = to_sequences(tokens).reshape(rows, width)
        doc = to_sequences(segment_ids).reshape(rows, 1)
        mine = absolute(piece_a[None], owners).reshape(width, -1)
        plan_a = [(None, 0), (None, 1)]
        pieces_a = [mine, swap(mine, "seq", 1)]
    small_full = small_full.astype(F32)
    vecs = small_full[:, :8].transpose(1, 0, 2).reshape(8, width)
    inner_vec = small_full[:, 8:].reshape(1, hidden)
    qkv_vec = jnp.concatenate([vecs[0:1], jnp.zeros((1, width), F32), vecs[1:2]], axis=1)
    ffn_vecs = vecs[2:]

    if aligned:
        qkv = project(at, after(x_rows, c_far), qkv_vec, plan_a, pieces_a, shard)
    else:
        qkv = project(at, x_rows, qkv_vec, plan_a, pieces_a, shard)
    pairs = width // PAIR
    calls = 3
    each = pairs // calls
    atts, logs = [], []
    if aligned:
        c_low = jnp.concatenate([piece_c, c_far])
        c_two = swap(c_low, "fsdp", 2)
        c_one = swap(c_low, "fsdp", 1)
        b_far = swap(after(piece_b, c_far)[None], "fsdp", 4)
        qkv = after(qkv, c_two, c_one)
        att, log = attend(doc, qkv, 0, each)
        atts.append(att)
        logs.append(log)
        c_three = swap(c_two, "fsdp", 1)
        c_side = [swap(c_low, "seq", 2), swap(c_two, "seq", 2)]
        b_low = jnp.concatenate([piece_b[None], b_far])
        qkv, _ = lax.optimization_barrier((qkv, (att, b_low, c_three, c_side)))
        att, log = attend(doc, qkv, each, each)
        atts.append(att)
        logs.append(log)
        b_two = swap(b_low, "fsdp", 2)
        b_one = swap(b_low, "fsdp", 1)
        c_side += [swap(c_one, "seq", 2), swap(c_three, "seq", 2)]
        grads_in = to_sequences(out_cotangent).reshape(rows, width)
        qkv, _ = lax.optimization_barrier((qkv, (att, b_two, b_one, c_side)))
        att, log = attend(doc, qkv, 2 * each, each)
        atts.append(att)
        logs.append(log)
        b_three = swap(b_two, "fsdp", 1)
        b_mine = [b_low, b_two, b_one, b_three]
        b_other = [swap(value, "seq", 1) for value in b_mine]
        plan_b, pieces_b = plan_a, b_mine + b_other
        c_mine = [c_low, c_two, c_one, c_three]
        c_all = c_mine + c_side
        plan_c = [(quad, mask) for mask in (0, 2, 1, 3) for quad in quads]
        pieces_c = c_all + [swap(value, "seq", 1) for value in c_all]
    else:
        for call in range(calls):
            att, log = attend(doc, qkv, call * each, each)
            atts.append(att)
            logs.append(log)
        grads_in = to_sequences(out_cotangent).reshape(rows, width)
        mine = absolute(piece_b[None], owners).reshape(width, -1)
        plan_b, pieces_b = plan_a, [mine, swap(mine, "seq", 1)]
        plan_c, pieces_c = [(None, 0)], [absolute(outer_weight[None], owners).reshape(hidden, width)]
    result, active, dinner, low, db2, db, dfirst, dattended, sums, dinner_vec = ffn(
        at, x_rows, grads_in, ffn_vecs, inner_vec, atts, plan_b, pieces_b, plan_c, pieces_c, shard
    )
    layer_out = to_tokens(result)

    backs = []

    def back(call, gate):
        return attend_back(doc, qkv, atts[call], gate, logs[call], call * each, each)

    def vectors():
        dq = jnp.concatenate([one[3] for one in backs], axis=1)
        dv = jnp.concatenate([one[4] for one in backs], axis=1)
        eight = jnp.concatenate([dq, dv, sums[:6]]).reshape(8, owners, shard).transpose(1, 0, 2)
        return jnp.concatenate([eight, dinner_vec.reshape(owners, lots, shard)], axis=1)

    if aligned:
        outer_keep, outer_send = grad_outer(at, owners, active, db2)
        outer_parts = [outer_keep, swap(outer_send, "seq", 1)]
        inner_kept, inner_side, inner_core, inner_both = grad_inner(at, masks, after(low, outer_keep), dinner, atts, db)
        outer_x, outer_parts = halve(outer_parts)
        gate = after(dattended, inner_kept, outer_x)
        backs.append(back(0, gate))
        outer_parts.append(swap(outer_x, "fsdp", 1))
        inner_parts = [inner_kept, swap(inner_core, "seq", 1)]
        inner_y = fold([inner_side, swap(inner_both, "seq", 1)]).astype(BF)
        gate, _ = lax.optimization_barrier((gate, (backs[0], inner_y, inner_parts)))
        backs.append(back(1, gate))
        inner_parts.append(swap(inner_y, "seq", 2))
        both = [jnp.concatenate([one[j] for one in backs], axis=1) for j in range(3)]
        first_keep, first_send = grad_wide(at, masks, x_rows, both)
        outer_z, outer_parts = halve(outer_parts)
        gate, _ = lax.optimization_barrier((gate, (first_keep, outer_z)))
        backs.append(back(2, gate))
        outer_parts.append(swap(outer_z, "fsdp", 2))
        first_parts = [first_keep, swap(first_send, "seq", 1)]
        outer_zz, outer_parts = halve(outer_parts)
        inner_x, inner_parts = halve(inner_parts)
        first_x, first_parts = halve(first_parts)
        extra = vectors()
        extra = jnp.pad(extra, ((0, 0), (0, 16 - extra.shape[1]), (0, each * PAIR - shard))).astype(BF)
        gated, _ = lax.optimization_barrier((x_rows, (outer_zz, inner_x, first_x)))
        second_keep, second_send = grad_wide(at, masks, gated, backs[2][:3], extra)
        dfirst, _ = lax.optimization_barrier((dfirst, (second_keep,)))
        parts = [value for one in backs for value in one[:3]]
        moved = input_gradient(at, dfirst, parts, plan_a, pieces_a, shard)
        input_grad = to_tokens(moved).astype(F32)
        outer_parts.append(swap(outer_zz, "fsdp", 4))
        inner_parts.append(swap(inner_x, "fsdp", 1))
        first_parts.append(swap(first_x, "fsdp", 1))
        second_parts = [second_keep, swap(second_send, "seq", 1)]
        second_x, second_parts = halve(second_parts)
        second_parts.append(swap(second_x, "fsdp", 1))
        groups_left = [inner_parts, first_parts, second_parts]
        for bit in (2, 4):
            sends = [halve(group) for group in groups_left]
            groups_left = [keep + [swap(sent, "fsdp", bit)] for sent, keep in sends]
        owns = [fold([part[0] for part in group]).astype(BF) for group in [outer_parts] + groups_left]
        others = [swap(own, "seq", 2) for own in owns]
        outer_own, first_own, second_own = (
            owns[i].astype(F32) + others[i].astype(F32) for i in (0, 2, 3)
        )
        side = place >> 1
        half = shard // 2
        cols = width // 2
        inner_own = pick(
            side,
            jnp.stack([value.reshape(half, -1, cols) for value in (owns[1], others[1])], axis=2),
            jnp.stack([value.reshape(half, -1, cols) for value in (others[1], owns[1])], axis=2),
        ).reshape(half, hidden + width)

        def whole(own):
            other = swap(own, "seq", 1)
            return pick(core, jnp.concatenate([own, other]), jnp.concatenate([other, own])).astype(F32)

        douter = whole(outer_own)
        dinner_full = whole(inner_own)
        part = 2 * each * PAIR
        firsts = whole(first_own)
        seconds = whole(second_own[:half])
        rest = each * PAIR
        dqkv = [
            jnp.concatenate([firsts[:, i * part : (i + 1) * part], seconds[:, i * rest : (i + 1) * rest]], axis=1)
            for i in range(3)
        ]
        vec = second_own[half : half + 8 + lots, :shard]
        dinner_w, doutput = dinner_full[:, :hidden], dinner_full[:, hidden:]
    else:
        for call in range(calls):
            backs.append(back(call, dattended))
        parts = [value for one in backs for value in one[:3]]
        moved = input_gradient(at, dfirst, parts, plan_a, pieces_a, shard)
        input_grad = to_tokens(moved).astype(F32)
        three = [jnp.concatenate([one[j] for one in backs], axis=1) for j in range(3)]
        att = jnp.concatenate(atts, axis=1)
        lefts = [x_rows, x_rows, x_rows, att, low]
        rights = three + [db, dinner]
        dqkv = []
        for left, right in zip(lefts, rights):
            dqkv.append(reduce_to_owner(dot_tn(left, right).astype(BF).reshape(owners, shard, -1), owners))
        doutput, dinner_w = dqkv[3:]
        douter = reduce_to_owner(dot_tn(active, db2).astype(BF).reshape(owners, wide, width), owners)
        vec = reduce_to_owner(vectors().astype(BF), owners)
    return (
        layer_out, input_grad, dqkv[0], vec[0], dqkv[1], dqkv[2], vec[1], doutput, vec[2], vec[3], vec[4], dinner_w,
        vec[8:].reshape(wide), douter, vec[5], vec[6], vec[7],
    )


def solution(mesh):
    rows = P(None, "fsdp", "seq", None)
    mat = P("fsdp", None)
    vec = P("fsdp")
    return jax.shard_map(
        body,
        mesh=mesh,
        in_specs=(
            rows, P(None, "fsdp", "seq"), rows, mat, vec, mat, mat, vec, mat, vec, vec, vec, mat, vec, mat, vec, vec, vec,
        ),
        out_specs=(rows, rows, mat, vec, mat, mat, vec, mat, vec, vec, vec, mat, vec, mat, vec, vec, vec),
        check_vma=False,
    )
```

time: 557 us -> 440 us (0.79)
  matrix products: 113 us -> 0 us
  Pallas kernels: 72.7 us -> 176 us
  waiting for transfers between devices: 196 us -> 117 us
  other arithmetic: 83.8 us -> 51.4 us
  starting transfers between devices: 50.9 us -> 69.7 us
  local copies, waits for them, and re-layouts: 33.8 us -> 18.6 us
    dot_general x12 -> x0, matrix products: 113 us -> none  [the longest x3 49.3 us: dot_nn(): lax.dot_general(a, b, (((1,), (0,)), ((), ())), preferred_element_type=F32)]
    pallas_call x1 -> x10, Pallas kernels: 29.2 us -> 127 us  [the longest x1 38 us: ffn(): pl.pallas_call(lambda *refs: ffn_kernel((inner_plan, outer_plan, len(atts...]
    ppermute x30 -> x61, waiting for transfers between devices: 180 us -> 97.8 us  [swap(): return lax.ppermute(value, axis, [(i, i ^ mask) for i in range(size)])]
    select_n x36 -> x10, other arithmetic: 44.7 us -> 4.54 us  [pick(): return jnp.where(flag == 0, low, high)]
    all_to_all x2, waiting for transfers between devices: 0.01 us -> 19.3 us  [to_tokens(): lax.all_to_all(value.reshape(groups, local_len, width), 'seq', 0, 0, tile...]
    ppermute x30 -> x61, starting transfers between devices: 31.6 us -> 49 us  [swap(): return lax.ppermute(value, axis, [(i, i ^ mask) for i in range(size)])]
    all_to_all x3, waiting for transfers between devices: 15.5 us -> 0.01 us  [to_sequences(): lax.all_to_all(value.reshape((groups, local_len) + value.shape[3:]), 'seq...]
    convert_element_type x13 -> x20, other arithmetic: 19.9 us -> 33.3 us  [the longest x12 21.1 us: halve(): fold([part[half:] for part in parts]).astype(BF)]
  transfers between devices with their start and end apart: 35 -> 66, of which waited for: 13 -> 21; matrix products, arithmetic and copies ran while one was open for 25% -> 14% of each run, Pallas kernels for 5% -> 29%
where the time goes in v2:
time: 440 us; the launch traced here: 435 us
  Pallas kernels  176 us (40%)
  waiting for transfers between devices  117 us (27%)
  starting transfers between devices  69.7 us (16%)
  other arithmetic  51.4 us (12%)
  local copies, waits for them, and re-layouts  18.6 us (4%)
    ppermute x61, waiting for transfers between devices, swap(): return lax.ppermute(value, axis, [(i, i ^ mask) for i in range(size)])  97.8 us
    pallas_call x3, Pallas kernels, attend_back(): pl.pallas_call(bwd_kernel, grid=(n,), in_specs=[pl.BlockSpec((rows, 1), l...  49.2 us
    ppermute x61, starting transfers between devices, swap(): return lax.ppermute(value, axis, [(i, i ^ mask) for i in range(size)])  49 us
    pallas_call x1, Pallas kernels, ffn(): pl.pallas_call(lambda *refs: ffn_kernel((inner_plan, outer_plan, len(atts...  38 us
    pallas_call x3, Pallas kernels, attend(): pl.pallas_call(fwd_kernel, grid=(n,), in_specs=[pl.BlockSpec((rows, 1), l...  34.5 us
    convert_element_type x12, other arithmetic, halve(): fold([part[half:] for part in parts]).astype(BF)  21.1 us
    all_to_all x2, waiting for transfers between devices, to_tokens(): lax.all_to_all(value.reshape(groups, local_len, width), 'seq', 0, 0, tile...  19.3 us
    all_to_all x3, starting transfers between devices, to_sequences(): lax.all_to_all(value.reshape((groups, local_len) + value.shape[3:]), 'seq...  12.5 us
  transfers between devices with their start and end apart: 66, of which 21 were waited for; matrix products, arithmetic and copies ran while one was open for 14% of the time, Pallas kernels for 29%

profile of v2, /device:TPU:0, one launch (start us, length us, event | category | flops | bytes accessed | tf_op | source)
XLA Modules:
  0.0 434.7 jit_solution(10797469986260887793)
XLA Ops:
  2.0 4.3 all-to-all-start.2
  8.0 3.1 collective-permute-start
  14.5 11.9 %collective-permute-done.3 = bf16[1,96,1152]{2,1,0:T(8,128)(2,1)S(1)} collective-permute-done((bf16[1,96,1152]{2,1,0:T(8,128)(2,1)S(1)}, bf16[1,96,1152]{2,1,0:T(8,128)(2,1)S(1)}, u32[]{:S(2)}, u32[]{:S(2)}) %collective-permute-start.3) | collective-permute-done | bytes 221216 | tf_op jit(solution)/shard_map/ppermute | solution.py:123
  28.9 9.0 %collective-permute-done.4.refs_4_.refs_12_ = bf16[2,96,1152]{2,1,0:T(8,128)(2,1)S(1)} collective-permute-done((bf16[2,96,1152]{2,1,0:T(8,128)(2,1)S(1)}, bf16[2,96,1152]{2,1,0:T(8,128)(2,1)S(1)}, u32[]{:S(2)}, u32[]{:S(2)}) %collective-permute-start.4) | collective-permute-done | bytes 442400 | tf_op jit(solution)/shard_map/ppermute | solution.py:123
  41.8 5.2 %collective-permute-done.5 = bf16[1,96,768]{2,1,0:T(8,128)(2,1)S(1)} collective-permute-done((bf16[1,96,768]{2,1,0:T(8,128)(2,1)S(1)}, bf16[1,96,768]{2,1,0:T(8,128)(2,1)S(1)}, u32[]{:S(2)}, u32[]{:S(2)}) %collective-permute-start.5) | collective-permute-done | bytes 147488 | tf_op jit(solution)/shard_map/ppermute | solution.py:123
  47.1 3.6 all-to-all-start
  55.5 2.0 collective-permute-start.16
  57.6 8.6 %collective-permute-done.14 = bf16[1,96,1920]{2,1,0:T(8,128)(2,1)S(1)} collective-permute-done((bf16[1,96,1920]{2,1,0:T(8,128)(2,1)}, bf16[1,96,1920]{2,1,0:T(8,128)(2,1)S(1)}, u32[]{:S(2)}, u32[]{:S(2)}) %collective-permute-start.14) | collective-permute-done | bytes 368672 | tf_op jit(solution)/shard_map/ppermute | solution.py:123
  70.2 6.8 %collective-permute-done.16.refs_20_ = bf16[2,96,768]{2,1,0:T(8,128)(2,1)S(1)} collective-permute-done((bf16[2,96,768]{2,1,0:T(8,128)(2,1)}, bf16[2,96,768]{2,1,0:T(8,128)(2,1)S(1)}, u32[]{:S(2)}, u32[]{:S(2)}) %collective-permute-start.16) | collective-permute-done | bytes 294944 | tf_op jit(solution)/shard_map/ppermute | solution.py:123
  77.0 3.2 collective-permute-start.18
  81.9 3.2 collective-permute-done.13.refs_18_
  87.5 4.6 %all-to-all-start.1 = ((bf16[4,256,768]{2,1,0:T(8,128)(2,1)}), bf16[4,256,768]{2,1,0:T(8,128)(2,1)}, u32[]{:S(2)}, u32[]{:S(2)}) async-start(bf16[4,256,768]{2,1,0:T(8,128)(2,1)} %bitcast.4), calls=%async_computation.1 | async-start | bytes 3145728 | tf_op jit(solution)/shard_map/all_to_all | solution.py:592
  98.1 8.9 %project.1.q_ref.k_ref.v_ref = bf16[1024,2304]{1,0:T(8,128)(2,1)} custom-call(s32[2]{0:T(128)} %pad_add_fusion.refs_0_.at_ref, bf16[1024,768]{1,0:T(8,128)(2,1)} %bitcast.82, f32[1,2304]{1,0:T(1,128)} %fusion.11.refs_2_, bf16[2,96,1152]{2,1,0:T(8,128)(2,1)} %copy-done.12, bf16[2,96,1152]{2,1,0:T(8,128)(2,1)} %copy-done.25, ...), custom_call_target="tpu_custom_call" | custom-call | flops 3623878656 | bytes 11010048 | tf_op jit(solution)/shard_map/project/pallas_call | solution.py:209
  107.1 11.3 %collective-permute-done.17.refs_21_ = bf16[2,96,768]{2,1,0:T(8,128)(2,1)S(1)} collective-permute-done((bf16[2,96,768]{2,1,0:T(8,128)(2,1)}, bf16[2,96,768]{2,1,0:T(8,128)(2,1)S(1)}, u32[]{:S(2)}, u32[]{:S(2)}) %collective-permute-start.17) | collective-permute-done | bytes 294944 | tf_op jit(solution)/shard_map/ppermute | solution.py:123
  118.9 11.2 %attend.3 = (bf16[1024,256]{1,0:T(8,128)(2,1)}, f32[2,1024,2]{2,1,0:T(8,128)}) custom-call(s32[1024,1]{1,0:T(8,128)} %copy.63.doc_ref, bf16[1024,2304]{1,0:T(8,128)(2,1)} %project.1.q_ref.k_ref.v_ref, bf16[1024,2304]{1,0:T(8,128)(2,1)} %project.1.q_ref.k_ref.v_ref, bf16[1024,2304]{1,0:T(8,128)(2,1)} %project.1.q_ref.k_ref.v_ref), custom_call_target="tpu_custom_call" | custom-call | flops 4294967296 | bytes 2097152 | tf_op jit(solution)/shard_map/attend/pallas_call | solution.py:47
  131.3 3.8 collective-permute-done.22.refs_11_
  135.1 11.5 %attend.4 = (bf16[1024,256]{1,0:T(8,128)(2,1)}, f32[2,1024,2]{2,1,0:T(8,128)}) custom-call(s32[1024,1]{1,0:T(8,128)} %copy.63.doc_ref, bf16[1024,2304]{1,0:T(8,128)(2,1)} %project.1.q_ref.k_ref.v_ref, bf16[1024,2304]{1,0:T(8,128)(2,1)} %project.1.q_ref.k_ref.v_ref, bf16[1024,2304]{1,0:T(8,128)(2,1)} %project.1.q_ref.k_ref.v_ref), custom_call_target="tpu_custom_call" | custom-call | flops 4294967296 | bytes 2097152 | tf_op jit(solution)/shard_map/attend/pallas_call | solution.py:47
  147.0 11.8 %attend.5 = (bf16[1024,256]{1,0:T(8,128)(2,1)}, f32[2,1024,2]{2,1,0:T(8,128)}) custom-call(s32[1024,1]{1,0:T(8,128)} %copy.63.doc_ref, bf16[1024,2304]{1,0:T(8,128)(2,1)} %project.1.q_ref.k_ref.v_ref, bf16[1024,2304]{1,0:T(8,128)(2,1)} %project.1.q_ref.k_ref.v_ref, bf16[1024,2304]{1,0:T(8,128)(2,1)} %project.1.q_ref.k_ref.v_ref), custom_call_target="tpu_custom_call" | custom-call | flops 4294967296 | bytes 2097152 | tf_op jit(solution)/shard_map/attend/pallas_call | solution.py:47
  159.5 38.0 %ffn.1 = (bf16[1024,768]{1,0:T(8,128)(2,1)}, bf16[1024,3072]{1,0:T(8,128)(2,1)}, bf16[1024,3072]{1,0:T(8,128)(2,1)}, bf16[1024,768]{1,0:T(8,128)(2,1)}, bf16[102...) custom-call(s32[2]{0:T(128)} %pad_add_fusion.refs_0_.at_ref, ...), custom_call_target="tpu_custom_call" | custom-call | flops 21743271936 | bytes 28311552 | tf_op jit(solution)/shard_map/ffn/pallas_call | solution.py:335
  197.5 12.3 %grad_outer.1 = (bf16[8,192,768]{2,1,0:T(8,128)(2,1)}, bf16[8,192,768]{2,1,0:T(8,128)(2,1)}) custom-call(s32[2]{0:T(128)} %pad_add_fusion.refs_0_.at_ref, bf16[1024,3072]{1,0:T(8,128)(2,1)} %get-tuple-element.83.refs_1_, bf16[1024,768]{1,0:T(8,128)(2,1)} %get-tuple-element.84.refs_2_), custom_call_target="tpu_custom_call" | custom-call | flops 4831838208 | bytes 12582912 | tf_op jit(solution)/shard_map/grad_outer/pallas_call | solution.py:488
  210.1 12.2 %grad_inner.1 = (bf16[8,48,1920]{2,1,0:T(8,128)(2,1)}, bf16[8,48,1920]{2,1,0:T(8,128)(2,1)}, bf16[8,48,1920]{2,1,0:T(8,128)(2,1)}, bf16[8,48,1920]{2,1,0:T(8,128)(2,1)}) custom-call(s32[2]{0:T(128)} %pad_add_fusion.refs_0_.at_ref, bf16[1024,768]{1,0:T(8,128)(2,1)} %get-tuple-element.86.low_ref, bf16[1024,3072]{1,0:T(8,128)(2,1)} %get-tuple-element.87.din_ref, ...), custom_call_target="tpu_custom_call" | custom-call | flops 6039797760 | bytes 12582912 | tf_op jit(solution)/shard_map/grad_inner/pallas_call | solution.py:450
  222.5 3.7 all-to-all-start.3
  226.9 19.3 %all-to-all-done.3 = bf16[4,256,768]{2,1,0:T(8,128)(2,1)S(1)} async-done(((bf16[4,256,768]{2,1,0:T(8,128)(2,1)}), bf16[4,256,768]{2,1,0:T(8,128)(2,1)S(1)}, u32[]{:S(2)}, u32[]{:S(2)}) %all-to-all-start.3) | async-done | bytes 1572896 | tf_op jit(solution)/shard_map/all_to_all | solution.py:595
  246.3 3.4 add_convert_fusion
  253.2 16.2 %attend_back.3 = (bf16[1024,256]{1,0:T(8,128)(2,1)}, bf16[1024,256]{1,0:T(8,128)(2,1)}, bf16[1024,256]{1,0:T(8,128)(2,1)}, f32[1,256]{1,0:T(1,128)}, f32[1,256]{1,0:T(1,128)}) custom-call(s32[1024,1]{1,0:T(8,128)} %copy.63.doc_ref, bf16[1024,2304]{1,0:T(8,128)(2,1)} %project.1.q_ref.k_ref.v_ref, bf16[1024,2304]{1,0:T(8,128)(2,1)} %project.1.q_ref.k_ref.v_ref, ...), custom_call_target="tpu_custom_call" | custom-call | flops 6442450944 | bytes 4194304 | tf_op jit(solution)/shard_map/attend_back/pallas_call | solution.py:105
  269.5 16.4 %attend_back.4 = (bf16[1024,256]{1,0:T(8,128)(2,1)}, bf16[1024,256]{1,0:T(8,128)(2,1)}, bf16[1024,256]{1,0:T(8,128)(2,1)}, f32[1,256]{1,0:T(1,128)}, f32[1,256]{1,0:T(1,128)}) custom-call(s32[1024,1]{1,0:T(8,128)} %copy.63.doc_ref, bf16[1024,2304]{1,0:T(8,128)(2,1)} %project.1.q_ref.k_ref.v_ref, bf16[1024,2304]{1,0:T(8,128)(2,1)} %project.1.q_ref.k_ref.v_ref, ...), custom_call_target="tpu_custom_call" | custom-call | flops 6442450944 | bytes 4194304 | tf_op jit(solution)/shard_map/attend_back/pallas_call | solution.py:105
  287.5 2.1 pad_maximum_fusion.2.refs_3_
  291.1 6.5 %grad_wide.2 = (bf16[8,48,1536]{2,1,0:T(8,128)(2,1)}, bf16[8,48,1536]{2,1,0:T(8,128)(2,1)}) custom-call(s32[2]{0:T(128)} %pad_add_fusion.refs_0_.at_ref, bf16[1024,768]{1,0:T(8,128)(2,1)} %bitcast.84, bf16[1024,512]{1,0:T(8,128)(2,1)} %get-tuple-element.153.refs_1_, bf16[1024,512]{1,0:T(8,128)(2,1)} %get-tuple-element.154.refs_2_, ...), custom_call_target="tpu_custom_call" | custom-call | flops 2415919104 | bytes 5505024 | tf_op jit(solution)/shard_map/grad_wide/pallas_call | solution.py:401
  297.6 2.7 add_convert_fusion.2
  300.9 2.5 add_convert_fusion.4
  303.4 16.6 %attend_back.5 = (bf16[1024,256]{1,0:T(8,128)(2,1)}, bf16[1024,256]{1,0:T(8,128)(2,1)}, bf16[1024,256]{1,0:T(8,128)(2,1)}, f32[1,256]{1,0:T(1,128)}, f32[1,256]{1,0:T(1,128)}) custom-call(s32[1024,1]{1,0:T(8,128)} %copy.63.doc_ref, bf16[1024,2304]{1,0:T(8,128)(2,1)} %project.1.q_ref.k_ref.v_ref, bf16[1024,2304]{1,0:T(8,128)(2,1)} %project.1.q_ref.k_ref.v_ref, ...), custom_call_target="tpu_custom_call" | custom-call | flops 6442450944 | bytes 4194304 | tf_op jit(solution)/shard_map/attend_back/pallas_call | solution.py:105
  323.0 2.1 collective-permute-start.54
  328.5 5.3 %collective-permute-done.54 = bf16[2,48,1920]{2,1,0:T(8,128)(2,1)S(1)} collective-permute-done((bf16[2,48,1920]{2,1,0:T(8,128)(2,1)S(1)}, bf16[2,48,1920]{2,1,0:T(8,128)(2,1)S(1)}, u32[]{:S(2)}, u32[]{:S(2)}) %collective-permute-start.54) | collective-permute-done | bytes 368672 | tf_op jit(solution)/shard_map/ppermute | solution.py:123
  336.5 2.2 collective-permute-start.55
  338.7 2.1 add_convert_fusion.9
  341.6 4.8 %grad_wide.3 = (bf16[8,64,768]{2,1,0:T(8,128)(2,1)}, bf16[8,64,768]{2,1,0:T(8,128)(2,1)}) custom-call(s32[2]{0:T(128)} %pad_add_fusion.refs_0_.at_ref, bf16[8,16,256]{2,1,0:T(8,128)(2,1)} %fusion.9.refs_0_, bf16[1024,768]{1,0:T(8,128)(2,1)} %bitcast.85, bf16[1024,256]{1,0:T(8,128)(2,1)} %get-tuple-element.117.refs_2_.refs_8_, ...), custom_call_target="tpu_custom_call" | custom-call | flops 1207959552 | bytes 2752512 | tf_op jit(solution)/shard_map/grad_wide/pallas_call | solution.py:401
  346.3 9.7 %input_gradient.1 = bf16[1024,768]{1,0:T(8,128)(2,1)} custom-call(s32[2]{0:T(128)} %pad_add_fusion.refs_0_.at_ref, f32[1024,768]{1,0:T(8,128)} %get-tuple-element.121.refs_1_, bf16[1024,256]{1,0:T(8,128)(2,1)} %get-tuple-element.94.refs_2_, bf16[1024,256]{1,0:T(8,128)(2,1)} %get-tuple-element.95.refs_3_, bf16[1024,256]{1,0:T(8,128)(2,1)} %get-tuple-element.96.refs_4_, ...), custom_call_target="tpu_custom_call" | custom-call | flops 3623878656 | bytes 11010048 | tf_op jit(solution)/shard_map/input_gradient/pallas_call | solution.py:530
  356.0 4.5 %all-to-all-start.4 = ((bf16[4,256,768]{2,1,0:T(8,128)(2,1)}), bf16[4,256,768]{2,1,0:T(8,128)(2,1)}, u32[]{:S(2)}, u32[]{:S(2)}) async-start(bf16[4,256,768]{2,1,0:T(8,128)(2,1)} %bitcast.86), calls=%async_computation.4 | async-start | bytes 3145728 | tf_op jit(solution)/shard_map/all_to_all | solution.py:595
  368.5 3.5 collective-permute-done.43
  373.9 2.2 collective-permute-start.44
  379.3 5.8 %collective-permute-done.56 = bf16[48,1920]{1,0:T(8,128)(2,1)S(1)} collective-permute-done((bf16[48,1920]{1,0:T(8,128)(2,1)S(1)}, bf16[48,1920]{1,0:T(8,128)(2,1)S(1)}, u32[]{:S(2)}, u32[]{:S(2)}) %collective-permute-start.56) | collective-permute-done | bytes 184352 | tf_op jit(solution)/shard_map/ppermute | solution.py:123
  388.9 2.1 collective-permute-done.59
  392.1 3.0 collective-permute-done.45
  399.8 8.1 %collective-permute-done.48 = bf16[4,64,768]{2,1,0:T(8,128)(2,1)S(1)} collective-permute-done((bf16[4,64,768]{2,1,0:T(8,128)(2,1)S(1)}, bf16[4,64,768]{2,1,0:T(8,128)(2,1)S(1)}, u32[]{:S(2)}, u32[]{:S(2)}) %collective-permute-start.48) | collective-permute-done | bytes 393248 | tf_op jit(solution)/shard_map/ppermute | solution.py:123
  410.9 4.6 %collective-permute-done.49 = bf16[2,64,768]{2,1,0:T(8,128)(2,1)S(1)} collective-permute-done((bf16[2,64,768]{2,1,0:T(8,128)(2,1)S(1)}, bf16[2,64,768]{2,1,0:T(8,128)(2,1)S(1)}, u32[]{:S(2)}, u32[]{:S(2)}) %collective-permute-start.49) | collective-permute-done | bytes 196640 | tf_op jit(solution)/shard_map/ppermute | solution.py:123
  417.1 2.2 collective-permute-start.50
  419.3 3.3 convert.50
  425.5 3.2 collective-permute-done.51
  (265 shorter events, 88.3 us)
Async XLA Ops:
  2.0 45.1 %all-to-all-start.2 = ((s32[4,1,256]{2,1,0:T(1,128)}), s32[4,1,256]{2,1,0:T(1,128)S(1)}, u32[]{:S(2)}, u32[]{:S(2)}) async-start(s32[4,1,256]{2,1,0:T(1,128)} %all_to_all.20), calls=%async_computation.2 | async-start | bytes 8192 | tf_op jit(solution)/shard_map/all_to_all | solution.py:592
  8.0 32.0 %collective-permute-start = (bf16[1,12,96]{2,1,0:T(8,128)(2,1)S(1)}, bf16[1,12,96]{2,1,0:T(8,128)(2,1)S(1)}, u32[]{:S(2)}, u32[]{:S(2)}) collective-permute-start(bf16[1,12,96]{2,1,0:T(8,128)(2,1)S(1)} %bitcast.96), channel_id=1, source_target_pairs={{0,4},{1,5},{2,6},{3,7},{4,0},{5,1},{6,2},{7,3},{8,12},{9,13},{10,... | collective-permute-start | bytes 6920 | tf_op jit(solution)/shard_map/ppermute | solution.py:123
  13.2 13.2 %collective-permute-start.3 = (bf16[1,96,1152]{2,1,0:T(8,128)(2,1)S(1)}, bf16[1,96,1152]{2,1,0:T(8,128)(2,1)S(1)}, u32[]{:S(2)}, u32[]{:S(2)}) collective-permute-start(bf16[1,96,1152]{2,1,0:T(8,128)(2,1)S(1)} %maximum_select_fusion.7), channel_id=1, source_target_pairs={{0,4},{1,5},{2,6},{3,7},{4,0},{5,1},{6,2},{7,3},{8,12},{9,13},{10,... | collective-permute-start | bytes 663560 | tf_op jit(solution)/shard_map/ppermute | solution.py:123
  27.4 26.1 %collective-permute-start.6 = (bf16[2,96,1152]{2,1,0:T(8,128)(2,1)S(1)}, bf16[2,96,1152]{2,1,0:T(8,128)(2,1)}, u32[]{:S(2)}, u32[]{:S(2)}) collective-permute-start(bf16[2,96,1152]{2,1,0:T(8,128)(2,1)S(1)} %pad_maximum_fusion.4.refs_3_.refs_11_), channel_id=1, source_target_pairs={{0,1},{1,0},{2,3},{3,2},{4,5},{5,4},{6,7},{7,6},{8,9},{9,8},{10,11... | collective-permute-start | bytes 1327112 | tf_op jit(solution)/shard_map/ppermute | solution.py:123
  47.1 19.1 %collective-permute-start.14 = (bf16[1,96,1920]{2,1,0:T(8,128)(2,1)}, bf16[1,96,1920]{2,1,0:T(8,128)(2,1)S(1)}, u32[]{:S(2)}, u32[]{:S(2)}) collective-permute-start(bf16[1,96,1920]{2,1,0:T(8,128)(2,1)} %bitcast.37), channel_id=1, source_target_pairs={{0,4},{1,5},{2,6},{3,7},{4,0},{5,1},{6,2},{7,3},{8,12},{9,13},{10,... | collective-permute-start | bytes 1105928 | tf_op jit(solution)/shard_map/ppermute | solution.py:123
  47.1 39.2 %all-to-all-start = ((bf16[4,256,768]{2,1,0:T(8,128)(2,1)}), bf16[4,256,768]{2,1,0:T(8,128)(2,1)S(1)}, u32[]{:S(2)}, u32[]{:S(2)}) async-start(bf16[4,256,768]{2,1,0:T(8,128)(2,1)} %bitcast.2), calls=%async_computation | async-start | bytes 3145728 | tf_op jit(solution)/shard_map/all_to_all | solution.py:592
  53.3 16.2 %collective-permute-start.8 = (bf16[2,96,1152]{2,1,0:T(8,128)(2,1)S(1)}, bf16[2,96,1152]{2,1,0:T(8,128)(2,1)S(1)}, u32[]{:S(2)}, u32[]{:S(2)}) collective-permute-start(bf16[2,96,1152]{2,1,0:T(8,128)(2,1)S(1)} %pad_maximum_fusion.4.refs_3_.refs_11_), channel_id=1, source_target_pairs={{0,8},{8,0},{16,24},{24,16},{1,9},{9,1},{17,25},{25,17},{2,10},{10... | collective-permute-start | bytes 1327112 | tf_op jit(solution)/shard_map/ppermute | solution.py:123
  53.5 16.1 %collective-permute-start.10 = (bf16[2,96,1152]{2,1,0:T(8,128)(2,1)}, bf16[2,96,1152]{2,1,0:T(8,128)(2,1)S(1)}, u32[]{:S(2)}, u32[]{:S(2)}) collective-permute-start(bf16[2,96,1152]{2,1,0:T(8,128)(2,1)} %collective-permute-done.6.refs_5_.refs_13_), channel_id=1, source_target_pairs={{0,8},{8,0},{16,24},{24,16},{1,9},{9,1},{17,25},{25,17},{2,10},{10... | collective-permute-start | bytes 1327112 | tf_op jit(solution)/shard_map/ppermute | solution.py:123
  54.6 15.6 %collective-permute-start.27 = (bf16[2,96,768]{2,1,0:T(8,128)(2,1)}, bf16[2,96,768]{2,1,0:T(8,128)(2,1)S(1)}, u32[]{:S(2)}, u32[]{:S(2)}) collective-permute-start(bf16[2,96,768]{2,1,0:T(8,128)(2,1)} %pad_maximum_fusion.5.refs_16_), channel_id=1, source_target_pairs={{0,8},{8,0},{16,24},{24,16},{1,9},{9,1},{17,25},{25,17},{2,10},{10... | collective-permute-start | bytes 884744 | tf_op jit(solution)/shard_map/ppermute | solution.py:123
  55.5 21.5 %collective-permute-start.16 = (bf16[2,96,768]{2,1,0:T(8,128)(2,1)}, bf16[2,96,768]{2,1,0:T(8,128)(2,1)S(1)}, u32[]{:S(2)}, u32[]{:S(2)}) collective-permute-start(bf16[2,96,768]{2,1,0:T(8,128)(2,1)} %pad_maximum_fusion.5.refs_16_), channel_id=1, source_target_pairs={{0,16},{8,24},{16,0},{24,8},{1,17},{9,25},{17,1},{25,9},{2,18},{10... | collective-permute-start | bytes 884744 | tf_op jit(solution)/shard_map/ppermute | solution.py:123
  66.9 13.4 %collective-permute-start.7 = (bf16[2,96,1152]{2,1,0:T(8,128)(2,1)}, bf16[2,96,1152]{2,1,0:T(8,128)(2,1)}, u32[]{:S(2)}, u32[]{:S(2)}) collective-permute-start(bf16[2,96,1152]{2,1,0:T(8,128)(2,1)} %copy-done.25), channel_id=1, source_target_pairs={{0,1},{1,0},{2,3},{3,2},{4,5},{5,4},{6,7},{7,6},{8,9},{9,8},{10,11... | collective-permute-start | bytes 1327112 | tf_op jit(solution)/shard_map/ppermute | solution.py:123
  69.5 15.7 %collective-permute-start.9 = (bf16[2,96,1152]{2,1,0:T(8,128)(2,1)}, bf16[2,96,1152]{2,1,0:T(8,128)(2,1)S(1)}, u32[]{:S(2)}, u32[]{:S(2)}) collective-permute-start(bf16[2,96,1152]{2,1,0:T(8,128)(2,1)} %copy-done.25), channel_id=1, source_target_pairs={{0,8},{8,0},{16,24},{24,16},{1,9},{9,1},{17,25},{25,17},{2,10},{10... | collective-permute-start | bytes 1327112 | tf_op jit(solution)/shard_map/ppermute | solution.py:123
  69.6 15.5 %collective-permute-start.13 = (bf16[2,96,768]{2,1,0:T(8,128)(2,1)}, bf16[2,96,768]{2,1,0:T(8,128)(2,1)S(1)}, u32[]{:S(2)}, u32[]{:S(2)}) collective-permute-start(bf16[2,96,768]{2,1,0:T(8,128)(2,1)} %pad_maximum_fusion.5.refs_16_), channel_id=1, source_target_pairs={{0,1},{1,0},{2,3},{3,2},{4,5},{5,4},{6,7},{7,6},{8,9},{9,8},{10,11... | collective-permute-start | bytes 884744 | tf_op jit(solution)/shard_map/ppermute | solution.py:123
  70.2 14.9 %collective-permute-start.12 = (bf16[2,96,768]{2,1,0:T(8,128)(2,1)}, bf16[2,96,768]{2,1,0:T(8,128)(2,1)}, u32[]{:S(2)}, u32[]{:S(2)}) collective-permute-start(bf16[2,96,768]{2,1,0:T(8,128)(2,1)} %pad_maximum_fusion.5.refs_16_), channel_id=1, source_target_pairs={{0,2},{1,3},{2,0},{3,1},{4,6},{5,7},{6,4},{7,5},{8,10},{9,11},{10,... | collective-permute-start | bytes 884744 | tf_op jit(solution)/shard_map/ppermute | solution.py:123
  77.0 19.6 %collective-permute-start.18 = (bf16[2,96,1920]{2,1,0:T(8,128)(2,1)S(1)}, bf16[2,96,1920]{2,1,0:T(8,128)(2,1)}, u32[]{:S(2)}, u32[]{:S(2)}) collective-permute-start(bf16[2,96,1920]{2,1,0:T(8,128)(2,1)S(1)} %pad_maximum_fusion.3.refs_8_), channel_id=1, source_target_pairs={{0,2},{1,3},{2,0},{3,1},{4,6},{5,7},{6,4},{7,5},{8,10},{9,11},{10,... | collective-permute-start | bytes 2211848 | tf_op jit(solution)/shard_map/ppermute | solution.py:123
  80.3 15.9 %collective-permute-start.11 = (bf16[2,96,1152]{2,1,0:T(8,128)(2,1)}, bf16[2,96,1152]{2,1,0:T(8,128)(2,1)}, u32[]{:S(2)}, u32[]{:S(2)}) collective-permute-start(bf16[2,96,1152]{2,1,0:T(8,128)(2,1)} %collective-permute-done.7.refs_6_.refs_14_), channel_id=1, source_target_pairs={{0,8},{8,0},{16,24},{24,16},{1,9},{9,1},{17,25},{25,17},{2,10},{10... | collective-permute-start | bytes 1327112 | tf_op jit(solution)/shard_map/ppermute | solution.py:123
  87.5 71.3 %all-to-all-start.1 = ((bf16[4,256,768]{2,1,0:T(8,128)(2,1)}), bf16[4,256,768]{2,1,0:T(8,128)(2,1)}, u32[]{:S(2)}, u32[]{:S(2)}) async-start(bf16[4,256,768]{2,1,0:T(8,128)(2,1)} %bitcast.4), calls=%async_computation.1 | async-start | bytes 3145728 | tf_op jit(solution)/shard_map/all_to_all | solution.py:592
  92.1 14.9 %collective-permute-start.28 = (bf16[2,96,768]{2,1,0:T(8,128)(2,1)}, bf16[2,96,768]{2,1,0:T(8,128)(2,1)S(1)}, u32[]{:S(2)}, u32[]{:S(2)}) collective-permute-start(bf16[2,96,768]{2,1,0:T(8,128)(2,1)} %collective-permute-done.12.refs_17_), channel_id=1, source_target_pairs={{0,8},{8,0},{16,24},{24,16},{1,9},{9,1},{17,25},{25,17},{2,10},{10... | collective-permute-start | bytes 884744 | tf_op jit(solution)/shard_map/ppermute | solution.py:123
  92.7 25.8 %collective-permute-start.17 = (bf16[2,96,768]{2,1,0:T(8,128)(2,1)}, bf16[2,96,768]{2,1,0:T(8,128)(2,1)S(1)}, u32[]{:S(2)}, u32[]{:S(2)}) collective-permute-start(bf16[2,96,768]{2,1,0:T(8,128)(2,1)} %collective-permute-done.12.refs_17_), channel_id=1, source_target_pairs={{0,16},{8,24},{16,0},{24,8},{1,17},{9,25},{17,1},{25,9},{2,18},{10... | collective-permute-start | bytes 884744 | tf_op jit(solution)/shard_map/ppermute | solution.py:123
  94.6 23.8 %collective-permute-start.15 = (bf16[2,96,768]{2,1,0:T(8,128)(2,1)}, bf16[2,96,768]{2,1,0:T(8,128)(2,1)S(1)}, u32[]{:S(2)}, u32[]{:S(2)}) collective-permute-start(bf16[2,96,768]{2,1,0:T(8,128)(2,1)} %collective-permute-done.12.refs_17_), channel_id=1, source_target_pairs={{0,1},{1,0},{2,3},{3,2},{4,5},{5,4},{6,7},{7,6},{8,9},{9,8},{10,11... | collective-permute-start | bytes 884744 | tf_op jit(solution)/shard_map/ppermute | solution.py:123
  96.1 34.9 %collective-permute-start.19 = (bf16[2,96,1920]{2,1,0:T(8,128)(2,1)S(1)}, bf16[2,96,1920]{2,1,0:T(8,128)(2,1)S(1)}, u32[]{:S(2)}, u32[]{:S(2)}) collective-permute-start(bf16[2,96,1920]{2,1,0:T(8,128)(2,1)S(1)} %pad_maximum_fusion.3.refs_8_), channel_id=1, source_target_pairs={{0,1},{1,0},{2,3},{3,2},{4,5},{5,4},{6,7},{7,6},{8,9},{9,8},{10,11... | collective-permute-start | bytes 2211848 | tf_op jit(solution)/shard_map/ppermute | solution.py:123
  96.7 38.5 %collective-permute-start.22 = (bf16[2,96,1920]{2,1,0:T(8,128)(2,1)}, bf16[2,96,1920]{2,1,0:T(8,128)(2,1)S(1)}, u32[]{:S(2)}, u32[]{:S(2)}) collective-permute-start(bf16[2,96,1920]{2,1,0:T(8,128)(2,1)} %collective-permute-done.18.refs_9_), channel_id=1, source_target_pairs={{0,1},{1,0},{2,3},{3,2},{4,5},{5,4},{6,7},{7,6},{8,9},{9,8},{10,11... | collective-permute-start | bytes 2211848 | tf_op jit(solution)/shard_map/ppermute | solution.py:123
  107.0 23.1 %collective-permute-start.33 = (bf16[2,96,768]{2,1,0:T(8,128)(2,1)}, bf16[2,96,768]{2,1,0:T(8,128)(2,1)S(1)}, u32[]{:S(2)}, u32[]{:S(2)}) collective-permute-start(bf16[2,96,768]{2,1,0:T(8,128)(2,1)} %collective-permute-done.20.refs_22_), channel_id=1, source_target_pairs={{0,8},{8,0},{16,24},{24,16},{1,9},{9,1},{17,25},{25,17},{2,10},{10... | collective-permute-start | bytes 884744 | tf_op jit(solution)/shard_map/ppermute | solution.py:123
  118.4 12.4 %collective-permute-start.21 = (bf16[2,96,768]{2,1,0:T(8,128)(2,1)S(1)}, bf16[2,96,768]{2,1,0:T(8,128)(2,1)}, u32[]{:S(2)}, u32[]{:S(2)}) collective-permute-start(bf16[2,96,768]{2,1,0:T(8,128)(2,1)S(1)} %collective-permute-done.15.refs_19_), channel_id=1, source_target_pairs={{0,16},{8,24},{16,0},{24,8},{1,17},{9,25},{17,1},{25,9},{2,18},{10... | collective-permute-start | bytes 884744 | tf_op jit(solution)/shard_map/ppermute | solution.py:123
  130.2 28.6 %collective-permute-start.23 = (bf16[2,96,1920]{2,1,0:T(8,128)(2,1)S(1)}, bf16[2,96,1920]{2,1,0:T(8,128)(2,1)}, u32[]{:S(2)}, u32[]{:S(2)}) collective-permute-start(bf16[2,96,1920]{2,1,0:T(8,128)(2,1)S(1)} %pad_maximum_fusion.3.refs_8_), channel_id=1, source_target_pairs={{0,8},{8,0},{16,24},{24,16},{1,9},{9,1},{17,25},{25,17},{2,10},{10... | collective-permute-start | bytes 2211848 | tf_op jit(solution)/shard_map/ppermute | solution.py:123
  130.4 16.3 %collective-permute-start.30 = (bf16[2,96,768]{2,1,0:T(8,128)(2,1)S(1)}, bf16[2,96,768]{2,1,0:T(8,128)(2,1)S(1)}, u32[]{:S(2)}, u32[]{:S(2)}) collective-permute-start(bf16[2,96,768]{2,1,0:T(8,128)(2,1)S(1)} %collective-permute-done.15.refs_19_), channel_id=1, source_target_pairs={{0,8},{8,0},{16,24},{24,16},{1,9},{9,1},{17,25},{25,17},{2,10},{10... | collective-permute-start | bytes 884744 | tf_op jit(solution)/shard_map/ppermute | solution.py:123
  130.8 28.0 %collective-permute-start.24 = (bf16[2,96,1920]{2,1,0:T(8,128)(2,1)}, bf16[2,96,1920]{2,1,0:T(8,128)(2,1)}, u32[]{:S(2)}, u32[]{:S(2)}) collective-permute-start(bf16[2,96,1920]{2,1,0:T(8,128)(2,1)} %collective-permute-done.18.refs_9_), channel_id=1, source_target_pairs={{0,8},{8,0},{16,24},{24,16},{1,9},{9,1},{17,25},{25,17},{2,10},{10... | collective-permute-start | bytes 2211848 | tf_op jit(solution)/shard_map/ppermute | solution.py:123
  131.0 27.8 %collective-permute-start.25 = (bf16[2,96,1920]{2,1,0:T(8,128)(2,1)S(1)}, bf16[2,96,1920]{2,1,0:T(8,128)(2,1)}, u32[]{:S(2)}, u32[]{:S(2)}) collective-permute-start(bf16[2,96,1920]{2,1,0:T(8,128)(2,1)S(1)} %collective-permute-done.19.refs_10_), channel_id=1, source_target_pairs={{0,8},{8,0},{16,24},{24,16},{1,9},{9,1},{17,25},{25,17},{2,10},{10... | collective-permute-start | bytes 2211848 | tf_op jit(solution)/shard_map/ppermute | solution.py:123
  135.1 23.7 %collective-permute-start.26 = (bf16[2,96,1920]{2,1,0:T(8,128)(2,1)S(1)}, bf16[2,96,1920]{2,1,0:T(8,128)(2,1)}, u32[]{:S(2)}, u32[]{:S(2)}) collective-permute-start(bf16[2,96,1920]{2,1,0:T(8,128)(2,1)S(1)} %collective-permute-done.22.refs_11_), channel_id=1, source_target_pairs={{0,8},{8,0},{16,24},{24,16},{1,9},{9,1},{17,25},{25,17},{2,10},{10... | collective-permute-start | bytes 2211848 | tf_op jit(solution)/shard_map/ppermute | solution.py:123
  209.8 40.3 %collective-permute-start.35 = (bf16[8,192,768]{2,1,0:T(8,128)(2,1)}, bf16[8,192,768]{2,1,0:T(8,128)(2,1)}, u32[]{:S(2)}, u32[]{:S(2)}) collective-permute-start(bf16[8,192,768]{2,1,0:T(8,128)(2,1)} %get-tuple-element.90), channel_id=1, source_target_pairs={{0,8},{8,0},{16,24},{24,16},{1,9},{9,1},{17,25},{25,17},{2,10},{10... | collective-permute-start | bytes 7077896 | tf_op jit(solution)/shard_map/ppermute | solution.py:123
  222.3 24.0 %collective-permute-start.36 = (bf16[8,48,1920]{2,1,0:T(8,128)(2,1)}, bf16[8,48,1920]{2,1,0:T(8,128)(2,1)}, u32[]{:S(2)}, u32[]{:S(2)}) collective-permute-start(bf16[8,48,1920]{2,1,0:T(8,128)(2,1)} %get-tuple-element.99), channel_id=1, source_target_pairs={{0,8},{8,0},{16,24},{24,16},{1,9},{9,1},{17,25},{25,17},{2,10},{10... | collective-permute-start | bytes 4423688 | tf_op jit(solution)/shard_map/ppermute | solution.py:123
  222.5 23.7 %all-to-all-start.3 = ((bf16[4,256,768]{2,1,0:T(8,128)(2,1)}), bf16[4,256,768]{2,1,0:T(8,128)(2,1)S(1)}, u32[]{:S(2)}, u32[]{:S(2)}) async-start(bf16[4,256,768]{2,1,0:T(8,128)(2,1)} %bitcast.87), calls=%async_computation.3 | async-start | bytes 3145728 | tf_op jit(solution)/shard_map/all_to_all | solution.py:595
  226.4 43.0 %collective-permute-start.37 = (bf16[8,48,1920]{2,1,0:T(8,128)(2,1)}, bf16[8,48,1920]{2,1,0:T(8,128)(2,1)}, u32[]{:S(2)}, u32[]{:S(2)}) collective-permute-start(bf16[8,48,1920]{2,1,0:T(8,128)(2,1)} %get-tuple-element.100), channel_id=1, source_target_pairs={{0,8},{8,0},{16,24},{24,16},{1,9},{9,1},{17,25},{25,17},{2,10},{10... | collective-permute-start | bytes 4423688 | tf_op jit(solution)/shard_map/ppermute | solution.py:123
  249.7 47.9 %collective-permute-start.40 = (bf16[8,48,1920]{2,1,0:T(8,128)(2,1)}, bf16[8,48,1920]{2,1,0:T(8,128)(2,1)}, u32[]{:S(2)}, u32[]{:S(2)}) collective-permute-start(bf16[8,48,1920]{2,1,0:T(8,128)(2,1)} %add_convert_fusion), channel_id=1, source_target_pairs={{0,16},{8,24},{16,0},{24,8},{1,17},{9,25},{17,1},{25,9},{2,18},{10... | collective-permute-start | bytes 4423688 | tf_op jit(solution)/shard_map/ppermute | solution.py:123
  251.7 49.2 %collective-permute-start.38 = (bf16[4,192,768]{2,1,0:T(8,128)(2,1)S(1)}, bf16[4,192,768]{2,1,0:T(8,128)(2,1)}, u32[]{:S(2)}, u32[]{:S(2)}) collective-permute-start(bf16[4,192,768]{2,1,0:T(8,128)(2,1)S(1)} %add_convert_fusion.1), channel_id=1, source_target_pairs={{0,1},{1,0},{2,3},{3,2},{4,5},{5,4},{6,7},{7,6},{8,9},{9,8},{10,11... | collective-permute-start | bytes 3538952 | tf_op jit(solution)/shard_map/ppermute | solution.py:123
  297.6 27.5 %collective-permute-start.41 = (bf16[8,48,1536]{2,1,0:T(8,128)(2,1)}, bf16[8,48,1536]{2,1,0:T(8,128)(2,1)}, u32[]{:S(2)}, u32[]{:S(2)}) collective-permute-start(bf16[8,48,1536]{2,1,0:T(8,128)(2,1)} %get-tuple-element.115), channel_id=1, source_target_pairs={{0,8},{8,0},{16,24},{24,16},{1,9},{9,1},{17,25},{25,17},{2,10},{10... | collective-permute-start | bytes 3538952 | tf_op jit(solution)/shard_map/ppermute | solution.py:123
  300.3 21.2 %collective-permute-start.53 = (bf16[4,48,1920]{2,1,0:T(8,128)(2,1)}, bf16[4,48,1920]{2,1,0:T(8,128)(2,1)}, u32[]{:S(2)}, u32[]{:S(2)}) collective-permute-start(bf16[4,48,1920]{2,1,0:T(8,128)(2,1)} %add_convert_fusion.2), channel_id=1, source_target_pairs={{0,1},{1,0},{2,3},{3,2},{4,5},{5,4},{6,7},{7,6},{8,9},{9,8},{10,11... | collective-permute-start | bytes 2211848 | tf_op jit(solution)/shard_map/ppermute | solution.py:123
  303.4 35.4 %collective-permute-start.39 = (bf16[2,192,768]{2,1,0:T(8,128)(2,1)}, bf16[2,192,768]{2,1,0:T(8,128)(2,1)}, u32[]{:S(2)}, u32[]{:S(2)}) collective-permute-start(bf16[2,192,768]{2,1,0:T(8,128)(2,1)} %add_convert_fusion.4), channel_id=1, source_target_pairs={{0,2},{1,3},{2,0},{3,1},{4,6},{5,7},{6,4},{7,5},{8,10},{9,11},{10,... | collective-permute-start | bytes 1769480 | tf_op jit(solution)/shard_map/ppermute | solution.py:123
  326.3 34.3 %collective-permute-start.42 = (bf16[4,48,1536]{2,1,0:T(8,128)(2,1)S(1)}, bf16[4,48,1536]{2,1,0:T(8,128)(2,1)}, u32[]{:S(2)}, u32[]{:S(2)}) collective-permute-start(bf16[4,48,1536]{2,1,0:T(8,128)(2,1)S(1)} %add_convert_fusion.3), channel_id=1, source_target_pairs={{0,1},{1,0},{2,3},{3,2},{4,5},{5,4},{6,7},{7,6},{8,9},{9,8},{10,11... | collective-permute-start | bytes 1769480 | tf_op jit(solution)/shard_map/ppermute | solution.py:123
  336.5 27.9 %collective-permute-start.55 = (bf16[1,48,1920]{2,1,0:T(8,128)(2,1)}, bf16[1,48,1920]{2,1,0:T(8,128)(2,1)S(1)}, u32[]{:S(2)}, u32[]{:S(2)}) collective-permute-start(bf16[1,48,1920]{2,1,0:T(8,128)(2,1)} %add_convert_fusion.12), channel_id=1, source_target_pairs={{0,4},{1,5},{2,6},{3,7},{4,0},{5,1},{6,2},{7,3},{8,12},{9,13},{10,... | collective-permute-start | bytes 552968 | tf_op jit(solution)/shard_map/ppermute | solution.py:123
  340.8 35.3 %collective-permute-start.58 = (bf16[1,192,768]{2,1,0:T(8,128)(2,1)}, bf16[1,192,768]{2,1,0:T(8,128)(2,1)}, u32[]{:S(2)}, u32[]{:S(2)}) collective-permute-start(bf16[1,192,768]{2,1,0:T(8,128)(2,1)} %add_convert_fusion.9), channel_id=1, source_target_pairs={{0,4},{1,5},{2,6},{3,7},{4,0},{5,1},{6,2},{7,3},{8,12},{9,13},{10,... | collective-permute-start | bytes 884744 | tf_op jit(solution)/shard_map/ppermute | solution.py:123
  356.0 63.3 %all-to-all-start.4 = ((bf16[4,256,768]{2,1,0:T(8,128)(2,1)}), bf16[4,256,768]{2,1,0:T(8,128)(2,1)}, u32[]{:S(2)}, u32[]{:S(2)}) async-start(bf16[4,256,768]{2,1,0:T(8,128)(2,1)} %bitcast.86), calls=%async_computation.4 | async-start | bytes 3145728 | tf_op jit(solution)/shard_map/all_to_all | solution.py:595
  364.2 30.9 %collective-permute-start.47 = (bf16[8,64,768]{2,1,0:T(8,128)(2,1)}, bf16[8,64,768]{2,1,0:T(8,128)(2,1)}, u32[]{:S(2)}, u32[]{:S(2)}) collective-permute-start(bf16[8,64,768]{2,1,0:T(8,128)(2,1)} %get-tuple-element.122), channel_id=1, source_target_pairs={{0,8},{8,0},{16,24},{24,16},{1,9},{9,1},{17,25},{25,17},{2,10},{10... | collective-permute-start | bytes 2359304 | tf_op jit(solution)/shard_map/ppermute | solution.py:123
  366.7 18.4 %collective-permute-start.56 = (bf16[48,1920]{1,0:T(8,128)(2,1)S(1)}, bf16[48,1920]{1,0:T(8,128)(2,1)S(1)}, u32[]{:S(2)}, u32[]{:S(2)}) collective-permute-start(bf16[48,1920]{1,0:T(8,128)(2,1)S(1)} %bitcast.88), channel_id=1, source_target_pairs={{0,16},{8,24},{16,0},{24,8},{1,17},{9,25},{17,1},{25,9},{2,18},{10... | collective-permute-start | bytes 552968 | tf_op jit(solution)/shard_map/ppermute | solution.py:123
  373.9 13.6 %collective-permute-start.44 = (bf16[1,48,1536]{2,1,0:T(8,128)(2,1)}, bf16[1,48,1536]{2,1,0:T(8,128)(2,1)}, u32[]{:S(2)}, u32[]{:S(2)}) collective-permute-start(bf16[1,48,1536]{2,1,0:T(8,128)(2,1)} %add_convert_fusion.14), channel_id=1, source_target_pairs={{0,4},{1,5},{2,6},{3,7},{4,0},{5,1},{6,2},{7,3},{8,12},{9,13},{10,... | collective-permute-start | bytes 442376 | tf_op jit(solution)/shard_map/ppermute | solution.py:123
  377.6 13.4 %collective-permute-start.59 = (bf16[192,768]{1,0:T(8,128)(2,1)S(1)}, bf16[192,768]{1,0:T(8,128)(2,1)}, u32[]{:S(2)}, u32[]{:S(2)}) collective-permute-start(bf16[192,768]{1,0:T(8,128)(2,1)S(1)} %fusion.1), channel_id=1, source_target_pairs={{0,16},{8,24},{16,0},{24,8},{1,17},{9,25},{17,1},{25,9},{2,18},{10... | collective-permute-start | bytes 884744 | tf_op jit(solution)/shard_map/ppermute | solution.py:123
  392.0 32.4 %collective-permute-start.60 = (f32[192,768]{1,0:T(8,128)S(1)}, f32[192,768]{1,0:T(8,128)S(1)}, u32[]{:S(2)}, u32[]{:S(2)}) collective-permute-start(f32[192,768]{1,0:T(8,128)S(1)} %convert_add_fusion), channel_id=1, source_target_pairs={{0,8},{8,0},{16,24},{24,16},{1,9},{9,1},{17,25},{25,17},{2,10},{10... | collective-permute-start | bytes 1769480 | tf_op jit(solution)/shard_map/ppermute | solution.py:123
  395.1 15.7 %collective-permute-start.46 = (f32[48,1536]{1,0:T(8,128)S(1)}, f32[48,1536]{1,0:T(8,128)S(1)}, u32[]{:S(2)}, u32[]{:S(2)}) collective-permute-start(f32[48,1536]{1,0:T(8,128)S(1)} %convert_add_fusion.1), channel_id=1, source_target_pairs={{0,8},{8,0},{16,24},{24,16},{1,9},{9,1},{17,25},{25,17},{2,10},{10... | collective-permute-start | bytes 884744 | tf_op jit(solution)/shard_map/ppermute | solution.py:123
  (57 other events, 531.1 us)

commit v3 on v2

--- a/solution.py
+++ b/solution.py
@@ -691,8 +691,6 @@
     result, active, dinner, low, db2, db, dfirst, dattended, sums, dinner_vec = ffn(
         at, x_rows, grads_in, ffn_vecs, inner_vec, atts, plan_b, pieces_b, plan_c, pieces_c, shard
     )
-    layer_out = to_tokens(result)
-
     backs = []
 
     def back(call, gate):
@@ -714,13 +712,14 @@
         outer_parts.append(swap(outer_x, "fsdp", 1))
         inner_parts = [inner_kept, swap(inner_core, "seq", 1)]
         inner_y = fold([inner_side, swap(inner_both, "seq", 1)]).astype(BF)
-        gate, _ = lax.optimization_barrier((gate, (backs[0], inner_y, inner_parts)))
+        gate, shown, _ = lax.optimization_barrier((gate, result, (backs[0], inner_y, inner_parts)))
+        layer_out = to_tokens(shown)
         backs.append(back(1, gate))
         inner_parts.append(swap(inner_y, "seq", 2))
         both = [jnp.concatenate([one[j] for one in backs], axis=1) for j in range(3)]
         first_keep, first_send = grad_wide(at, masks, x_rows, both)
         outer_z, outer_parts = halve(outer_parts)
-        gate, _ = lax.optimization_barrier((gate, (first_keep, outer_z)))
+        gate, layer_out, _ = lax.optimization_barrier((gate, layer_out, (first_keep, outer_z)))
         backs.append(back(2, gate))
         outer_parts.append(swap(outer_z, "fsdp", 2))
         first_parts = [first_keep, swap(first_send, "seq", 1)]
@@ -781,6 +780,7 @@
         parts = [value for one in backs for value in one[:3]]
         moved = input_gradient(at, dfirst, parts, plan_a, pieces_a, shard)
         input_grad = to_tokens(moved).astype(F32)
+        layer_out = to_tokens(result)
         three = [jnp.concatenate([one[j] for one in backs], axis=1) for j in range(3)]
         att = jnp.concatenate(atts, axis=1)
         lefts = [x_rows, x_rows, x_rows, att, low]

time: 440 us -> 422 us (0.959)
  waiting for transfers between devices: 117 us -> 100 us
    all_to_all x2, waiting for transfers between devices: 19.3 us -> 0.01 us  [to_tokens(): lax.all_to_all(value.reshape(groups, local_len, width), 'seq', 0, 0, tile...]
  transfers between devices with their start and end apart: 66 -> 66, of which waited for: 21 -> 21; matrix products, arithmetic and copies ran while one was open for 14% -> 14% of each run, Pallas kernels for 29% -> 30%
where the time goes in v3:
time: 422 us; the launch traced here: 417 us
  Pallas kernels  176 us (42%)
  waiting for transfers between devices  100 us (24%)
  starting transfers between devices  70 us (17%)
  other arithmetic  50.1 us (12%)
  local copies, waits for them, and re-layouts  18.9 us (4%)
    ppermute x61, waiting for transfers between devices, swap(): return lax.ppermute(value, axis, [(i, i ^ mask) for i in range(size)])  100 us
    ppermute x61, starting transfers between devices, swap(): return lax.ppermute(value, axis, [(i, i ^ mask) for i in range(size)])  49.2 us
    pallas_call x3, Pallas kernels, attend_back(): pl.pallas_call(bwd_kernel, grid=(n,), in_specs=[pl.BlockSpec((rows, 1), l...  49 us
    pallas_call x1, Pallas kernels, ffn(): pl.pallas_call(lambda *refs: ffn_kernel((inner_plan, outer_plan, len(atts...  38 us
    pallas_call x3, Pallas kernels, attend(): pl.pallas_call(fwd_kernel, grid=(n,), in_specs=[pl.BlockSpec((rows, 1), l...  34.5 us
    convert_element_type x12, other arithmetic, halve(): fold([part[half:] for part in parts]).astype(BF)  21.1 us
    all_to_all x3, starting transfers between devices, to_sequences(): lax.all_to_all(value.reshape((groups, local_len) + value.shape[3:]), 'seq...  12.5 us
    pallas_call x1, Pallas kernels, grad_inner(): pl.pallas_call(lambda at_ref, low_ref, din_ref, *refs: grad_inner_kernel(...  12.3 us
  transfers between devices with their start and end apart: 66, of which 21 were waited for; matrix products, arithmetic and copies ran while one was open for 14% of the time, Pallas kernels for 30%

profile of v3, /device:TPU:0, one launch (start us, length us, event | category | flops | bytes accessed | tf_op | source)
XLA Modules:
  0.0 417.1 jit_solution(13693288085268606658)
XLA Ops:
  2.0 4.3 %all-to-all-start.2 = ((s32[4,1,256]{2,1,0:T(1,128)}), s32[4,1,256]{2,1,0:T(1,128)S(1)}, u32[]{:S(2)}, u32[]{:S(2)}) async-start(s32[4,1,256]{2,1,0:T(1,128)} %all_to_all.20), calls=%async_computation.2 | async-start | bytes 8192 | tf_op jit(solution)/shard_map/all_to_all | solution.py:592
  8.0 3.1 collective-permute-start
  14.5 11.9 %collective-permute-done.3 = bf16[1,96,1152]{2,1,0:T(8,128)(2,1)S(1)} collective-permute-done((bf16[1,96,1152]{2,1,0:T(8,128)(2,1)S(1)}, bf16[1,96,1152]{2,1,0:T(8,128)(2,1)S(1)}, u32[]{:S(2)}, u32[]{:S(2)}) %collective-permute-start.3) | collective-permute-done | bytes 221216 | tf_op jit(solution)/shard_map/ppermute | solution.py:123
  28.9 9.0 %collective-permute-done.4.refs_4_.refs_12_ = bf16[2,96,1152]{2,1,0:T(8,128)(2,1)S(1)} collective-permute-done((bf16[2,96,1152]{2,1,0:T(8,128)(2,1)S(1)}, bf16[2,96,1152]{2,1,0:T(8,128)(2,1)S(1)}, u32[]{:S(2)}, u32[]{:S(2)}) %collective-permute-start.4) | collective-permute-done | bytes 442400 | tf_op jit(solution)/shard_map/ppermute | solution.py:123
  41.9 5.2 %collective-permute-done.5 = bf16[1,96,768]{2,1,0:T(8,128)(2,1)S(1)} collective-permute-done((bf16[1,96,768]{2,1,0:T(8,128)(2,1)S(1)}, bf16[1,96,768]{2,1,0:T(8,128)(2,1)S(1)}, u32[]{:S(2)}, u32[]{:S(2)}) %collective-permute-start.5) | collective-permute-done | bytes 147488 | tf_op jit(solution)/shard_map/ppermute | solution.py:123
  47.1 3.6 all-to-all-start
  55.5 2.0 collective-permute-start.16
  57.6 8.6 %collective-permute-done.14 = bf16[1,96,1920]{2,1,0:T(8,128)(2,1)S(1)} collective-permute-done((bf16[1,96,1920]{2,1,0:T(8,128)(2,1)}, bf16[1,96,1920]{2,1,0:T(8,128)(2,1)S(1)}, u32[]{:S(2)}, u32[]{:S(2)}) %collective-permute-start.14) | collective-permute-done | bytes 368672 | tf_op jit(solution)/shard_map/ppermute | solution.py:123
  70.2 6.8 %collective-permute-done.16.refs_20_ = bf16[2,96,768]{2,1,0:T(8,128)(2,1)S(1)} collective-permute-done((bf16[2,96,768]{2,1,0:T(8,128)(2,1)}, bf16[2,96,768]{2,1,0:T(8,128)(2,1)S(1)}, u32[]{:S(2)}, u32[]{:S(2)}) %collective-permute-start.16) | collective-permute-done | bytes 294944 | tf_op jit(solution)/shard_map/ppermute | solution.py:123
  77.0 3.2 collective-permute-start.18
  81.9 3.2 collective-permute-done.13.refs_18_
  87.5 4.6 %all-to-all-start.1 = ((bf16[4,256,768]{2,1,0:T(8,128)(2,1)}), bf16[4,256,768]{2,1,0:T(8,128)(2,1)}, u32[]{:S(2)}, u32[]{:S(2)}) async-start(bf16[4,256,768]{2,1,0:T(8,128)(2,1)} %bitcast.4), calls=%async_computation.1 | async-start | bytes 3145728 | tf_op jit(solution)/shard_map/all_to_all | solution.py:592
  98.2 8.9 %project.1.q_ref.k_ref.v_ref = bf16[1024,2304]{1,0:T(8,128)(2,1)} custom-call(s32[2]{0:T(128)} %pad_add_fusion.refs_0_.at_ref, bf16[1024,768]{1,0:T(8,128)(2,1)} %bitcast.82, f32[1,2304]{1,0:T(1,128)} %fusion.11.refs_2_, bf16[2,96,1152]{2,1,0:T(8,128)(2,1)} %copy-done.12, bf16[2,96,1152]{2,1,0:T(8,128)(2,1)} %copy-done.27, ...), custom_call_target="tpu_custom_call" | custom-call | flops 3623878656 | bytes 11010048 | tf_op jit(solution)/shard_map/project/pallas_call | solution.py:209
  107.1 11.3 %collective-permute-done.17.refs_21_ = bf16[2,96,768]{2,1,0:T(8,128)(2,1)S(1)} collective-permute-done((bf16[2,96,768]{2,1,0:T(8,128)(2,1)}, bf16[2,96,768]{2,1,0:T(8,128)(2,1)S(1)}, u32[]{:S(2)}, u32[]{:S(2)}) %collective-permute-start.17) | collective-permute-done | bytes 294944 | tf_op jit(solution)/shard_map/ppermute | solution.py:123
  118.9 11.2 %attend.3 = (bf16[1024,256]{1,0:T(8,128)(2,1)}, f32[2,1024,2]{2,1,0:T(8,128)}) custom-call(s32[1024,1]{1,0:T(8,128)} %copy.63.doc_ref, bf16[1024,2304]{1,0:T(8,128)(2,1)} %project.1.q_ref.k_ref.v_ref, bf16[1024,2304]{1,0:T(8,128)(2,1)} %project.1.q_ref.k_ref.v_ref, bf16[1024,2304]{1,0:T(8,128)(2,1)} %project.1.q_ref.k_ref.v_ref), custom_call_target="tpu_custom_call" | custom-call | flops 4294967296 | bytes 2097152 | tf_op jit(solution)/shard_map/attend/pallas_call | solution.py:47
  131.4 3.8 collective-permute-done.22.refs_11_
  135.2 11.5 %attend.4 = (bf16[1024,256]{1,0:T(8,128)(2,1)}, f32[2,1024,2]{2,1,0:T(8,128)}) custom-call(s32[1024,1]{1,0:T(8,128)} %copy.63.doc_ref, bf16[1024,2304]{1,0:T(8,128)(2,1)} %project.1.q_ref.k_ref.v_ref, bf16[1024,2304]{1,0:T(8,128)(2,1)} %project.1.q_ref.k_ref.v_ref, bf16[1024,2304]{1,0:T(8,128)(2,1)} %project.1.q_ref.k_ref.v_ref), custom_call_target="tpu_custom_call" | custom-call | flops 4294967296 | bytes 2097152 | tf_op jit(solution)/shard_map/attend/pallas_call | solution.py:47
  147.1 11.8 %attend.5 = (bf16[1024,256]{1,0:T(8,128)(2,1)}, f32[2,1024,2]{2,1,0:T(8,128)}) custom-call(s32[1024,1]{1,0:T(8,128)} %copy.63.doc_ref, bf16[1024,2304]{1,0:T(8,128)(2,1)} %project.1.q_ref.k_ref.v_ref, bf16[1024,2304]{1,0:T(8,128)(2,1)} %project.1.q_ref.k_ref.v_ref, bf16[1024,2304]{1,0:T(8,128)(2,1)} %project.1.q_ref.k_ref.v_ref), custom_call_target="tpu_custom_call" | custom-call | flops 4294967296 | bytes 2097152 | tf_op jit(solution)/shard_map/attend/pallas_call | solution.py:47
  159.6 38.0 %ffn.1 = (bf16[1024,768]{1,0:T(8,128)(2,1)}, bf16[1024,3072]{1,0:T(8,128)(2,1)}, bf16[1024,3072]{1,0:T(8,128)(2,1)}, bf16[1024,768]{1,0:T(8,128)(2,1)}, bf16[102...) custom-call(s32[2]{0:T(128)} %pad_add_fusion.refs_0_.at_ref, ...), custom_call_target="tpu_custom_call" | custom-call | flops 21743271936 | bytes 28311552 | tf_op jit(solution)/shard_map/ffn/pallas_call | solution.py:335
  197.6 12.3 %grad_outer.1 = (bf16[8,192,768]{2,1,0:T(8,128)(2,1)}, bf16[8,192,768]{2,1,0:T(8,128)(2,1)}) custom-call(s32[2]{0:T(128)} %pad_add_fusion.refs_0_.at_ref, bf16[1024,3072]{1,0:T(8,128)(2,1)} %get-tuple-element.83.refs_1_, bf16[1024,768]{1,0:T(8,128)(2,1)} %get-tuple-element.84.refs_2_), custom_call_target="tpu_custom_call" | custom-call | flops 4831838208 | bytes 12582912 | tf_op jit(solution)/shard_map/grad_outer/pallas_call | solution.py:488
  210.1 12.3 %grad_inner.1 = (bf16[8,48,1920]{2,1,0:T(8,128)(2,1)}, bf16[8,48,1920]{2,1,0:T(8,128)(2,1)}, bf16[8,48,1920]{2,1,0:T(8,128)(2,1)}, bf16[8,48,1920]{2,1,0:T(8,128)(2,1)}) custom-call(s32[2]{0:T(128)} %pad_add_fusion.refs_0_.at_ref, bf16[1024,768]{1,0:T(8,128)(2,1)} %get-tuple-element.86.low_ref, bf16[1024,3072]{1,0:T(8,128)(2,1)} %get-tuple-element.87.din_ref, ...), custom_call_target="tpu_custom_call" | custom-call | flops 6039797760 | bytes 12582912 | tf_op jit(solution)/shard_map/grad_inner/pallas_call | solution.py:450
  223.2 2.9 collective-permute-done.36
  226.1 3.4 add_convert_fusion
  233.2 16.3 %attend_back.3 = (bf16[1024,256]{1,0:T(8,128)(2,1)}, bf16[1024,256]{1,0:T(8,128)(2,1)}, bf16[1024,256]{1,0:T(8,128)(2,1)}, f32[1,256]{1,0:T(1,128)}, f32[1,256]{1,0:T(1,128)}) custom-call(s32[1024,1]{1,0:T(8,128)} %copy.63.doc_ref, bf16[1024,2304]{1,0:T(8,128)(2,1)} %project.1.q_ref.k_ref.v_ref, bf16[1024,2304]{1,0:T(8,128)(2,1)} %project.1.q_ref.k_ref.v_ref, ...), custom_call_target="tpu_custom_call" | custom-call | flops 6442450944 | bytes 4194304 | tf_op jit(solution)/shard_map/attend_back/pallas_call | solution.py:105
  249.4 3.8 all-to-all-start.3
  253.3 16.2 %attend_back.4 = (bf16[1024,256]{1,0:T(8,128)(2,1)}, bf16[1024,256]{1,0:T(8,128)(2,1)}, bf16[1024,256]{1,0:T(8,128)(2,1)}, f32[1,256]{1,0:T(1,128)}, f32[1,256]{1,0:T(1,128)}) custom-call(s32[1024,1]{1,0:T(8,128)} %copy.63.doc_ref, bf16[1024,2304]{1,0:T(8,128)(2,1)} %project.1.q_ref.k_ref.v_ref, bf16[1024,2304]{1,0:T(8,128)(2,1)} %project.1.q_ref.k_ref.v_ref, ...), custom_call_target="tpu_custom_call" | custom-call | flops 6442450944 | bytes 4194304 | tf_op jit(solution)/shard_map/attend_back/pallas_call | solution.py:105
  269.6 2.8 pad_maximum_fusion
  273.5 6.5 %grad_wide.2 = (bf16[8,48,1536]{2,1,0:T(8,128)(2,1)}, bf16[8,48,1536]{2,1,0:T(8,128)(2,1)}) custom-call(s32[2]{0:T(128)} %pad_add_fusion.refs_0_.at_ref, bf16[1024,768]{1,0:T(8,128)(2,1)} %bitcast.84, bf16[1024,512]{1,0:T(8,128)(2,1)} %get-tuple-element.157.refs_1_, bf16[1024,512]{1,0:T(8,128)(2,1)} %get-tuple-element.158.refs_2_, ...), custom_call_target="tpu_custom_call" | custom-call | flops 2415919104 | bytes 5505024 | tf_op jit(solution)/shard_map/grad_wide/pallas_call | solution.py:401
  280.4 2.7 add_convert_fusion.2
  283.7 2.5 add_convert_fusion.4
  286.2 16.6 %attend_back.5 = (bf16[1024,256]{1,0:T(8,128)(2,1)}, bf16[1024,256]{1,0:T(8,128)(2,1)}, bf16[1024,256]{1,0:T(8,128)(2,1)}, f32[1,256]{1,0:T(1,128)}, f32[1,256]{1,0:T(1,128)}) custom-call(s32[1024,1]{1,0:T(8,128)} %copy.63.doc_ref, bf16[1024,2304]{1,0:T(8,128)(2,1)} %project.1.q_ref.k_ref.v_ref, bf16[1024,2304]{1,0:T(8,128)(2,1)} %project.1.q_ref.k_ref.v_ref, ...), custom_call_target="tpu_custom_call" | custom-call | flops 6442450944 | bytes 4194304 | tf_op jit(solution)/shard_map/attend_back/pallas_call | solution.py:105
  305.8 2.1 collective-permute-start.54
  311.3 4.8 %collective-permute-done.54 = bf16[2,48,1920]{2,1,0:T(8,128)(2,1)S(1)} collective-permute-done((bf16[2,48,1920]{2,1,0:T(8,128)(2,1)S(1)}, bf16[2,48,1920]{2,1,0:T(8,128)(2,1)S(1)}, u32[]{:S(2)}, u32[]{:S(2)}) %collective-permute-start.54) | collective-permute-done | bytes 368672 | tf_op jit(solution)/shard_map/ppermute | solution.py:123
  318.9 2.2 collective-permute-start.55
  321.1 2.1 add_convert_fusion.9
  323.9 4.8 %grad_wide.3 = (bf16[8,64,768]{2,1,0:T(8,128)(2,1)}, bf16[8,64,768]{2,1,0:T(8,128)(2,1)}) custom-call(s32[2]{0:T(128)} %pad_add_fusion.refs_0_.at_ref, bf16[8,16,256]{2,1,0:T(8,128)(2,1)} %fusion.9.refs_0_, bf16[1024,768]{1,0:T(8,128)(2,1)} %bitcast.85, bf16[1024,256]{1,0:T(8,128)(2,1)} %get-tuple-element.121.refs_2_.refs_8_, ...), custom_call_target="tpu_custom_call" | custom-call | flops 1207959552 | bytes 2752512 | tf_op jit(solution)/shard_map/grad_wide/pallas_call | solution.py:401
  328.7 9.7 %input_gradient.1 = bf16[1024,768]{1,0:T(8,128)(2,1)} custom-call(s32[2]{0:T(128)} %pad_add_fusion.refs_0_.at_ref, f32[1024,768]{1,0:T(8,128)} %get-tuple-element.125.refs_1_, bf16[1024,256]{1,0:T(8,128)(2,1)} %get-tuple-element.94.refs_2_, bf16[1024,256]{1,0:T(8,128)(2,1)} %get-tuple-element.95.refs_3_, bf16[1024,256]{1,0:T(8,128)(2,1)} %get-tuple-element.96.refs_4_, ...), custom_call_target="tpu_custom_call" | custom-call | flops 3623878656 | bytes 11010048 | tf_op jit(solution)/shard_map/input_gradient/pallas_call | solution.py:530
  338.4 4.5 %all-to-all-start.4 = ((bf16[4,256,768]{2,1,0:T(8,128)(2,1)}), bf16[4,256,768]{2,1,0:T(8,128)(2,1)}, u32[]{:S(2)}, u32[]{:S(2)}) async-start(bf16[4,256,768]{2,1,0:T(8,128)(2,1)} %bitcast.86), calls=%async_computation.4 | async-start | bytes 3145728 | tf_op jit(solution)/shard_map/all_to_all | solution.py:595
  350.9 3.5 collective-permute-done.43
  356.3 2.2 collective-permute-start.44
  361.6 5.8 %collective-permute-done.56 = bf16[48,1920]{1,0:T(8,128)(2,1)S(1)} collective-permute-done((bf16[48,1920]{1,0:T(8,128)(2,1)S(1)}, bf16[48,1920]{1,0:T(8,128)(2,1)S(1)}, u32[]{:S(2)}, u32[]{:S(2)}) %collective-permute-start.56) | collective-permute-done | bytes 184352 | tf_op jit(solution)/shard_map/ppermute | solution.py:123
  371.2 2.1 collective-permute-done.59
  374.4 3.0 collective-permute-done.45
  382.1 8.0 %collective-permute-done.48 = bf16[4,64,768]{2,1,0:T(8,128)(2,1)S(1)} collective-permute-done((bf16[4,64,768]{2,1,0:T(8,128)(2,1)S(1)}, bf16[4,64,768]{2,1,0:T(8,128)(2,1)S(1)}, u32[]{:S(2)}, u32[]{:S(2)}) %collective-permute-start.48) | collective-permute-done | bytes 393248 | tf_op jit(solution)/shard_map/ppermute | solution.py:123
  393.2 4.6 %collective-permute-done.49 = bf16[2,64,768]{2,1,0:T(8,128)(2,1)S(1)} collective-permute-done((bf16[2,64,768]{2,1,0:T(8,128)(2,1)S(1)}, bf16[2,64,768]{2,1,0:T(8,128)(2,1)S(1)}, u32[]{:S(2)}, u32[]{:S(2)}) %collective-permute-start.49) | collective-permute-done | bytes 196640 | tf_op jit(solution)/shard_map/ppermute | solution.py:123
  399.4 2.2 collective-permute-start.50
  401.7 3.3 convert.50
  407.8 3.2 collective-permute-done.51
  (269 shorter events, 86.9 us)
Async XLA Ops:
  2.0 45.1 %all-to-all-start.2 = ((s32[4,1,256]{2,1,0:T(1,128)}), s32[4,1,256]{2,1,0:T(1,128)S(1)}, u32[]{:S(2)}, u32[]{:S(2)}) async-start(s32[4,1,256]{2,1,0:T(1,128)} %all_to_all.20), calls=%async_computation.2 | async-start | bytes 8192 | tf_op jit(solution)/shard_map/all_to_all | solution.py:592
  8.0 32.0 %collective-permute-start = (bf16[1,12,96]{2,1,0:T(8,128)(2,1)S(1)}, bf16[1,12,96]{2,1,0:T(8,128)(2,1)S(1)}, u32[]{:S(2)}, u32[]{:S(2)}) collective-permute-start(bf16[1,12,96]{2,1,0:T(8,128)(2,1)S(1)} %bitcast.96), channel_id=1, source_target_pairs={{0,4},{1,5},{2,6},{3,7},{4,0},{5,1},{6,2},{7,3},{8,12},{9,13},{10,... | collective-permute-start | bytes 6920 | tf_op jit(solution)/shard_map/ppermute | solution.py:123
  13.2 13.2 %collective-permute-start.3 = (bf16[1,96,1152]{2,1,0:T(8,128)(2,1)S(1)}, bf16[1,96,1152]{2,1,0:T(8,128)(2,1)S(1)}, u32[]{:S(2)}, u32[]{:S(2)}) collective-permute-start(bf16[1,96,1152]{2,1,0:T(8,128)(2,1)S(1)} %maximum_select_fusion.7), channel_id=1, source_target_pairs={{0,4},{1,5},{2,6},{3,7},{4,0},{5,1},{6,2},{7,3},{8,12},{9,13},{10,... | collective-permute-start | bytes 663560 | tf_op jit(solution)/shard_map/ppermute | solution.py:123
  27.4 26.1 %collective-permute-start.6 = (bf16[2,96,1152]{2,1,0:T(8,128)(2,1)S(1)}, bf16[2,96,1152]{2,1,0:T(8,128)(2,1)}, u32[]{:S(2)}, u32[]{:S(2)}) collective-permute-start(bf16[2,96,1152]{2,1,0:T(8,128)(2,1)S(1)} %pad_maximum_fusion.4.refs_3_.refs_11_), channel_id=1, source_target_pairs={{0,1},{1,0},{2,3},{3,2},{4,5},{5,4},{6,7},{7,6},{8,9},{9,8},{10,11... | collective-permute-start | bytes 1327112 | tf_op jit(solution)/shard_map/ppermute | solution.py:123
  47.1 19.1 %collective-permute-start.14 = (bf16[1,96,1920]{2,1,0:T(8,128)(2,1)}, bf16[1,96,1920]{2,1,0:T(8,128)(2,1)S(1)}, u32[]{:S(2)}, u32[]{:S(2)}) collective-permute-start(bf16[1,96,1920]{2,1,0:T(8,128)(2,1)} %bitcast.37), channel_id=1, source_target_pairs={{0,4},{1,5},{2,6},{3,7},{4,0},{5,1},{6,2},{7,3},{8,12},{9,13},{10,... | collective-permute-start | bytes 1105928 | tf_op jit(solution)/shard_map/ppermute | solution.py:123
  47.1 39.2 %all-to-all-start = ((bf16[4,256,768]{2,1,0:T(8,128)(2,1)}), bf16[4,256,768]{2,1,0:T(8,128)(2,1)S(1)}, u32[]{:S(2)}, u32[]{:S(2)}) async-start(bf16[4,256,768]{2,1,0:T(8,128)(2,1)} %bitcast.2), calls=%async_computation | async-start | bytes 3145728 | tf_op jit(solution)/shard_map/all_to_all | solution.py:592
  53.3 16.2 %collective-permute-start.8 = (bf16[2,96,1152]{2,1,0:T(8,128)(2,1)S(1)}, bf16[2,96,1152]{2,1,0:T(8,128)(2,1)S(1)}, u32[]{:S(2)}, u32[]{:S(2)}) collective-permute-start(bf16[2,96,1152]{2,1,0:T(8,128)(2,1)S(1)} %pad_maximum_fusion.4.refs_3_.refs_11_), channel_id=1, source_target_pairs={{0,8},{8,0},{16,24},{24,16},{1,9},{9,1},{17,25},{25,17},{2,10},{10... | collective-permute-start | bytes 1327112 | tf_op jit(solution)/shard_map/ppermute | solution.py:123
  53.5 16.1 %collective-permute-start.10 = (bf16[2,96,1152]{2,1,0:T(8,128)(2,1)}, bf16[2,96,1152]{2,1,0:T(8,128)(2,1)S(1)}, u32[]{:S(2)}, u32[]{:S(2)}) collective-permute-start(bf16[2,96,1152]{2,1,0:T(8,128)(2,1)} %collective-permute-done.6.refs_5_.refs_13_), channel_id=1, source_target_pairs={{0,8},{8,0},{16,24},{24,16},{1,9},{9,1},{17,25},{25,17},{2,10},{10... | collective-permute-start | bytes 1327112 | tf_op jit(solution)/shard_map/ppermute | solution.py:123
  54.6 15.6 %collective-permute-start.27 = (bf16[2,96,768]{2,1,0:T(8,128)(2,1)}, bf16[2,96,768]{2,1,0:T(8,128)(2,1)S(1)}, u32[]{:S(2)}, u32[]{:S(2)}) collective-permute-start(bf16[2,96,768]{2,1,0:T(8,128)(2,1)} %pad_maximum_fusion.5.refs_16_), channel_id=1, source_target_pairs={{0,8},{8,0},{16,24},{24,16},{1,9},{9,1},{17,25},{25,17},{2,10},{10... | collective-permute-start | bytes 884744 | tf_op jit(solution)/shard_map/ppermute | solution.py:123
  55.5 21.5 %collective-permute-start.16 = (bf16[2,96,768]{2,1,0:T(8,128)(2,1)}, bf16[2,96,768]{2,1,0:T(8,128)(2,1)S(1)}, u32[]{:S(2)}, u32[]{:S(2)}) collective-permute-start(bf16[2,96,768]{2,1,0:T(8,128)(2,1)} %pad_maximum_fusion.5.refs_16_), channel_id=1, source_target_pairs={{0,16},{8,24},{16,0},{24,8},{1,17},{9,25},{17,1},{25,9},{2,18},{10... | collective-permute-start | bytes 884744 | tf_op jit(solution)/shard_map/ppermute | solution.py:123
  66.9 13.4 %collective-permute-start.7 = (bf16[2,96,1152]{2,1,0:T(8,128)(2,1)}, bf16[2,96,1152]{2,1,0:T(8,128)(2,1)}, u32[]{:S(2)}, u32[]{:S(2)}) collective-permute-start(bf16[2,96,1152]{2,1,0:T(8,128)(2,1)} %copy-done.27), channel_id=1, source_target_pairs={{0,1},{1,0},{2,3},{3,2},{4,5},{5,4},{6,7},{7,6},{8,9},{9,8},{10,11... | collective-permute-start | bytes 1327112 | tf_op jit(solution)/shard_map/ppermute | solution.py:123
  69.5 15.7 %collective-permute-start.9 = (bf16[2,96,1152]{2,1,0:T(8,128)(2,1)}, bf16[2,96,1152]{2,1,0:T(8,128)(2,1)S(1)}, u32[]{:S(2)}, u32[]{:S(2)}) collective-permute-start(bf16[2,96,1152]{2,1,0:T(8,128)(2,1)} %copy-done.27), channel_id=1, source_target_pairs={{0,8},{8,0},{16,24},{24,16},{1,9},{9,1},{17,25},{25,17},{2,10},{10... | collective-permute-start | bytes 1327112 | tf_op jit(solution)/shard_map/ppermute | solution.py:123
  69.6 15.5 %collective-permute-start.13 = (bf16[2,96,768]{2,1,0:T(8,128)(2,1)}, bf16[2,96,768]{2,1,0:T(8,128)(2,1)S(1)}, u32[]{:S(2)}, u32[]{:S(2)}) collective-permute-start(bf16[2,96,768]{2,1,0:T(8,128)(2,1)} %pad_maximum_fusion.5.refs_16_), channel_id=1, source_target_pairs={{0,1},{1,0},{2,3},{3,2},{4,5},{5,4},{6,7},{7,6},{8,9},{9,8},{10,11... | collective-permute-start | bytes 884744 | tf_op jit(solution)/shard_map/ppermute | solution.py:123
  70.2 14.9 %collective-permute-start.12 = (bf16[2,96,768]{2,1,0:T(8,128)(2,1)}, bf16[2,96,768]{2,1,0:T(8,128)(2,1)}, u32[]{:S(2)}, u32[]{:S(2)}) collective-permute-start(bf16[2,96,768]{2,1,0:T(8,128)(2,1)} %pad_maximum_fusion.5.refs_16_), channel_id=1, source_target_pairs={{0,2},{1,3},{2,0},{3,1},{4,6},{5,7},{6,4},{7,5},{8,10},{9,11},{10,... | collective-permute-start | bytes 884744 | tf_op jit(solution)/shard_map/ppermute | solution.py:123
  77.0 19.6 %collective-permute-start.18 = (bf16[2,96,1920]{2,1,0:T(8,128)(2,1)S(1)}, bf16[2,96,1920]{2,1,0:T(8,128)(2,1)}, u32[]{:S(2)}, u32[]{:S(2)}) collective-permute-start(bf16[2,96,1920]{2,1,0:T(8,128)(2,1)S(1)} %pad_maximum_fusion.3.refs_8_), channel_id=1, source_target_pairs={{0,2},{1,3},{2,0},{3,1},{4,6},{5,7},{6,4},{7,5},{8,10},{9,11},{10,... | collective-permute-start | bytes 2211848 | tf_op jit(solution)/shard_map/ppermute | solution.py:123
  80.3 15.9 %collective-permute-start.11 = (bf16[2,96,1152]{2,1,0:T(8,128)(2,1)}, bf16[2,96,1152]{2,1,0:T(8,128)(2,1)}, u32[]{:S(2)}, u32[]{:S(2)}) collective-permute-start(bf16[2,96,1152]{2,1,0:T(8,128)(2,1)} %collective-permute-done.7.refs_6_.refs_14_), channel_id=1, source_target_pairs={{0,8},{8,0},{16,24},{24,16},{1,9},{9,1},{17,25},{25,17},{2,10},{10... | collective-permute-start | bytes 1327112 | tf_op jit(solution)/shard_map/ppermute | solution.py:123
  87.5 71.3 %all-to-all-start.1 = ((bf16[4,256,768]{2,1,0:T(8,128)(2,1)}), bf16[4,256,768]{2,1,0:T(8,128)(2,1)}, u32[]{:S(2)}, u32[]{:S(2)}) async-start(bf16[4,256,768]{2,1,0:T(8,128)(2,1)} %bitcast.4), calls=%async_computation.1 | async-start | bytes 3145728 | tf_op jit(solution)/shard_map/all_to_all | solution.py:592
  92.2 14.9 %collective-permute-start.28 = (bf16[2,96,768]{2,1,0:T(8,128)(2,1)}, bf16[2,96,768]{2,1,0:T(8,128)(2,1)S(1)}, u32[]{:S(2)}, u32[]{:S(2)}) collective-permute-start(bf16[2,96,768]{2,1,0:T(8,128)(2,1)} %collective-permute-done.12.refs_17_), channel_id=1, source_target_pairs={{0,8},{8,0},{16,24},{24,16},{1,9},{9,1},{17,25},{25,17},{2,10},{10... | collective-permute-start | bytes 884744 | tf_op jit(solution)/shard_map/ppermute | solution.py:123
  92.7 25.8 %collective-permute-start.17 = (bf16[2,96,768]{2,1,0:T(8,128)(2,1)}, bf16[2,96,768]{2,1,0:T(8,128)(2,1)S(1)}, u32[]{:S(2)}, u32[]{:S(2)}) collective-permute-start(bf16[2,96,768]{2,1,0:T(8,128)(2,1)} %collective-permute-done.12.refs_17_), channel_id=1, source_target_pairs={{0,16},{8,24},{16,0},{24,8},{1,17},{9,25},{17,1},{25,9},{2,18},{10... | collective-permute-start | bytes 884744 | tf_op jit(solution)/shard_map/ppermute | solution.py:123
  94.7 23.8 %collective-permute-start.15 = (bf16[2,96,768]{2,1,0:T(8,128)(2,1)}, bf16[2,96,768]{2,1,0:T(8,128)(2,1)S(1)}, u32[]{:S(2)}, u32[]{:S(2)}) collective-permute-start(bf16[2,96,768]{2,1,0:T(8,128)(2,1)} %collective-permute-done.12.refs_17_), channel_id=1, source_target_pairs={{0,1},{1,0},{2,3},{3,2},{4,5},{5,4},{6,7},{7,6},{8,9},{9,8},{10,11... | collective-permute-start | bytes 884744 | tf_op jit(solution)/shard_map/ppermute | solution.py:123
  96.1 34.9 %collective-permute-start.19 = (bf16[2,96,1920]{2,1,0:T(8,128)(2,1)S(1)}, bf16[2,96,1920]{2,1,0:T(8,128)(2,1)S(1)}, u32[]{:S(2)}, u32[]{:S(2)}) collective-permute-start(bf16[2,96,1920]{2,1,0:T(8,128)(2,1)S(1)} %pad_maximum_fusion.3.refs_8_), channel_id=1, source_target_pairs={{0,1},{1,0},{2,3},{3,2},{4,5},{5,4},{6,7},{7,6},{8,9},{9,8},{10,11... | collective-permute-start | bytes 2211848 | tf_op jit(solution)/shard_map/ppermute | solution.py:123
  96.7 38.5 %collective-permute-start.22 = (bf16[2,96,1920]{2,1,0:T(8,128)(2,1)}, bf16[2,96,1920]{2,1,0:T(8,128)(2,1)S(1)}, u32[]{:S(2)}, u32[]{:S(2)}) collective-permute-start(bf16[2,96,1920]{2,1,0:T(8,128)(2,1)} %collective-permute-done.18.refs_9_), channel_id=1, source_target_pairs={{0,1},{1,0},{2,3},{3,2},{4,5},{5,4},{6,7},{7,6},{8,9},{9,8},{10,11... | collective-permute-start | bytes 2211848 | tf_op jit(solution)/shard_map/ppermute | solution.py:123
  107.1 23.1 %collective-permute-start.33 = (bf16[2,96,768]{2,1,0:T(8,128)(2,1)}, bf16[2,96,768]{2,1,0:T(8,128)(2,1)S(1)}, u32[]{:S(2)}, u32[]{:S(2)}) collective-permute-start(bf16[2,96,768]{2,1,0:T(8,128)(2,1)} %collective-permute-done.20.refs_22_), channel_id=1, source_target_pairs={{0,8},{8,0},{16,24},{24,16},{1,9},{9,1},{17,25},{25,17},{2,10},{10... | collective-permute-start | bytes 884744 | tf_op jit(solution)/shard_map/ppermute | solution.py:123
  118.5 12.4 %collective-permute-start.21 = (bf16[2,96,768]{2,1,0:T(8,128)(2,1)S(1)}, bf16[2,96,768]{2,1,0:T(8,128)(2,1)}, u32[]{:S(2)}, u32[]{:S(2)}) collective-permute-start(bf16[2,96,768]{2,1,0:T(8,128)(2,1)S(1)} %collective-permute-done.15.refs_19_), channel_id=1, source_target_pairs={{0,16},{8,24},{16,0},{24,8},{1,17},{9,25},{17,1},{25,9},{2,18},{10... | collective-permute-start | bytes 884744 | tf_op jit(solution)/shard_map/ppermute | solution.py:123
  130.2 28.6 %collective-permute-start.23 = (bf16[2,96,1920]{2,1,0:T(8,128)(2,1)S(1)}, bf16[2,96,1920]{2,1,0:T(8,128)(2,1)}, u32[]{:S(2)}, u32[]{:S(2)}) collective-permute-start(bf16[2,96,1920]{2,1,0:T(8,128)(2,1)S(1)} %pad_maximum_fusion.3.refs_8_), channel_id=1, source_target_pairs={{0,8},{8,0},{16,24},{24,16},{1,9},{9,1},{17,25},{25,17},{2,10},{10... | collective-permute-start | bytes 2211848 | tf_op jit(solution)/shard_map/ppermute | solution.py:123
  130.4 16.3 %collective-permute-start.30 = (bf16[2,96,768]{2,1,0:T(8,128)(2,1)S(1)}, bf16[2,96,768]{2,1,0:T(8,128)(2,1)S(1)}, u32[]{:S(2)}, u32[]{:S(2)}) collective-permute-start(bf16[2,96,768]{2,1,0:T(8,128)(2,1)S(1)} %collective-permute-done.15.refs_19_), channel_id=1, source_target_pairs={{0,8},{8,0},{16,24},{24,16},{1,9},{9,1},{17,25},{25,17},{2,10},{10... | collective-permute-start | bytes 884744 | tf_op jit(solution)/shard_map/ppermute | solution.py:123
  130.9 28.0 %collective-permute-start.24 = (bf16[2,96,1920]{2,1,0:T(8,128)(2,1)}, bf16[2,96,1920]{2,1,0:T(8,128)(2,1)}, u32[]{:S(2)}, u32[]{:S(2)}) collective-permute-start(bf16[2,96,1920]{2,1,0:T(8,128)(2,1)} %collective-permute-done.18.refs_9_), channel_id=1, source_target_pairs={{0,8},{8,0},{16,24},{24,16},{1,9},{9,1},{17,25},{25,17},{2,10},{10... | collective-permute-start | bytes 2211848 | tf_op jit(solution)/shard_map/ppermute | solution.py:123
  131.0 27.8 %collective-permute-start.25 = (bf16[2,96,1920]{2,1,0:T(8,128)(2,1)S(1)}, bf16[2,96,1920]{2,1,0:T(8,128)(2,1)}, u32[]{:S(2)}, u32[]{:S(2)}) collective-permute-start(bf16[2,96,1920]{2,1,0:T(8,128)(2,1)S(1)} %collective-permute-done.19.refs_10_), channel_id=1, source_target_pairs={{0,8},{8,0},{16,24},{24,16},{1,9},{9,1},{17,25},{25,17},{2,10},{10... | collective-permute-start | bytes 2211848 | tf_op jit(solution)/shard_map/ppermute | solution.py:123
  135.2 23.7 %collective-permute-start.26 = (bf16[2,96,1920]{2,1,0:T(8,128)(2,1)S(1)}, bf16[2,96,1920]{2,1,0:T(8,128)(2,1)}, u32[]{:S(2)}, u32[]{:S(2)}) collective-permute-start(bf16[2,96,1920]{2,1,0:T(8,128)(2,1)S(1)} %collective-permute-done.22.refs_11_), channel_id=1, source_target_pairs={{0,8},{8,0},{16,24},{24,16},{1,9},{9,1},{17,25},{25,17},{2,10},{10... | collective-permute-start | bytes 2211848 | tf_op jit(solution)/shard_map/ppermute | solution.py:123
  146.8 12.1 %collective-permute-start.34 = (bf16[2,96,768]{2,1,0:T(8,128)(2,1)}, bf16[2,96,768]{2,1,0:T(8,128)(2,1)S(1)}, u32[]{:S(2)}, u32[]{:S(2)}) collective-permute-start(bf16[2,96,768]{2,1,0:T(8,128)(2,1)} %collective-permute-done.21.refs_23_), channel_id=1, source_target_pairs={{0,8},{8,0},{16,24},{24,16},{1,9},{9,1},{17,25},{25,17},{2,10},{10... | collective-permute-start | bytes 884744 | tf_op jit(solution)/shard_map/ppermute | solution.py:123
  209.8 20.1 %collective-permute-start.35 = (bf16[8,192,768]{2,1,0:T(8,128)(2,1)}, bf16[8,192,768]{2,1,0:T(8,128)(2,1)S(1)}, u32[]{:S(2)}, u32[]{:S(2)}) collective-permute-start(bf16[8,192,768]{2,1,0:T(8,128)(2,1)} %get-tuple-element.90), channel_id=1, source_target_pairs={{0,8},{8,0},{16,24},{24,16},{1,9},{9,1},{17,25},{25,17},{2,10},{10... | collective-permute-start | bytes 7077896 | tf_op jit(solution)/shard_map/ppermute | solution.py:123
  222.8 26.6 %collective-permute-start.37 = (bf16[8,48,1920]{2,1,0:T(8,128)(2,1)}, bf16[8,48,1920]{2,1,0:T(8,128)(2,1)}, u32[]{:S(2)}, u32[]{:S(2)}) collective-permute-start(bf16[8,48,1920]{2,1,0:T(8,128)(2,1)} %get-tuple-element.101), channel_id=1, source_target_pairs={{0,8},{8,0},{16,24},{24,16},{1,9},{9,1},{17,25},{25,17},{2,10},{10... | collective-permute-start | bytes 4423688 | tf_op jit(solution)/shard_map/ppermute | solution.py:123
  229.5 50.9 %collective-permute-start.40 = (bf16[8,48,1920]{2,1,0:T(8,128)(2,1)}, bf16[8,48,1920]{2,1,0:T(8,128)(2,1)}, u32[]{:S(2)}, u32[]{:S(2)}) collective-permute-start(bf16[8,48,1920]{2,1,0:T(8,128)(2,1)} %add_convert_fusion), channel_id=1, source_target_pairs={{0,16},{8,24},{16,0},{24,8},{1,17},{9,25},{17,1},{25,9},{2,18},{10... | collective-permute-start | bytes 4423688 | tf_op jit(solution)/shard_map/ppermute | solution.py:123
  231.7 52.0 %collective-permute-start.38 = (bf16[4,192,768]{2,1,0:T(8,128)(2,1)}, bf16[4,192,768]{2,1,0:T(8,128)(2,1)}, u32[]{:S(2)}, u32[]{:S(2)}) collective-permute-start(bf16[4,192,768]{2,1,0:T(8,128)(2,1)} %add_convert_fusion.1), channel_id=1, source_target_pairs={{0,1},{1,0},{2,3},{3,2},{4,5},{5,4},{6,7},{7,6},{8,9},{9,8},{10,11... | collective-permute-start | bytes 3538952 | tf_op jit(solution)/shard_map/ppermute | solution.py:123
  249.4 36.7 %all-to-all-start.3 = ((bf16[4,256,768]{2,1,0:T(8,128)(2,1)}), bf16[4,256,768]{2,1,0:T(8,128)(2,1)S(1)}, u32[]{:S(2)}, u32[]{:S(2)}) async-start(bf16[4,256,768]{2,1,0:T(8,128)(2,1)} %bitcast.87), calls=%async_computation.3 | async-start | bytes 3145728 | tf_op jit(solution)/shard_map/all_to_all | solution.py:595
  280.0 28.0 %collective-permute-start.41 = (bf16[8,48,1536]{2,1,0:T(8,128)(2,1)}, bf16[8,48,1536]{2,1,0:T(8,128)(2,1)}, u32[]{:S(2)}, u32[]{:S(2)}) collective-permute-start(bf16[8,48,1536]{2,1,0:T(8,128)(2,1)} %get-tuple-element.119), channel_id=1, source_target_pairs={{0,8},{8,0},{16,24},{24,16},{1,9},{9,1},{17,25},{25,17},{2,10},{10... | collective-permute-start | bytes 3538952 | tf_op jit(solution)/shard_map/ppermute | solution.py:123
  283.1 21.2 %collective-permute-start.53 = (bf16[4,48,1920]{2,1,0:T(8,128)(2,1)}, bf16[4,48,1920]{2,1,0:T(8,128)(2,1)}, u32[]{:S(2)}, u32[]{:S(2)}) collective-permute-start(bf16[4,48,1920]{2,1,0:T(8,128)(2,1)} %add_convert_fusion.2), channel_id=1, source_target_pairs={{0,1},{1,0},{2,3},{3,2},{4,5},{5,4},{6,7},{7,6},{8,9},{9,8},{10,11... | collective-permute-start | bytes 2211848 | tf_op jit(solution)/shard_map/ppermute | solution.py:123
  286.2 34.9 %collective-permute-start.39 = (bf16[2,192,768]{2,1,0:T(8,128)(2,1)}, bf16[2,192,768]{2,1,0:T(8,128)(2,1)}, u32[]{:S(2)}, u32[]{:S(2)}) collective-permute-start(bf16[2,192,768]{2,1,0:T(8,128)(2,1)} %add_convert_fusion.4), channel_id=1, source_target_pairs={{0,2},{1,3},{2,0},{3,1},{4,6},{5,7},{6,4},{7,5},{8,10},{9,11},{10,... | collective-permute-start | bytes 1769480 | tf_op jit(solution)/shard_map/ppermute | solution.py:123
  309.1 33.8 %collective-permute-start.42 = (bf16[4,48,1536]{2,1,0:T(8,128)(2,1)S(1)}, bf16[4,48,1536]{2,1,0:T(8,128)(2,1)}, u32[]{:S(2)}, u32[]{:S(2)}) collective-permute-start(bf16[4,48,1536]{2,1,0:T(8,128)(2,1)S(1)} %add_convert_fusion.3), channel_id=1, source_target_pairs={{0,1},{1,0},{2,3},{3,2},{4,5},{5,4},{6,7},{7,6},{8,9},{9,8},{10,11... | collective-permute-start | bytes 1769480 | tf_op jit(solution)/shard_map/ppermute | solution.py:123
  318.9 27.9 %collective-permute-start.55 = (bf16[1,48,1920]{2,1,0:T(8,128)(2,1)}, bf16[1,48,1920]{2,1,0:T(8,128)(2,1)S(1)}, u32[]{:S(2)}, u32[]{:S(2)}) collective-permute-start(bf16[1,48,1920]{2,1,0:T(8,128)(2,1)} %add_convert_fusion.12), channel_id=1, source_target_pairs={{0,4},{1,5},{2,6},{3,7},{4,0},{5,1},{6,2},{7,3},{8,12},{9,13},{10,... | collective-permute-start | bytes 552968 | tf_op jit(solution)/shard_map/ppermute | solution.py:123
  323.2 35.3 %collective-permute-start.58 = (bf16[1,192,768]{2,1,0:T(8,128)(2,1)}, bf16[1,192,768]{2,1,0:T(8,128)(2,1)}, u32[]{:S(2)}, u32[]{:S(2)}) collective-permute-start(bf16[1,192,768]{2,1,0:T(8,128)(2,1)} %add_convert_fusion.9), channel_id=1, source_target_pairs={{0,4},{1,5},{2,6},{3,7},{4,0},{5,1},{6,2},{7,3},{8,12},{9,13},{10,... | collective-permute-start | bytes 884744 | tf_op jit(solution)/shard_map/ppermute | solution.py:123
  338.4 63.3 %all-to-all-start.4 = ((bf16[4,256,768]{2,1,0:T(8,128)(2,1)}), bf16[4,256,768]{2,1,0:T(8,128)(2,1)}, u32[]{:S(2)}, u32[]{:S(2)}) async-start(bf16[4,256,768]{2,1,0:T(8,128)(2,1)} %bitcast.86), calls=%async_computation.4 | async-start | bytes 3145728 | tf_op jit(solution)/shard_map/all_to_all | solution.py:595
  346.6 30.9 %collective-permute-start.47 = (bf16[8,64,768]{2,1,0:T(8,128)(2,1)}, bf16[8,64,768]{2,1,0:T(8,128)(2,1)}, u32[]{:S(2)}, u32[]{:S(2)}) collective-permute-start(bf16[8,64,768]{2,1,0:T(8,128)(2,1)} %get-tuple-element.126), channel_id=1, source_target_pairs={{0,8},{8,0},{16,24},{24,16},{1,9},{9,1},{17,25},{25,17},{2,10},{10... | collective-permute-start | bytes 2359304 | tf_op jit(solution)/shard_map/ppermute | solution.py:123
  349.1 18.4 %collective-permute-start.56 = (bf16[48,1920]{1,0:T(8,128)(2,1)S(1)}, bf16[48,1920]{1,0:T(8,128)(2,1)S(1)}, u32[]{:S(2)}, u32[]{:S(2)}) collective-permute-start(bf16[48,1920]{1,0:T(8,128)(2,1)S(1)} %bitcast.88), channel_id=1, source_target_pairs={{0,16},{8,24},{16,0},{24,8},{1,17},{9,25},{17,1},{25,9},{2,18},{10... | collective-permute-start | bytes 552968 | tf_op jit(solution)/shard_map/ppermute | solution.py:123
  356.3 13.6 %collective-permute-start.44 = (bf16[1,48,1536]{2,1,0:T(8,128)(2,1)}, bf16[1,48,1536]{2,1,0:T(8,128)(2,1)}, u32[]{:S(2)}, u32[]{:S(2)}) collective-permute-start(bf16[1,48,1536]{2,1,0:T(8,128)(2,1)} %add_convert_fusion.14), channel_id=1, source_target_pairs={{0,4},{1,5},{2,6},{3,7},{4,0},{5,1},{6,2},{7,3},{8,12},{9,13},{10,... | collective-permute-start | bytes 442376 | tf_op jit(solution)/shard_map/ppermute | solution.py:123
  359.9 13.4 %collective-permute-start.59 = (bf16[192,768]{1,0:T(8,128)(2,1)S(1)}, bf16[192,768]{1,0:T(8,128)(2,1)}, u32[]{:S(2)}, u32[]{:S(2)}) collective-permute-start(bf16[192,768]{1,0:T(8,128)(2,1)S(1)} %fusion.1), channel_id=1, source_target_pairs={{0,16},{8,24},{16,0},{24,8},{1,17},{9,25},{17,1},{25,9},{2,18},{10... | collective-permute-start | bytes 884744 | tf_op jit(solution)/shard_map/ppermute | solution.py:123
  374.3 32.4 %collective-permute-start.60 = (f32[192,768]{1,0:T(8,128)S(1)}, f32[192,768]{1,0:T(8,128)S(1)}, u32[]{:S(2)}, u32[]{:S(2)}) collective-permute-start(f32[192,768]{1,0:T(8,128)S(1)} %convert_add_fusion), channel_id=1, source_target_pairs={{0,8},{8,0},{16,24},{24,16},{1,9},{9,1},{17,25},{25,17},{2,10},{10... | collective-permute-start | bytes 1769480 | tf_op jit(solution)/shard_map/ppermute | solution.py:123
  377.4 15.7 %collective-permute-start.46 = (f32[48,1536]{1,0:T(8,128)S(1)}, f32[48,1536]{1,0:T(8,128)S(1)}, u32[]{:S(2)}, u32[]{:S(2)}) collective-permute-start(f32[48,1536]{1,0:T(8,128)S(1)} %convert_add_fusion.1), channel_id=1, source_target_pairs={{0,8},{8,0},{16,24},{24,16},{1,9},{9,1},{17,25},{25,17},{2,10},{10... | collective-permute-start | bytes 884744 | tf_op jit(solution)/shard_map/ppermute | solution.py:123
  (59 other events, 525.7 us)

commit v4 on v3

--- a/solution.py
+++ b/solution.py
@@ -610,17 +610,30 @@
         jnp.concatenate([inner_weight[:, hidden // 2 :], output_weight[:, width // 2 :]], axis=1),
     )
     if aligned:
+        index = lax.axis_index("fsdp")
+
+        def join(held, bit):
+            other = swap(held, "fsdp", bit)
+            flag = (index // bit) & 1
+            held = pick(flag, jnp.stack([held, other], axis=1), jnp.stack([other, held], axis=1))
+            return held.reshape((-1,) + held.shape[2:])
+
         a_far = swap(piece_a[None], "fsdp", 4)
-        small_full = absolute(small[None], owners)
+        small_far = join(small[None], 4)
         x_rows = to_sequences(tokens).reshape(rows, width)
         doc = to_sequences(segment_ids).reshape(rows, 1)
+        a_far, small_far, doc = lax.optimization_barrier((a_far, small_far, doc))
         a_low = jnp.concatenate([piece_a[None], a_far])
         a_two = swap(a_low, "fsdp", 2)
         a_one = swap(a_low, "fsdp", 1)
+        small_two = join(small_far, 2)
+        a_two, a_one, small_two = lax.optimization_barrier((a_two, a_one, small_two))
+        small_full = join(small_two, 1)
         quarter = wide // 4
         piece_c = lax.dynamic_slice(outer_weight, (place * quarter, 0), (quarter, width))[None]
         c_far = swap(after(piece_c, a_two), "fsdp", 4)
         a_three = swap(a_two, "fsdp", 1)
+        b_far = swap(after(piece_b, a_two)[None], "fsdp", 4)
         a_mine = [a_low, a_two, a_one, a_three]
         a_other = [swap(value, "seq", 1) for value in a_mine]
         quads = [(0, 4), (2, 6), (1, 5), (3, 7)]
@@ -639,39 +652,38 @@
     qkv_vec = jnp.concatenate([vecs[0:1], jnp.zeros((1, width), F32), vecs[1:2]], axis=1)
     ffn_vecs = vecs[2:]
 
-    if aligned:
-        qkv = project(at, after(x_rows, c_far), qkv_vec, plan_a, pieces_a, shard)
-    else:
-        qkv = project(at, x_rows, qkv_vec, plan_a, pieces_a, shard)
+    qkv = project(at, x_rows, qkv_vec, plan_a, pieces_a, shard)
     pairs = width // PAIR
     calls = 3
     each = pairs // calls
     atts, logs = [], []
     if aligned:
         c_low = jnp.concatenate([piece_c, c_far])
+        b_low = jnp.concatenate([piece_b[None], b_far])
+        qkv, c_low, b_low, gout = lax.optimization_barrier((qkv, c_low, b_low, out_cotangent))
         c_two = swap(c_low, "fsdp", 2)
         c_one = swap(c_low, "fsdp", 1)
-        b_far = swap(after(piece_b, c_far)[None], "fsdp", 4)
-        qkv = after(qkv, c_two, c_one)
+        b_two = swap(b_low, "fsdp", 2)
+        b_one = swap(b_low, "fsdp", 1)
         att, log = attend(doc, qkv, 0, each)
         atts.append(att)
         logs.append(log)
+        grads_in = to_sequences(gout).reshape(rows, width)
+        qkv, c_two, c_one, _ = lax.optimization_barrier((qkv, c_two, c_one, att))
         c_three = swap(c_two, "fsdp", 1)
         c_side = [swap(c_low, "seq", 2), swap(c_two, "seq", 2)]
-        b_low = jnp.concatenate([piece_b[None], b_far])
-        qkv, _ = lax.optimization_barrier((qkv, (att, b_low, c_three, c_side)))
         att, log = attend(doc, qkv, each, each)
         atts.append(att)
         logs.append(log)
-        b_two = swap(b_low, "fsdp", 2)
-        b_one = swap(b_low, "fsdp", 1)
-        c_side += [swap(c_one, "seq", 2), swap(c_three, "seq", 2)]
-        grads_in = to_sequences(out_cotangent).reshape(rows, width)
-        qkv, _ = lax.optimization_barrier((qkv, (att, b_two, b_one, c_side)))
+        qkv, b_two, b_one, c_three, c_side, grads_in, _ = lax.optimization_barrier(
+            (qkv, b_two, b_one, c_three, c_side, grads_in, att)
+        )
+        c_side = c_side + [swap(c_one, "seq", 2), swap(c_three, "seq", 2)]
         att, log = attend(doc, qkv, 2 * each, each)
         atts.append(att)
         logs.append(log)
         b_three = swap(b_two, "fsdp", 1)
+        b_three, b_two, b_one, c_side, _ = lax.optimization_barrier((b_three, b_two, b_one, c_side, att))
         b_mine = [b_low, b_two, b_one, b_three]
         b_other = [swap(value, "seq", 1) for value in b_mine]
         plan_b, pieces_b = plan_a, b_mine + b_other

time: 422 us -> 421 us (level)
  starting transfers between devices: 70 us -> 64.9 us
  waiting for transfers between devices: 100 us -> 105 us
    ppermute x61, waiting for transfers between devices: 100 us -> 105 us  [swap(): return lax.ppermute(value, axis, [(i, i ^ mask) for i in range(size)])]
    ppermute x61, starting transfers between devices: 49.2 us -> 44.8 us  [swap(): return lax.ppermute(value, axis, [(i, i ^ mask) for i in range(size)])]
  transfers between devices with their start and end apart: 66 -> 66, of which waited for: 21 -> 22; matrix products, arithmetic and copies ran while one was open for 14% -> 14% of each run, Pallas kernels for 30% -> 28%
where the time goes in v4:
time: 421 us; the launch traced here: 417 us
  Pallas kernels  175 us (42%)
  waiting for transfers between devices  105 us (25%)
  starting transfers between devices  64.9 us (15%)
  other arithmetic  51 us (12%)
  local copies, waits for them, and re-layouts  18.5 us (4%)
    ppermute x61, waiting for transfers between devices, swap(): return lax.ppermute(value, axis, [(i, i ^ mask) for i in range(size)])  105 us
    pallas_call x3, Pallas kernels, attend_back(): pl.pallas_call(bwd_kernel, grid=(n,), in_specs=[pl.BlockSpec((rows, 1), l...  49.2 us
    ppermute x61, starting transfers between devices, swap(): return lax.ppermute(value, axis, [(i, i ^ mask) for i in range(size)])  44.8 us
    pallas_call x1, Pallas kernels, ffn(): pl.pallas_call(lambda *refs: ffn_kernel((inner_plan, outer_plan, len(atts...  38 us
    pallas_call x3, Pallas kernels, attend(): pl.pallas_call(fwd_kernel, grid=(n,), in_specs=[pl.BlockSpec((rows, 1), l...  34 us
    convert_element_type x12, other arithmetic, halve(): fold([part[half:] for part in parts]).astype(BF)  21.1 us
    pallas_call x1, Pallas kernels, grad_inner(): pl.pallas_call(lambda at_ref, low_ref, din_ref, *refs: grad_inner_kernel(...  12.2 us
    pallas_call x1, Pallas kernels, grad_outer(): pl.pallas_call(lambda *refs: grad_outer_kernel(size // 2, *refs), grid_sp...  12.1 us
  transfers between devices with their start and end apart: 66, of which 22 were waited for; matrix products, arithmetic and copies ran while one was open for 14% of the time, Pallas kernels for 28%

profile of v4, /device:TPU:0, one launch (start us, length us, event | category | flops | bytes accessed | tf_op | source)
XLA Modules:
  0.0 416.5 jit_solution(13688981235048419315)
XLA Ops:
  2.1 4.3 %all-to-all-start.1 = ((s32[4,1,256]{2,1,0:T(1,128)}), s32[4,1,256]{2,1,0:T(1,128)S(1)}, u32[]{:S(2)}, u32[]{:S(2)}) async-start(s32[4,1,256]{2,1,0:T(1,128)} %all_to_all.19), calls=%async_computation.1 | async-start | bytes 8192 | tf_op jit(solution)/shard_map/all_to_all | solution.py:592
  8.1 3.1 collective-permute-start.1
  15.1 3.6 all-to-all-start
  18.7 7.8 %collective-permute-done = bf16[1,96,1152]{2,1,0:T(8,128)(2,1)} collective-permute-done((bf16[1,96,1152]{2,1,0:T(8,128)(2,1)S(1)}, bf16[1,96,1152]{2,1,0:T(8,128)(2,1)}, u32[]{:S(2)}, u32[]{:S(2)}) %collective-permute-start) | collective-permute-done | bytes 221216 | tf_op jit(solution)/shard_map/ppermute | solution.py:123
  30.8 2.1 collective-permute-start.4
  32.9 8.4 %collective-permute-done.4 = bf16[2,12,96]{2,1,0:T(8,128)(2,1)S(1)} collective-permute-done((bf16[2,12,96]{2,1,0:T(8,128)(2,1)S(1)}, bf16[2,12,96]{2,1,0:T(8,128)(2,1)S(1)}, u32[]{:S(2)}, u32[]{:S(2)}) %collective-permute-start.4) | collective-permute-done | bytes 4640 | tf_op jit(solution)/shard_map/ppermute | solution.py:123
  45.6 8.3 %collective-permute-done.11 = bf16[1,96,768]{2,1,0:T(8,128)(2,1)S(1)} collective-permute-done((bf16[1,96,768]{2,1,0:T(8,128)(2,1)S(1)}, bf16[1,96,768]{2,1,0:T(8,128)(2,1)S(1)}, u32[]{:S(2)}, u32[]{:S(2)}) %collective-permute-start.11) | collective-permute-done | bytes 147488 | tf_op jit(solution)/shard_map/ppermute | solution.py:123
  56.9 15.6 %collective-permute-done.12 = bf16[1,96,1920]{2,1,0:T(8,128)(2,1)S(1)} collective-permute-done((bf16[1,96,1920]{2,1,0:T(8,128)(2,1)S(1)}, bf16[1,96,1920]{2,1,0:T(8,128)(2,1)S(1)}, u32[]{:S(2)}, u32[]{:S(2)}) %collective-permute-start.12) | collective-permute-done | bytes 368672 | tf_op jit(solution)/shard_map/ppermute | solution.py:123
  73.8 8.9 %project.1.q_ref.k_ref.v_ref = bf16[1024,2304]{1,0:T(8,128)(2,1)} custom-call(s32[2]{0:T(128)} %pad_add_fusion.refs_0_.at_ref, bf16[1024,768]{1,0:T(8,128)(2,1)} %bitcast.81, f32[1,2304]{1,0:T(1,128)} %fusion.11.refs_2_, bf16[2,96,1152]{2,1,0:T(8,128)(2,1)} %pad_maximum_fusion.4.refs_3_.refs_11_, ...), custom_call_target="tpu_custom_call" | custom-call | flops 3623878656 | bytes 11010048 | tf_op jit(solution)/shard_map/project/pallas_call | solution.py:209
  82.7 3.9 all-to-all-start.2
  93.7 11.2 %attend.3 = (bf16[1024,256]{1,0:T(8,128)(2,1)}, f32[2,1024,2]{2,1,0:T(8,128)}) custom-call(s32[1024,1]{1,0:T(8,128)} %copy.59.doc_ref, bf16[1024,2304]{1,0:T(8,128)(2,1)} %project.1.q_ref.k_ref.v_ref, bf16[1024,2304]{1,0:T(8,128)(2,1)} %project.1.q_ref.k_ref.v_ref, bf16[1024,2304]{1,0:T(8,128)(2,1)} %project.1.q_ref.k_ref.v_ref), custom_call_target="tpu_custom_call" | custom-call | flops 4294967296 | bytes 2097152 | tf_op jit(solution)/shard_map/attend/pallas_call | solution.py:47
  105.7 11.3 %attend.4 = (bf16[1024,256]{1,0:T(8,128)(2,1)}, f32[2,1024,2]{2,1,0:T(8,128)}) custom-call(s32[1024,1]{1,0:T(8,128)} %copy.59.doc_ref, bf16[1024,2304]{1,0:T(8,128)(2,1)} %project.1.q_ref.k_ref.v_ref, bf16[1024,2304]{1,0:T(8,128)(2,1)} %project.1.q_ref.k_ref.v_ref, bf16[1024,2304]{1,0:T(8,128)(2,1)} %project.1.q_ref.k_ref.v_ref), custom_call_target="tpu_custom_call" | custom-call | flops 4294967296 | bytes 2097152 | tf_op jit(solution)/shard_map/attend/pallas_call | solution.py:47
  117.0 2.4 collective-permute-done.19.refs_21_
  123.8 7.7 %collective-permute-done.21.refs_22_ = bf16[2,96,768]{2,1,0:T(8,128)(2,1)} collective-permute-done((bf16[2,96,768]{2,1,0:T(8,128)(2,1)}, bf16[2,96,768]{2,1,0:T(8,128)(2,1)}, u32[]{:S(2)}, u32[]{:S(2)}) %collective-permute-start.21) | collective-permute-done | bytes 294944 | tf_op jit(solution)/shard_map/ppermute | solution.py:123
  131.4 4.1 collective-permute-done.22.refs_23_
  135.5 2.9 collective-permute-done.20.refs_11_
  138.4 11.5 %attend.5 = (bf16[1024,256]{1,0:T(8,128)(2,1)}, f32[2,1024,2]{2,1,0:T(8,128)}) custom-call(s32[1024,1]{1,0:T(8,128)} %copy.59.doc_ref, bf16[1024,2304]{1,0:T(8,128)(2,1)} %project.1.q_ref.k_ref.v_ref, bf16[1024,2304]{1,0:T(8,128)(2,1)} %project.1.q_ref.k_ref.v_ref, bf16[1024,2304]{1,0:T(8,128)(2,1)} %project.1.q_ref.k_ref.v_ref), custom_call_target="tpu_custom_call" | custom-call | flops 4294967296 | bytes 2097152 | tf_op jit(solution)/shard_map/attend/pallas_call | solution.py:47
  151.5 3.5 collective-permute-done.31.refs_28_
  158.6 38.0 %ffn.1 = (bf16[1024,768]{1,0:T(8,128)(2,1)}, bf16[1024,3072]{1,0:T(8,128)(2,1)}, bf16[1024,3072]{1,0:T(8,128)(2,1)}, bf16[1024,768]{1,0:T(8,128)(2,1)}, bf16[102...) custom-call(s32[2]{0:T(128)} %pad_add_fusion.refs_0_.at_ref, ...), custom_call_target="tpu_custom_call" | custom-call | flops 21743271936 | bytes 28311552 | tf_op jit(solution)/shard_map/ffn/pallas_call | solution.py:335
  196.6 12.1 %grad_outer.1 = (bf16[8,192,768]{2,1,0:T(8,128)(2,1)}, bf16[8,192,768]{2,1,0:T(8,128)(2,1)}) custom-call(s32[2]{0:T(128)} %pad_add_fusion.refs_0_.at_ref, bf16[1024,3072]{1,0:T(8,128)(2,1)} %get-tuple-element.129.refs_1_, bf16[1024,768]{1,0:T(8,128)(2,1)} %get-tuple-element.130.refs_2_), custom_call_target="tpu_custom_call" | custom-call | flops 4831838208 | bytes 12582912 | tf_op jit(solution)/shard_map/grad_outer/pallas_call | solution.py:488
  209.0 12.2 %grad_inner.1 = (bf16[8,48,1920]{2,1,0:T(8,128)(2,1)}, bf16[8,48,1920]{2,1,0:T(8,128)(2,1)}, bf16[8,48,1920]{2,1,0:T(8,128)(2,1)}, bf16[8,48,1920]{2,1,0:T(8,128)(2,1)}) custom-call(s32[2]{0:T(128)} %pad_add_fusion.refs_0_.at_ref, bf16[1024,768]{1,0:T(8,128)(2,1)} %get-tuple-element.132.low_ref, bf16[1024,3072]{1,0:T(8,128)(2,1)} %get-tuple-element.133.din_ref, ...), custom_call_target="tpu_custom_call" | custom-call | flops 6039797760 | bytes 12582912 | tf_op jit(solution)/shard_map/grad_inner/pallas_call | solution.py:450
  222.0 2.9 collective-permute-done.36
  224.9 3.4 add_convert_fusion
  231.4 16.7 %attend_back.3 = (bf16[1024,256]{1,0:T(8,128)(2,1)}, bf16[1024,256]{1,0:T(8,128)(2,1)}, bf16[1024,256]{1,0:T(8,128)(2,1)}, f32[1,256]{1,0:T(1,128)}, f32[1,256]{1,0:T(1,128)}) custom-call(s32[1024,1]{1,0:T(8,128)} %copy.59.doc_ref, bf16[1024,2304]{1,0:T(8,128)(2,1)} %project.1.q_ref.k_ref.v_ref, bf16[1024,2304]{1,0:T(8,128)(2,1)} %project.1.q_ref.k_ref.v_ref, ...), custom_call_target="tpu_custom_call" | custom-call | flops 6442450944 | bytes 4194304 | tf_op jit(solution)/shard_map/attend_back/pallas_call | solution.py:105
  248.0 3.7 all-to-all-start.3
  251.8 16.2 %attend_back.4 = (bf16[1024,256]{1,0:T(8,128)(2,1)}, bf16[1024,256]{1,0:T(8,128)(2,1)}, bf16[1024,256]{1,0:T(8,128)(2,1)}, f32[1,256]{1,0:T(1,128)}, f32[1,256]{1,0:T(1,128)}) custom-call(s32[1024,1]{1,0:T(8,128)} %copy.59.doc_ref, bf16[1024,2304]{1,0:T(8,128)(2,1)} %project.1.q_ref.k_ref.v_ref, bf16[1024,2304]{1,0:T(8,128)(2,1)} %project.1.q_ref.k_ref.v_ref, ...), custom_call_target="tpu_custom_call" | custom-call | flops 6442450944 | bytes 4194304 | tf_op jit(solution)/shard_map/attend_back/pallas_call | solution.py:105
  268.1 2.7 pad_maximum_fusion
  272.0 6.5 %grad_wide.2 = (bf16[8,48,1536]{2,1,0:T(8,128)(2,1)}, bf16[8,48,1536]{2,1,0:T(8,128)(2,1)}) custom-call(s32[2]{0:T(128)} %pad_add_fusion.refs_0_.at_ref, bf16[1024,768]{1,0:T(8,128)(2,1)} %bitcast.83, bf16[1024,512]{1,0:T(8,128)(2,1)} %get-tuple-element.203.refs_1_, bf16[1024,512]{1,0:T(8,128)(2,1)} %get-tuple-element.204.refs_2_, ...), custom_call_target="tpu_custom_call" | custom-call | flops 2415919104 | bytes 5505024 | tf_op jit(solution)/shard_map/grad_wide/pallas_call | solution.py:401
  279.0 2.7 add_convert_fusion.2
  283.2 2.5 add_convert_fusion.4
  285.7 16.3 %attend_back.5 = (bf16[1024,256]{1,0:T(8,128)(2,1)}, bf16[1024,256]{1,0:T(8,128)(2,1)}, bf16[1024,256]{1,0:T(8,128)(2,1)}, f32[1,256]{1,0:T(1,128)}, f32[1,256]{1,0:T(1,128)}) custom-call(s32[1024,1]{1,0:T(8,128)} %copy.59.doc_ref, bf16[1024,2304]{1,0:T(8,128)(2,1)} %project.1.q_ref.k_ref.v_ref, bf16[1024,2304]{1,0:T(8,128)(2,1)} %project.1.q_ref.k_ref.v_ref, ...), custom_call_target="tpu_custom_call" | custom-call | flops 6442450944 | bytes 4194304 | tf_op jit(solution)/shard_map/attend_back/pallas_call | solution.py:105
  305.1 2.1 collective-permute-start.54
  309.7 5.8 %collective-permute-done.54 = bf16[2,48,1920]{2,1,0:T(8,128)(2,1)S(1)} collective-permute-done((bf16[2,48,1920]{2,1,0:T(8,128)(2,1)S(1)}, bf16[2,48,1920]{2,1,0:T(8,128)(2,1)S(1)}, u32[]{:S(2)}, u32[]{:S(2)}) %collective-permute-start.54) | collective-permute-done | bytes 368672 | tf_op jit(solution)/shard_map/ppermute | solution.py:123
  318.2 2.2 collective-permute-start.55
  320.4 2.1 add_convert_fusion.9
  323.2 4.8 %grad_wide.3 = (bf16[8,64,768]{2,1,0:T(8,128)(2,1)}, bf16[8,64,768]{2,1,0:T(8,128)(2,1)}) custom-call(s32[2]{0:T(128)} %pad_add_fusion.refs_0_.at_ref, bf16[8,16,256]{2,1,0:T(8,128)(2,1)} %fusion.9.refs_0_, bf16[1024,768]{1,0:T(8,128)(2,1)} %bitcast.84, bf16[1024,256]{1,0:T(8,128)(2,1)} %get-tuple-element.167.refs_2_.refs_8_, ...), custom_call_target="tpu_custom_call" | custom-call | flops 1207959552 | bytes 2752512 | tf_op jit(solution)/shard_map/grad_wide/pallas_call | solution.py:401
  328.0 9.7 %input_gradient.1 = bf16[1024,768]{1,0:T(8,128)(2,1)} custom-call(s32[2]{0:T(128)} %pad_add_fusion.refs_0_.at_ref, f32[1024,768]{1,0:T(8,128)} %get-tuple-element.171.refs_1_, bf16[1024,256]{1,0:T(8,128)(2,1)} %get-tuple-element.140.refs_2_, bf16[1024,256]{1,0:T(8,128)(2,1)} %get-tuple-element.141.refs_3_, bf16[1024,256]{1,0:T(8,128)(2,1)} %get-tuple-element.142.refs_4_, ...), custom_call_target="tpu_custom_call" | custom-call | flops 3623878656 | bytes 11010048 | tf_op jit(solution)/shard_map/input_gradient/pallas_call | solution.py:530
  337.7 4.6 %all-to-all-start.4 = ((bf16[4,256,768]{2,1,0:T(8,128)(2,1)}), bf16[4,256,768]{2,1,0:T(8,128)(2,1)}, u32[]{:S(2)}, u32[]{:S(2)}) async-start(bf16[4,256,768]{2,1,0:T(8,128)(2,1)} %bitcast.86), calls=%async_computation.4 | async-start | bytes 3145728 | tf_op jit(solution)/shard_map/all_to_all | solution.py:595
  350.2 3.5 collective-permute-done.43
  355.6 2.2 collective-permute-start.44
  361.0 5.8 %collective-permute-done.56 = bf16[48,1920]{1,0:T(8,128)(2,1)S(1)} collective-permute-done((bf16[48,1920]{1,0:T(8,128)(2,1)S(1)}, bf16[48,1920]{1,0:T(8,128)(2,1)S(1)}, u32[]{:S(2)}, u32[]{:S(2)}) %collective-permute-start.56) | collective-permute-done | bytes 184352 | tf_op jit(solution)/shard_map/ppermute | solution.py:123
  370.6 2.1 collective-permute-done.59
  373.8 3.0 collective-permute-done.45
  380.5 9.0 %collective-permute-done.48 = bf16[4,64,768]{2,1,0:T(8,128)(2,1)S(1)} collective-permute-done((bf16[4,64,768]{2,1,0:T(8,128)(2,1)S(1)}, bf16[4,64,768]{2,1,0:T(8,128)(2,1)S(1)}, u32[]{:S(2)}, u32[]{:S(2)}) %collective-permute-start.48) | collective-permute-done | bytes 393248 | tf_op jit(solution)/shard_map/ppermute | solution.py:123
  392.6 4.6 %collective-permute-done.49 = bf16[2,64,768]{2,1,0:T(8,128)(2,1)S(1)} collective-permute-done((bf16[2,64,768]{2,1,0:T(8,128)(2,1)S(1)}, bf16[2,64,768]{2,1,0:T(8,128)(2,1)S(1)}, u32[]{:S(2)}, u32[]{:S(2)}) %collective-permute-start.49) | collective-permute-done | bytes 196640 | tf_op jit(solution)/shard_map/ppermute | solution.py:123
  398.8 2.2 collective-permute-start.50
  401.0 3.3 convert.50
  407.2 3.2 collective-permute-done.51
  (254 shorter events, 88.1 us)
Async XLA Ops:
  2.1 13.0 %all-to-all-start.1 = ((s32[4,1,256]{2,1,0:T(1,128)}), s32[4,1,256]{2,1,0:T(1,128)S(1)}, u32[]{:S(2)}, u32[]{:S(2)}) async-start(s32[4,1,256]{2,1,0:T(1,128)} %all_to_all.19), calls=%async_computation.1 | async-start | bytes 8192 | tf_op jit(solution)/shard_map/all_to_all | solution.py:592
  13.2 13.3 %collective-permute-start = (bf16[1,96,1152]{2,1,0:T(8,128)(2,1)S(1)}, bf16[1,96,1152]{2,1,0:T(8,128)(2,1)}, u32[]{:S(2)}, u32[]{:S(2)}) collective-permute-start(bf16[1,96,1152]{2,1,0:T(8,128)(2,1)S(1)} %maximum_select_fusion.7), channel_id=1, source_target_pairs={{0,4},{1,5},{2,6},{3,7},{4,0},{5,1},{6,2},{7,3},{8,12},{9,13},{10,... | collective-permute-start | bytes 663560 | tf_op jit(solution)/shard_map/ppermute | solution.py:123
  15.1 57.5 %all-to-all-start = ((bf16[4,256,768]{2,1,0:T(8,128)(2,1)}), bf16[4,256,768]{2,1,0:T(8,128)(2,1)S(1)}, u32[]{:S(2)}, u32[]{:S(2)}) async-start(bf16[4,256,768]{2,1,0:T(8,128)(2,1)} %bitcast.2), calls=%async_computation | async-start | bytes 3145728 | tf_op jit(solution)/shard_map/all_to_all | solution.py:592
  28.3 13.1 %collective-permute-start.3 = (bf16[2,96,1152]{2,1,0:T(8,128)(2,1)}, bf16[2,96,1152]{2,1,0:T(8,128)(2,1)}, u32[]{:S(2)}, u32[]{:S(2)}) collective-permute-start(bf16[2,96,1152]{2,1,0:T(8,128)(2,1)} %pad_maximum_fusion.4.refs_3_.refs_11_), channel_id=1, source_target_pairs={{0,1},{1,0},{2,3},{3,2},{4,5},{5,4},{6,7},{7,6},{8,9},{9,8},{10,11... | collective-permute-start | bytes 1327112 | tf_op jit(solution)/shard_map/ppermute | solution.py:123
  29.8 11.6 %collective-permute-start.2 = (bf16[2,96,1152]{2,1,0:T(8,128)(2,1)}, bf16[2,96,1152]{2,1,0:T(8,128)(2,1)}, u32[]{:S(2)}, u32[]{:S(2)}) collective-permute-start(bf16[2,96,1152]{2,1,0:T(8,128)(2,1)} %pad_maximum_fusion.4.refs_3_.refs_11_), channel_id=1, source_target_pairs={{0,2},{1,3},{2,0},{3,1},{4,6},{5,7},{6,4},{7,5},{8,10},{9,11},{10,... | collective-permute-start | bytes 1327112 | tf_op jit(solution)/shard_map/ppermute | solution.py:123
  30.8 10.5 %collective-permute-start.4 = (bf16[2,12,96]{2,1,0:T(8,128)(2,1)S(1)}, bf16[2,12,96]{2,1,0:T(8,128)(2,1)S(1)}, u32[]{:S(2)}, u32[]{:S(2)}) collective-permute-start(bf16[2,12,96]{2,1,0:T(8,128)(2,1)S(1)} %maximum_select_fusion.10), channel_id=1, source_target_pairs={{0,2},{1,3},{2,0},{3,1},{4,6},{5,7},{6,4},{7,5},{8,10},{9,11},{10,... | collective-permute-start | bytes 13832 | tf_op jit(solution)/shard_map/ppermute | solution.py:123
  42.5 30.1 %collective-permute-start.7 = (bf16[2,96,1152]{2,1,0:T(8,128)(2,1)}, bf16[2,96,1152]{2,1,0:T(8,128)(2,1)}, u32[]{:S(2)}, u32[]{:S(2)}) collective-permute-start(bf16[2,96,1152]{2,1,0:T(8,128)(2,1)} %pad_maximum_fusion.4.refs_3_.refs_11_), channel_id=1, source_target_pairs={{0,8},{8,0},{16,24},{24,16},{1,9},{9,1},{17,25},{25,17},{2,10},{10... | collective-permute-start | bytes 1327112 | tf_op jit(solution)/shard_map/ppermute | solution.py:123
  42.5 30.1 %collective-permute-start.8 = (bf16[2,96,1152]{2,1,0:T(8,128)(2,1)}, bf16[2,96,1152]{2,1,0:T(8,128)(2,1)}, u32[]{:S(2)}, u32[]{:S(2)}) collective-permute-start(bf16[2,96,1152]{2,1,0:T(8,128)(2,1)} %collective-permute-done.2.refs_4_.refs_12_), channel_id=1, source_target_pairs={{0,8},{8,0},{16,24},{24,16},{1,9},{9,1},{17,25},{25,17},{2,10},{10... | collective-permute-start | bytes 1327112 | tf_op jit(solution)/shard_map/ppermute | solution.py:123
  43.0 12.5 %collective-permute-start.6 = (bf16[2,96,1152]{2,1,0:T(8,128)(2,1)}, bf16[2,96,1152]{2,1,0:T(8,128)(2,1)}, u32[]{:S(2)}, u32[]{:S(2)}) collective-permute-start(bf16[2,96,1152]{2,1,0:T(8,128)(2,1)} %collective-permute-done.2.refs_4_.refs_12_), channel_id=1, source_target_pairs={{0,1},{1,0},{2,3},{3,2},{4,5},{5,4},{6,7},{7,6},{8,9},{9,8},{10,11... | collective-permute-start | bytes 1327112 | tf_op jit(solution)/shard_map/ppermute | solution.py:123
  45.3 27.3 %collective-permute-start.9 = (bf16[2,96,1152]{2,1,0:T(8,128)(2,1)}, bf16[2,96,1152]{2,1,0:T(8,128)(2,1)}, u32[]{:S(2)}, u32[]{:S(2)}) collective-permute-start(bf16[2,96,1152]{2,1,0:T(8,128)(2,1)} %collective-permute-done.3.refs_5_.refs_13_), channel_id=1, source_target_pairs={{0,8},{8,0},{16,24},{24,16},{1,9},{9,1},{17,25},{25,17},{2,10},{10... | collective-permute-start | bytes 1327112 | tf_op jit(solution)/shard_map/ppermute | solution.py:123
  53.9 18.6 %collective-permute-start.12 = (bf16[1,96,1920]{2,1,0:T(8,128)(2,1)S(1)}, bf16[1,96,1920]{2,1,0:T(8,128)(2,1)S(1)}, u32[]{:S(2)}, u32[]{:S(2)}) collective-permute-start(bf16[1,96,1920]{2,1,0:T(8,128)(2,1)S(1)} %bitcast.89), channel_id=1, source_target_pairs={{0,4},{1,5},{2,6},{3,7},{4,0},{5,1},{6,2},{7,3},{8,12},{9,13},{10,... | collective-permute-start | bytes 1105928 | tf_op jit(solution)/shard_map/ppermute | solution.py:123
  55.5 17.1 %collective-permute-start.10 = (bf16[2,96,1152]{2,1,0:T(8,128)(2,1)}, bf16[2,96,1152]{2,1,0:T(8,128)(2,1)}, u32[]{:S(2)}, u32[]{:S(2)}) collective-permute-start(bf16[2,96,1152]{2,1,0:T(8,128)(2,1)} %collective-permute-done.6.refs_6_.refs_14_), channel_id=1, source_target_pairs={{0,8},{8,0},{16,24},{24,16},{1,9},{9,1},{17,25},{25,17},{2,10},{10... | collective-permute-start | bytes 1327112 | tf_op jit(solution)/shard_map/ppermute | solution.py:123
  82.7 37.9 %all-to-all-start.2 = ((bf16[4,256,768]{2,1,0:T(8,128)(2,1)}), bf16[4,256,768]{2,1,0:T(8,128)(2,1)S(1)}, u32[]{:S(2)}, u32[]{:S(2)}) async-start(bf16[4,256,768]{2,1,0:T(8,128)(2,1)} %bitcast.35), calls=%async_computation.2 | async-start | bytes 3145728 | tf_op jit(solution)/shard_map/all_to_all | solution.py:592
  87.7 29.3 %collective-permute-start.18 = (bf16[2,96,768]{2,1,0:T(8,128)(2,1)S(1)}, bf16[2,96,768]{2,1,0:T(8,128)(2,1)S(1)}, u32[]{:S(2)}, u32[]{:S(2)}) collective-permute-start(bf16[2,96,768]{2,1,0:T(8,128)(2,1)S(1)} %copy-done.16), channel_id=1, source_target_pairs={{0,16},{8,24},{16,0},{24,8},{1,17},{9,25},{17,1},{25,9},{2,18},{10... | collective-permute-start | bytes 884744 | tf_op jit(solution)/shard_map/ppermute | solution.py:123
  89.7 15.3 %collective-permute-start.14 = (bf16[2,96,768]{2,1,0:T(8,128)(2,1)S(1)}, bf16[2,96,768]{2,1,0:T(8,128)(2,1)S(1)}, u32[]{:S(2)}, u32[]{:S(2)}) collective-permute-start(bf16[2,96,768]{2,1,0:T(8,128)(2,1)S(1)} %copy-done.16), channel_id=1, source_target_pairs={{0,1},{1,0},{2,3},{3,2},{4,5},{5,4},{6,7},{7,6},{8,9},{9,8},{10,11... | collective-permute-start | bytes 884744 | tf_op jit(solution)/shard_map/ppermute | solution.py:123
  90.2 14.8 %collective-permute-start.13 = (bf16[2,96,768]{2,1,0:T(8,128)(2,1)S(1)}, bf16[2,96,768]{2,1,0:T(8,128)(2,1)}, u32[]{:S(2)}, u32[]{:S(2)}) collective-permute-start(bf16[2,96,768]{2,1,0:T(8,128)(2,1)S(1)} %copy-done.16), channel_id=1, source_target_pairs={{0,2},{1,3},{2,0},{3,1},{4,6},{5,7},{6,4},{7,5},{8,10},{9,11},{10,... | collective-permute-start | bytes 884744 | tf_op jit(solution)/shard_map/ppermute | solution.py:123
  90.2 30.5 %collective-permute-start.16 = (bf16[2,96,1920]{2,1,0:T(8,128)(2,1)S(1)}, bf16[2,96,1920]{2,1,0:T(8,128)(2,1)}, u32[]{:S(2)}, u32[]{:S(2)}) collective-permute-start(bf16[2,96,1920]{2,1,0:T(8,128)(2,1)S(1)} %pad_maximum_fusion.3.refs_8_), channel_id=1, source_target_pairs={{0,1},{1,0},{2,3},{3,2},{4,5},{5,4},{6,7},{7,6},{8,9},{9,8},{10,11... | collective-permute-start | bytes 2211848 | tf_op jit(solution)/shard_map/ppermute | solution.py:123
  91.7 29.0 %collective-permute-start.15 = (bf16[2,96,1920]{2,1,0:T(8,128)(2,1)S(1)}, bf16[2,96,1920]{2,1,0:T(8,128)(2,1)}, u32[]{:S(2)}, u32[]{:S(2)}) collective-permute-start(bf16[2,96,1920]{2,1,0:T(8,128)(2,1)S(1)} %pad_maximum_fusion.3.refs_8_), channel_id=1, source_target_pairs={{0,2},{1,3},{2,0},{3,1},{4,6},{5,7},{6,4},{7,5},{8,10},{9,11},{10,... | collective-permute-start | bytes 2211848 | tf_op jit(solution)/shard_map/ppermute | solution.py:123
  105.0 14.4 %collective-permute-start.19 = (bf16[2,96,768]{2,1,0:T(8,128)(2,1)}, bf16[2,96,768]{2,1,0:T(8,128)(2,1)}, u32[]{:S(2)}, u32[]{:S(2)}) collective-permute-start(bf16[2,96,768]{2,1,0:T(8,128)(2,1)} %collective-permute-done.13.refs_17_), channel_id=1, source_target_pairs={{0,16},{8,24},{16,0},{24,8},{1,17},{9,25},{17,1},{25,9},{2,18},{10... | collective-permute-start | bytes 884744 | tf_op jit(solution)/shard_map/ppermute | solution.py:123
  105.1 15.5 %collective-permute-start.17 = (bf16[2,96,768]{2,1,0:T(8,128)(2,1)}, bf16[2,96,768]{2,1,0:T(8,128)(2,1)}, u32[]{:S(2)}, u32[]{:S(2)}) collective-permute-start(bf16[2,96,768]{2,1,0:T(8,128)(2,1)} %collective-permute-done.13.refs_17_), channel_id=1, source_target_pairs={{0,1},{1,0},{2,3},{3,2},{4,5},{5,4},{6,7},{7,6},{8,9},{9,8},{10,11... | collective-permute-start | bytes 884744 | tf_op jit(solution)/shard_map/ppermute | solution.py:123
  120.7 17.8 %collective-permute-start.20 = (bf16[2,96,1920]{2,1,0:T(8,128)(2,1)}, bf16[2,96,1920]{2,1,0:T(8,128)(2,1)}, u32[]{:S(2)}, u32[]{:S(2)}) collective-permute-start(bf16[2,96,1920]{2,1,0:T(8,128)(2,1)} %collective-permute-done.15.refs_9_), channel_id=1, source_target_pairs={{0,1},{1,0},{2,3},{3,2},{4,5},{5,4},{6,7},{7,6},{8,9},{9,8},{10,11... | collective-permute-start | bytes 2211848 | tf_op jit(solution)/shard_map/ppermute | solution.py:123
  121.2 10.2 %collective-permute-start.21 = (bf16[2,96,768]{2,1,0:T(8,128)(2,1)}, bf16[2,96,768]{2,1,0:T(8,128)(2,1)}, u32[]{:S(2)}, u32[]{:S(2)}) collective-permute-start(bf16[2,96,768]{2,1,0:T(8,128)(2,1)} %copy-done.28), channel_id=1, source_target_pairs={{0,16},{8,24},{16,0},{24,8},{1,17},{9,25},{17,1},{25,9},{2,18},{10... | collective-permute-start | bytes 884744 | tf_op jit(solution)/shard_map/ppermute | solution.py:123
  121.6 13.9 %collective-permute-start.22 = (bf16[2,96,768]{2,1,0:T(8,128)(2,1)}, bf16[2,96,768]{2,1,0:T(8,128)(2,1)}, u32[]{:S(2)}, u32[]{:S(2)}) collective-permute-start(bf16[2,96,768]{2,1,0:T(8,128)(2,1)} %collective-permute-done.17.refs_19_), channel_id=1, source_target_pairs={{0,16},{8,24},{16,0},{24,8},{1,17},{9,25},{17,1},{25,9},{2,18},{10... | collective-permute-start | bytes 884744 | tf_op jit(solution)/shard_map/ppermute | solution.py:123
  123.3 27.7 %collective-permute-start.23 = (bf16[2,96,1920]{2,1,0:T(8,128)(2,1)S(1)}, bf16[2,96,1920]{2,1,0:T(8,128)(2,1)}, u32[]{:S(2)}, u32[]{:S(2)}) collective-permute-start(bf16[2,96,1920]{2,1,0:T(8,128)(2,1)S(1)} %pad_maximum_fusion.3.refs_8_), channel_id=1, source_target_pairs={{0,8},{8,0},{16,24},{24,16},{1,9},{9,1},{17,25},{25,17},{2,10},{10... | collective-permute-start | bytes 2211848 | tf_op jit(solution)/shard_map/ppermute | solution.py:123
  123.3 26.6 %collective-permute-start.27 = (bf16[2,96,768]{2,1,0:T(8,128)(2,1)S(1)}, bf16[2,96,768]{2,1,0:T(8,128)(2,1)S(1)}, u32[]{:S(2)}, u32[]{:S(2)}) collective-permute-start(bf16[2,96,768]{2,1,0:T(8,128)(2,1)S(1)} %copy-done.16), channel_id=1, source_target_pairs={{0,8},{8,0},{16,24},{24,16},{1,9},{9,1},{17,25},{25,17},{2,10},{10... | collective-permute-start | bytes 884744 | tf_op jit(solution)/shard_map/ppermute | solution.py:123
  131.4 19.0 %collective-permute-start.29 = (bf16[2,96,768]{2,1,0:T(8,128)(2,1)}, bf16[2,96,768]{2,1,0:T(8,128)(2,1)}, u32[]{:S(2)}, u32[]{:S(2)}) collective-permute-start(bf16[2,96,768]{2,1,0:T(8,128)(2,1)} %copy-done.28), channel_id=1, source_target_pairs={{0,8},{8,0},{16,24},{24,16},{1,9},{9,1},{17,25},{25,17},{2,10},{10... | collective-permute-start | bytes 884744 | tf_op jit(solution)/shard_map/ppermute | solution.py:123
  135.5 15.1 %collective-permute-start.28 = (bf16[2,96,768]{2,1,0:T(8,128)(2,1)}, bf16[2,96,768]{2,1,0:T(8,128)(2,1)}, u32[]{:S(2)}, u32[]{:S(2)}) collective-permute-start(bf16[2,96,768]{2,1,0:T(8,128)(2,1)} %collective-permute-done.13.refs_17_), channel_id=1, source_target_pairs={{0,8},{8,0},{16,24},{24,16},{1,9},{9,1},{17,25},{25,17},{2,10},{10... | collective-permute-start | bytes 884744 | tf_op jit(solution)/shard_map/ppermute | solution.py:123
  138.4 12.6 %collective-permute-start.30 = (bf16[2,96,768]{2,1,0:T(8,128)(2,1)}, bf16[2,96,768]{2,1,0:T(8,128)(2,1)}, u32[]{:S(2)}, u32[]{:S(2)}) collective-permute-start(bf16[2,96,768]{2,1,0:T(8,128)(2,1)} %collective-permute-done.17.refs_19_), channel_id=1, source_target_pairs={{0,8},{8,0},{16,24},{24,16},{1,9},{9,1},{17,25},{25,17},{2,10},{10... | collective-permute-start | bytes 884744 | tf_op jit(solution)/shard_map/ppermute | solution.py:123
  208.7 20.3 %collective-permute-start.35 = (bf16[8,192,768]{2,1,0:T(8,128)(2,1)}, bf16[8,192,768]{2,1,0:T(8,128)(2,1)S(1)}, u32[]{:S(2)}, u32[]{:S(2)}) collective-permute-start(bf16[8,192,768]{2,1,0:T(8,128)(2,1)} %get-tuple-element.136), channel_id=1, source_target_pairs={{0,8},{8,0},{16,24},{24,16},{1,9},{9,1},{17,25},{25,17},{2,10},{10... | collective-permute-start | bytes 7077896 | tf_op jit(solution)/shard_map/ppermute | solution.py:123
  221.6 26.5 %collective-permute-start.37 = (bf16[8,48,1920]{2,1,0:T(8,128)(2,1)}, bf16[8,48,1920]{2,1,0:T(8,128)(2,1)}, u32[]{:S(2)}, u32[]{:S(2)}) collective-permute-start(bf16[8,48,1920]{2,1,0:T(8,128)(2,1)} %get-tuple-element.147), channel_id=1, source_target_pairs={{0,8},{8,0},{16,24},{24,16},{1,9},{9,1},{17,25},{25,17},{2,10},{10... | collective-permute-start | bytes 4423688 | tf_op jit(solution)/shard_map/ppermute | solution.py:123
  228.3 50.7 %collective-permute-start.40 = (bf16[8,48,1920]{2,1,0:T(8,128)(2,1)}, bf16[8,48,1920]{2,1,0:T(8,128)(2,1)}, u32[]{:S(2)}, u32[]{:S(2)}) collective-permute-start(bf16[8,48,1920]{2,1,0:T(8,128)(2,1)} %add_convert_fusion), channel_id=1, source_target_pairs={{0,16},{8,24},{16,0},{24,8},{1,17},{9,25},{17,1},{25,9},{2,18},{10... | collective-permute-start | bytes 4423688 | tf_op jit(solution)/shard_map/ppermute | solution.py:123
  230.9 52.4 %collective-permute-start.38 = (bf16[4,192,768]{2,1,0:T(8,128)(2,1)}, bf16[4,192,768]{2,1,0:T(8,128)(2,1)}, u32[]{:S(2)}, u32[]{:S(2)}) collective-permute-start(bf16[4,192,768]{2,1,0:T(8,128)(2,1)} %add_convert_fusion.1), channel_id=1, source_target_pairs={{0,1},{1,0},{2,3},{3,2},{4,5},{5,4},{6,7},{7,6},{8,9},{9,8},{10,11... | collective-permute-start | bytes 3538952 | tf_op jit(solution)/shard_map/ppermute | solution.py:123
  248.0 37.7 %all-to-all-start.3 = ((bf16[4,256,768]{2,1,0:T(8,128)(2,1)}), bf16[4,256,768]{2,1,0:T(8,128)(2,1)S(1)}, u32[]{:S(2)}, u32[]{:S(2)}) async-start(bf16[4,256,768]{2,1,0:T(8,128)(2,1)} %bitcast.87), calls=%async_computation.3 | async-start | bytes 3145728 | tf_op jit(solution)/shard_map/all_to_all | solution.py:595
  278.5 28.7 %collective-permute-start.41 = (bf16[8,48,1536]{2,1,0:T(8,128)(2,1)}, bf16[8,48,1536]{2,1,0:T(8,128)(2,1)}, u32[]{:S(2)}, u32[]{:S(2)}) collective-permute-start(bf16[8,48,1536]{2,1,0:T(8,128)(2,1)} %get-tuple-element.165), channel_id=1, source_target_pairs={{0,8},{8,0},{16,24},{24,16},{1,9},{9,1},{17,25},{25,17},{2,10},{10... | collective-permute-start | bytes 3538952 | tf_op jit(solution)/shard_map/ppermute | solution.py:123
  281.7 21.9 %collective-permute-start.53 = (bf16[4,48,1920]{2,1,0:T(8,128)(2,1)}, bf16[4,48,1920]{2,1,0:T(8,128)(2,1)}, u32[]{:S(2)}, u32[]{:S(2)}) collective-permute-start(bf16[4,48,1920]{2,1,0:T(8,128)(2,1)} %add_convert_fusion.2), channel_id=1, source_target_pairs={{0,1},{1,0},{2,3},{3,2},{4,5},{5,4},{6,7},{7,6},{8,9},{9,8},{10,11... | collective-permute-start | bytes 2211848 | tf_op jit(solution)/shard_map/ppermute | solution.py:123
  285.7 34.7 %collective-permute-start.39 = (bf16[2,192,768]{2,1,0:T(8,128)(2,1)}, bf16[2,192,768]{2,1,0:T(8,128)(2,1)}, u32[]{:S(2)}, u32[]{:S(2)}) collective-permute-start(bf16[2,192,768]{2,1,0:T(8,128)(2,1)} %add_convert_fusion.4), channel_id=1, source_target_pairs={{0,2},{1,3},{2,0},{3,1},{4,6},{5,7},{6,4},{7,5},{8,10},{9,11},{10,... | collective-permute-start | bytes 1769480 | tf_op jit(solution)/shard_map/ppermute | solution.py:123
  305.1 10.3 %collective-permute-start.54 = (bf16[2,48,1920]{2,1,0:T(8,128)(2,1)S(1)}, bf16[2,48,1920]{2,1,0:T(8,128)(2,1)S(1)}, u32[]{:S(2)}, u32[]{:S(2)}) collective-permute-start(bf16[2,48,1920]{2,1,0:T(8,128)(2,1)S(1)} %add_convert_fusion.6), channel_id=1, source_target_pairs={{0,2},{1,3},{2,0},{3,1},{4,6},{5,7},{6,4},{7,5},{8,10},{9,11},{10,... | collective-permute-start | bytes 1105928 | tf_op jit(solution)/shard_map/ppermute | solution.py:123
  308.4 33.9 %collective-permute-start.42 = (bf16[4,48,1536]{2,1,0:T(8,128)(2,1)S(1)}, bf16[4,48,1536]{2,1,0:T(8,128)(2,1)}, u32[]{:S(2)}, u32[]{:S(2)}) collective-permute-start(bf16[4,48,1536]{2,1,0:T(8,128)(2,1)S(1)} %add_convert_fusion.3), channel_id=1, source_target_pairs={{0,1},{1,0},{2,3},{3,2},{4,5},{5,4},{6,7},{7,6},{8,9},{9,8},{10,11... | collective-permute-start | bytes 1769480 | tf_op jit(solution)/shard_map/ppermute | solution.py:123
  318.2 27.9 %collective-permute-start.55 = (bf16[1,48,1920]{2,1,0:T(8,128)(2,1)}, bf16[1,48,1920]{2,1,0:T(8,128)(2,1)S(1)}, u32[]{:S(2)}, u32[]{:S(2)}) collective-permute-start(bf16[1,48,1920]{2,1,0:T(8,128)(2,1)} %add_convert_fusion.12), channel_id=1, source_target_pairs={{0,4},{1,5},{2,6},{3,7},{4,0},{5,1},{6,2},{7,3},{8,12},{9,13},{10,... | collective-permute-start | bytes 552968 | tf_op jit(solution)/shard_map/ppermute | solution.py:123
  322.4 35.3 %collective-permute-start.58 = (bf16[1,192,768]{2,1,0:T(8,128)(2,1)}, bf16[1,192,768]{2,1,0:T(8,128)(2,1)}, u32[]{:S(2)}, u32[]{:S(2)}) collective-permute-start(bf16[1,192,768]{2,1,0:T(8,128)(2,1)} %add_convert_fusion.9), channel_id=1, source_target_pairs={{0,4},{1,5},{2,6},{3,7},{4,0},{5,1},{6,2},{7,3},{8,12},{9,13},{10,... | collective-permute-start | bytes 884744 | tf_op jit(solution)/shard_map/ppermute | solution.py:123
  337.7 63.3 %all-to-all-start.4 = ((bf16[4,256,768]{2,1,0:T(8,128)(2,1)}), bf16[4,256,768]{2,1,0:T(8,128)(2,1)}, u32[]{:S(2)}, u32[]{:S(2)}) async-start(bf16[4,256,768]{2,1,0:T(8,128)(2,1)} %bitcast.86), calls=%async_computation.4 | async-start | bytes 3145728 | tf_op jit(solution)/shard_map/all_to_all | solution.py:595
  345.9 30.9 %collective-permute-start.47 = (bf16[8,64,768]{2,1,0:T(8,128)(2,1)}, bf16[8,64,768]{2,1,0:T(8,128)(2,1)}, u32[]{:S(2)}, u32[]{:S(2)}) collective-permute-start(bf16[8,64,768]{2,1,0:T(8,128)(2,1)} %get-tuple-element.172), channel_id=1, source_target_pairs={{0,8},{8,0},{16,24},{24,16},{1,9},{9,1},{17,25},{25,17},{2,10},{10... | collective-permute-start | bytes 2359304 | tf_op jit(solution)/shard_map/ppermute | solution.py:123
  348.4 18.4 %collective-permute-start.56 = (bf16[48,1920]{1,0:T(8,128)(2,1)S(1)}, bf16[48,1920]{1,0:T(8,128)(2,1)S(1)}, u32[]{:S(2)}, u32[]{:S(2)}) collective-permute-start(bf16[48,1920]{1,0:T(8,128)(2,1)S(1)} %bitcast.88), channel_id=1, source_target_pairs={{0,16},{8,24},{16,0},{24,8},{1,17},{9,25},{17,1},{25,9},{2,18},{10... | collective-permute-start | bytes 552968 | tf_op jit(solution)/shard_map/ppermute | solution.py:123
  355.6 13.6 %collective-permute-start.44 = (bf16[1,48,1536]{2,1,0:T(8,128)(2,1)}, bf16[1,48,1536]{2,1,0:T(8,128)(2,1)}, u32[]{:S(2)}, u32[]{:S(2)}) collective-permute-start(bf16[1,48,1536]{2,1,0:T(8,128)(2,1)} %add_convert_fusion.14), channel_id=1, source_target_pairs={{0,4},{1,5},{2,6},{3,7},{4,0},{5,1},{6,2},{7,3},{8,12},{9,13},{10,... | collective-permute-start | bytes 442376 | tf_op jit(solution)/shard_map/ppermute | solution.py:123
  359.3 13.4 %collective-permute-start.59 = (bf16[192,768]{1,0:T(8,128)(2,1)S(1)}, bf16[192,768]{1,0:T(8,128)(2,1)}, u32[]{:S(2)}, u32[]{:S(2)}) collective-permute-start(bf16[192,768]{1,0:T(8,128)(2,1)S(1)} %fusion.1), channel_id=1, source_target_pairs={{0,16},{8,24},{16,0},{24,8},{1,17},{9,25},{17,1},{25,9},{2,18},{10... | collective-permute-start | bytes 884744 | tf_op jit(solution)/shard_map/ppermute | solution.py:123
  373.7 32.4 %collective-permute-start.60 = (f32[192,768]{1,0:T(8,128)S(1)}, f32[192,768]{1,0:T(8,128)S(1)}, u32[]{:S(2)}, u32[]{:S(2)}) collective-permute-start(f32[192,768]{1,0:T(8,128)S(1)} %convert_add_fusion), channel_id=1, source_target_pairs={{0,8},{8,0},{16,24},{24,16},{1,9},{9,1},{17,25},{25,17},{2,10},{10... | collective-permute-start | bytes 1769480 | tf_op jit(solution)/shard_map/ppermute | solution.py:123
  376.8 15.7 %collective-permute-start.46 = (f32[48,1536]{1,0:T(8,128)S(1)}, f32[48,1536]{1,0:T(8,128)S(1)}, u32[]{:S(2)}, u32[]{:S(2)}) collective-permute-start(f32[48,1536]{1,0:T(8,128)S(1)} %convert_add_fusion.1), channel_id=1, source_target_pairs={{0,8},{8,0},{16,24},{24,16},{1,9},{9,1},{17,25},{25,17},{2,10},{10... | collective-permute-start | bytes 884744 | tf_op jit(solution)/shard_map/ppermute | solution.py:123
  378.0 11.6 %collective-permute-start.48 = (bf16[4,64,768]{2,1,0:T(8,128)(2,1)S(1)}, bf16[4,64,768]{2,1,0:T(8,128)(2,1)S(1)}, u32[]{:S(2)}, u32[]{:S(2)}) collective-permute-start(bf16[4,64,768]{2,1,0:T(8,128)(2,1)S(1)} %add_convert_fusion.5), channel_id=1, source_target_pairs={{0,1},{1,0},{2,3},{3,2},{4,5},{5,4},{6,7},{7,6},{8,9},{9,8},{10,11... | collective-permute-start | bytes 1179656 | tf_op jit(solution)/shard_map/ppermute | solution.py:123
  (52 other events, 413.5 us)
